TPU v7x, 128 devices: a whole 4x4x4 slice. The times are simulated.
128 devices in a mesh: section: 8 (over y, z_lo), dp: 16 (over x, z_hi, core).
Axes of the slice: x: 4, y: 4, z: 4 (z_hi: 2, z_lo: 2; z = z_hi * 2 + z_lo), core: 2. Of those that a mesh axis runs over, the one named last changes fastest.
Arguments:
- enter_a: bfloat16 [8, 2048, 7168], P('section', 'dp'), may hold values from -6 to 6
- enter_b: bfloat16 [8, 2048, 7168], P('section', 'dp'), may hold values from -6 to 6
- cotan_a: bfloat16 [8, 2048, 7168], P('section', 'dp'), may hold values from -6 to 6
- cotan_b: bfloat16 [8, 2048, 7168], P('section', 'dp'), may hold values from -6 to 6
- saved_a: bfloat16 [2, 8, 2048, 7168], P(None, 'section', 'dp'), may hold values from -6 to 6
- saved_b: bfloat16 [2, 8, 2048, 7168], P(None, 'section', 'dp'), may hold values from -6 to 6
- norm_gain: float32 [8, 7168], P('section'), may hold values from 0.1 to 1.9
- w_down: bfloat16 [8, 7168, 256], P('section', 'dp'), may hold values from -0.0625 to 0.0625
- latent_gain: float32 [8, 256], P('section'), may hold values from 0.1 to 1.9
- w_up: bfloat16 [8, 256, 7168], P('section', None, 'dp'), may hold values from -0.375 to 0.375
Outputs:
- out_a: bfloat16 [8, 2048, 7168], P('section', 'dp')
- out_b: bfloat16 [8, 2048, 7168], P('section', 'dp')
- back_a: bfloat16 [8, 2048, 7168], P('section', 'dp')
- back_b: bfloat16 [8, 2048, 7168], P('section', 'dp')
- grad_norm_gain: float32 [8, 7168], P('section', 'dp')
- grad_down: float32 [8, 7168, 256], P('section', 'dp')
- grad_latent_gain: float32 [8, 256], P('section', 'dp')
- grad_up: float32 [8, 256, 7168], P('section', None, 'dp')
All inputs are finite; a program needn't handle non-finite values.
Results may differ from a plain program's by a relative error of at most 0.035.
Values may be sent and summed in bfloat16 or wider, within the bound.
No kernel may reach another device: no remote copies, remote signals or barrier semaphores. Data moves between devices by JAX's collectives and lax.ppermute only.
A program may use at most 192 MiB of HBM per device.

v0:
```python
import jax
import jax.numpy as jnp
from jax import lax
from jax.sharding import PartitionSpec as P

TICKS = 2


def swapped(value, axis, distance):
    return lax.ppermute(value, axis, [(i, i ^ 1 << distance) for i in range(lax.axis_size(axis))])


def from_behind(block, axis, distance):
    devices = range(lax.axis_size(axis))
    route = [(i - distance, i) for i in devices if i - distance in devices]
    return lax.ppermute(block, axis, route)


def shortened(value):

    def short(part):
        return part.astype(jnp.bfloat16) if part.dtype == jnp.float32 else part

    return jax.tree.map(short, value)


def layer(x, norm_gain, w_down, latent_gain, w_up):
    xf = x.astype(jnp.float32)
    normed = (xf * lax.rsqrt(jnp.mean(xf * xf, axis=-1, keepdims=True) + 1e-06) * norm_gain).astype(
        jnp.bfloat16
    )
    latent = jnp.dot(normed, w_down, preferred_element_type=jnp.float32)
    scaled = (
        latent * lax.rsqrt(jnp.mean(latent * latent, axis=-1, keepdims=True) + 1e-06) * latent_gain
    ).astype(jnp.bfloat16)
    return (xf + jnp.dot(scaled, w_up, preferred_element_type=jnp.float32)).astype(jnp.bfloat16)


def layer_grads(x, cotangent, weights):
    _, pull = jax.vjp(layer, x, *weights)
    return pull(cotangent)


def body(
    enter_a, enter_b, cotan_a, cotan_b, saved_a, saved_b, norm_gain, w_down, latent_gain, w_up
):
    section_count = lax.axis_size("section")
    section_bits = section_count.bit_length() - 1
    moved = (norm_gain, w_down, latent_gain, w_up)
    for bit in range(section_bits):
        moved = (
            swapped(moved[0].astype(jnp.bfloat16), "section", bit).astype(jnp.float32),
            swapped(moved[1], "section", bit),
            swapped(moved[2].astype(jnp.bfloat16), "section", bit).astype(jnp.float32),
            swapped(moved[3], "section", bit),
        )
    mirror_small = tuple((v[0] for v in moved))
    full = (
        lax.all_gather(w_down[0], "dp", axis=0, tiled=True),
        lax.all_gather(w_up[0], "dp", axis=1, tiled=True),
        lax.all_gather(mirror_small[1], "dp", axis=0, tiled=True),
        lax.all_gather(mirror_small[3], "dp", axis=1, tiled=True),
    )
    own_weights = (norm_gain[0], full[0], latent_gain[0], full[1])
    mirror_weights = (mirror_small[0], full[2], mirror_small[2], full[3])
    accum_own = tuple((jnp.zeros(v.shape, jnp.float32) for v in own_weights))
    accum_mirror = tuple((jnp.zeros(v.shape, jnp.float32) for v in mirror_weights))
    state_a = enter_a[0]
    state_b = enter_b[0]
    grad_a = cotan_a[0]
    grad_b = cotan_b[0]
    for tick in range(TICKS):
        out_a = layer(state_a, *own_weights)
        out_b = layer(state_b, *mirror_weights)
        result_a = layer_grads(saved_a[tick, 0], grad_a, own_weights)
        result_b = layer_grads(saved_b[tick, 0], grad_b, mirror_weights)
        back_a = result_a[0]
        back_b = result_b[0]
        accum_own = tuple((p + q.astype(jnp.float32) for p, q in zip(accum_own, result_a[1:])))
        accum_mirror = tuple(
            (p + q.astype(jnp.float32) for p, q in zip(accum_mirror, result_b[1:]))
        )
        if tick < TICKS - 1:
            state_a = from_behind(out_a, "section", 1)
            state_b = from_behind(out_b, "section", -1)
            grad_a = from_behind(back_a, "section", -1)
            grad_b = from_behind(back_b, "section", 1)
    part_own = tuple((v.astype(jnp.bfloat16) for v in accum_own))
    part_mirror = tuple((v.astype(jnp.bfloat16) for v in accum_mirror))
    paired = tuple((jnp.stack([p, q]) for p, q in zip(part_own, part_mirror)))
    sums = (
        lax.psum_scatter(paired[0], "dp", scatter_dimension=1, tiled=True).astype(jnp.float32),
        lax.psum_scatter(paired[1], "dp", scatter_dimension=1, tiled=True).astype(jnp.float32),
        lax.psum_scatter(paired[2], "dp", scatter_dimension=1, tiled=True).astype(jnp.float32),
        lax.psum_scatter(paired[3], "dp", scatter_dimension=2, tiled=True).astype(jnp.float32),
    )
    mine = tuple((v[0] for v in sums))
    theirs = tuple((v[1] for v in sums))
    arrived = theirs
    for bit in range(section_bits):
        arrived = swapped(
            (
                shortened(arrived[0]),
                shortened(arrived[1]),
                shortened(arrived[2]),
                shortened(arrived[3]),
            ),
            "section",
            bit,
        )
    totals = tuple((p + q for p, q in zip(mine, arrived)))
    return (
        out_a[None],
        out_b[None],
        back_a[None],
        back_b[None],
        totals[0][None],
        totals[1][None],
        totals[2][None],
        totals[3][None],
    )


def solution(mesh):
    placed = (
        P("section", "dp", None),
        P("section", "dp", None),
        P("section", "dp", None),
        P("section", "dp", None),
        P(None, "section", "dp", None),
        P(None, "section", "dp", None),
        P("section", None),
        P("section", "dp", None),
        P("section", None),
        P("section", None, "dp"),
    )
    return jax.shard_map(
        body,
        mesh=mesh,
        in_specs=placed,
        out_specs=(
            P("section", "dp", None),
            P("section", "dp", None),
            P("section", "dp", None),
            P("section", "dp", None),
            P("section", "dp"),
            P("section", "dp", None),
            P("section", "dp"),
            P("section", None, "dp"),
        ),
        check_vma=False,
    )
```

profile of v0, /device:TPU:0, one launch (start us, length us, event | category | flops | bytes accessed | tf_op | source)
XLA Modules:
  0.0 882.6 jit_solution(12329885674693998641)
XLA Ops:
  10.8 5.8 collective-permute-done.4
  18.2 5.2 collective-permute-done.5
  23.4 3.1 collective-permute-start.6
  26.5 4.4 collective-permute-done.6
  33.2 4.8 collective-permute-done.10
  39.4 4.6 collective-permute-done.11
  44.1 4.3 collective-permute-start.12
  48.4 4.0 collective-permute-done.12
  64.3 3.9 collective-permute-start.9
  70.5 3.0 collective-permute-done.3
  73.6 3.5 multiply_reduce_fusion.11
  77.1 45.5 %all-gather.11.cloned.1.call-done = bf16[1,256,7168]{1,2,0:T(8,128)(2,1)} async-done(((bf16[1,256,448]{1,2,0:T(8,128)(2,1)}), bf16[1,256,7168]{1,2,0:T(8,128)(2,1)}) %all-gather.11.cloned.1.call-update) | async-done | bytes 3670032 | tf_op jit(solution)/shard_map/all_gather | solution.py:60
  122.7 2.9 multiply_reduce_fusion.3
  125.8 3.8 fusion.45
  134.6 4.2 fusion.8
  138.8 78.3 %all-gather.13.cloned.1.call-done = bf16[1,7168,256]{2,1,0:T(8,128)(2,1)} async-done(((bf16[1,448,256]{2,1,0:T(8,128)(2,1)}), bf16[1,7168,256]{2,1,0:T(8,128)(2,1)}) %all-gather.13.cloned.1.call-update) | async-done | bytes 3670032 | tf_op jit(solution)/shard_map/all_gather | solution.py:61
  217.1 3.5 multiply_reduce_fusion.7
  220.6 52.1 %all-gather.15.cloned.1.call-done = bf16[1,256,7168]{1,2,0:T(8,128)(2,1)} async-done(((bf16[1,256,448]{1,2,0:T(8,128)(2,1)}), bf16[1,256,7168]{1,2,0:T(8,128)(2,1)}) %all-gather.15.cloned.1.call-update) | async-done | bytes 3670032 | tf_op jit(solution)/shard_map/all_gather | solution.py:62
  272.7 2.9 multiply_reduce_fusion.1
  275.9 3.8 fusion.41
  286.9 2.8 fusion.17
  289.7 33.4 %collective-permute-done.15 = bf16[128,7168]{1,0:T(8,128)(2,1)S(1)} collective-permute-done((bf16[128,7168]{1,0:T(8,128)(2,1)S(1)}, bf16[128,7168]{1,0:T(8,128)(2,1)S(1)}, u32[]{:S(2)}, u32[]{:S(2)}) %collective-permute-start.15) | collective-permute-done | bytes 1835040 | tf_op jit(solution)/shard_map/ppermute | solution.py:16
  325.5 3.7 pad_maximum_fusion.1
  329.2 18.5 %copy.21 = bf16[2,256,7168]{1,0,2:T(2,128)(2,1)} copy(bf16[2,256,7168]{2,1,0:T(8,128)(2,1)} %pad_maximum_fusion.1) | data formatting | bytes 14680064 | tf_op jit(solution)/shard_map/stack | solution.py:90
  348.0 3.5 multiply_reduce_fusion.2
  351.6 5.4 fusion.43
  358.4 3.3 fusion.19
  364.5 3.4 fusion.39
  369.8 2.9 fusion.7
  372.7 3.2 fusion.18
  376.0 6.8 pad_maximum_fusion
  385.0 3.5 multiply_reduce_fusion.15
  391.9 5.8 collective-permute-start
  400.9 3.6 multiply_reduce_fusion.13
  409.0 103.3 %collective-permute-done = bf16[128,7168]{1,0:T(8,128)(2,1)} collective-permute-done((bf16[128,7168]{1,0:T(8,128)(2,1)}, bf16[128,7168]{1,0:T(8,128)(2,1)}, u32[]{:S(2)}, u32[]{:S(2)}) %collective-permute-start) | collective-permute-done | bytes 1835040 | tf_op jit(solution)/shard_map/ppermute | solution.py:16
  516.9 4.2 fusion.29
  521.1 3.9 fusion.105
  527.9 3.4 multiply_reduce_fusion.12
  531.3 5.0 fusion.104
  536.3 68.5 %all-reduce.3.cloned.1.call-done = bf16[2,256,7168]{1,0,2:T(2,128)(2,1)} async-done(((bf16[2,256,7168]{1,0,2:T(2,128)(2,1)}), bf16[2,256,7168]{1,0,2:T(2,128)(2,1)}) %all-reduce.3.cloned.1.call-update) | async-done | bytes 7340048
  606.9 73.6 %reduce-scatter.10.cloned.1.call-done = bf16[448,2]{1,0:T(8,128)(2,1)} async-done(((bf16[7168,2]{1,0:T(8,128)(2,1)}), bf16[448,2]{1,0:T(8,128)(2,1)}) %reduce-scatter.10.cloned.1.call-update) | async-done | bytes 1808
  684.0 94.5 %reduce-scatter.8.cloned.1.call-done = bf16[2,448,256]{2,1,0:T(8,128)(2,1)} async-done(((bf16[2,7168,256]{2,1,0:T(8,128)(2,1)}), bf16[2,448,256]{2,1,0:T(8,128)(2,1)}) %reduce-scatter.8.cloned.1.call-update) | async-done | bytes 458768 | tf_op jit(solution)/shard_map/reduce_scatter | solution.py:93
  780.4 5.2 fusion.28
  787.1 55.9 %reduce-scatter.12.cloned.1.call-done = bf16[16,2]{1,0:T(8,128)(2,1)} async-done(((bf16[256,2]{1,0:T(8,128)(2,1)}), bf16[16,2]{1,0:T(8,128)(2,1)}) %reduce-scatter.12.cloned.1.call-update) | async-done | bytes 80
  851.1 3.0 collective-permute-start.24
  854.7 3.0 collective-permute-start.27
  859.8 7.4 collective-permute-done.20
  869.4 5.3 collective-permute-done.21
  (185 shorter events, 87.4 us)
Async XLA Ops:
  7.2 66.4 %copy-start.17 = (f32[1,7168]{1,0:T(1,128)S(1)}, f32[1,7168]{1,0:T(1,128)}, u32[]{:S(2)}) copy-start(f32[1,7168]{1,0:T(1,128)} %param.16) | copy-start | bytes 86020
  7.2 66.4 %all-gather.9.cloned.1.call-start = ((), (), s32[]{:S(2)}) async-start(), calls=%async_computation.4 | async-start | bytes 3899392 | tf_op jit(solution)/shard_map/all_gather | solution.py:59
  7.9 114.7 %all-gather.11.cloned.1.call-start = ((), (), s32[]{:S(2)}) async-start(), calls=%async_computation.5 | async-start | bytes 3899392 | tf_op jit(solution)/shard_map/all_gather | solution.py:60
  8.7 208.4 %all-gather.13.cloned.1.call-start = ((), (), s32[]{:S(2)}) async-start(), calls=%async_computation.6 | async-start | bytes 3899392 | tf_op jit(solution)/shard_map/all_gather | solution.py:61
  8.7 7.9 collective-permute-start.4
  16.6 6.8 collective-permute-start.5
  23.4 7.5 collective-permute-start.6
  31.6 241.1 %all-gather.15.cloned.1.call-start = ((), (), s32[]{:S(2)}) async-start(), calls=%async_computation.7 | async-start | bytes 3899392 | tf_op jit(solution)/shard_map/all_gather | solution.py:62
  31.7 6.3 collective-permute-start.10
  38.0 6.1 collective-permute-start.11
  44.1 8.3 collective-permute-start.12
  53.1 551.8 %all-reduce.3.cloned.1.call-start = ((), (), s32[]{:S(2)}) async-start(), calls=%async_computation.10 | async-start | bytes 14680064
  53.9 8.5 collective-permute-start.1
  56.5 4.1 collective-permute-start.7
  60.6 3.6 collective-permute-start.8
  62.4 5.8 collective-permute-start.2
  64.3 6.2 collective-permute-start.9
  68.2 5.4 collective-permute-start.3
  73.6 49.0 %copy-start.10 = (bf16[1,128,7168]{2,1,0:T(8,128)(2,1)S(1)}, bf16[1,128,7168]{2,1,0:T(8,128)(2,1)}, u32[]{:S(2)}) copy-start(bf16[1,128,7168]{2,1,0:T(8,128)(2,1)} %param.12) | copy-start | bytes 5505028
  73.6 49.0 %copy-start.21 = (f32[1,256]{1,0:T(1,128)S(1)}, f32[1,256]{1,0:T(1,128)}, u32[]{:S(2)}) copy-start(f32[1,256]{1,0:T(1,128)} %param.18) | copy-start | bytes 3076
  129.6 4.3 copy-start.22
  132.0 153.6 %collective-permute-start.14 = (bf16[128,7168]{1,0:T(8,128)(2,1)}, bf16[128,7168]{1,0:T(8,128)(2,1)}, u32[]{:S(2)}, u32[]{:S(2)}) collective-permute-start(bf16[128,7168]{1,0:T(8,128)(2,1)} %fusion.52), channel_id=1, source_target_pairs={{16,0},{32,16},{48,32},{64,48},{80,64},{96,80},{112,96},{17,1},{33... | collective-permute-start | bytes 5505032 | tf_op jit(solution)/shard_map/ppermute | solution.py:16
  217.1 55.7 %copy-start.11 = (bf16[1,128,7168]{2,1,0:T(8,128)(2,1)S(1)}, bf16[1,128,7168]{2,1,0:T(8,128)(2,1)}, u32[]{:S(2)}) copy-start(bf16[1,128,7168]{2,1,0:T(8,128)(2,1)} %param.13) | copy-start | bytes 5505028
  280.9 42.2 %collective-permute-start.15 = (bf16[128,7168]{1,0:T(8,128)(2,1)S(1)}, bf16[128,7168]{1,0:T(8,128)(2,1)S(1)}, u32[]{:S(2)}, u32[]{:S(2)}) collective-permute-start(bf16[128,7168]{1,0:T(8,128)(2,1)S(1)} %fusion.54), channel_id=1, source_target_pairs={{0,16},{16,32},{32,48},{48,64},{64,80},{80,96},{96,112},{1,17},{17... | collective-permute-start | bytes 5505032 | tf_op jit(solution)/shard_map/ppermute | solution.py:16
  347.7 332.8 %reduce-scatter.10.cloned.1.call-start = ((), (), s32[]{:S(2)}) async-start(), calls=%async_computation.8 | async-start | bytes 1949696
  358.4 5.0 copy-start.25
  375.9 402.6 %reduce-scatter.8.cloned.1.call-start = ((), (), s32[]{:S(2)}) async-start(), calls=%async_computation.3 | async-start | bytes 7798784 | tf_op jit(solution)/shard_map/reduce_scatter | solution.py:93
  382.8 460.2 %reduce-scatter.12.cloned.1.call-start = ((), (), s32[]{:S(2)}) async-start(), calls=%async_computation.9 | async-start | bytes 69632
  385.0 4.3 copy-start.14
  389.3 8.3 copy-start.26
  391.9 120.5 %collective-permute-start = (bf16[128,7168]{1,0:T(8,128)(2,1)}, bf16[128,7168]{1,0:T(8,128)(2,1)}, u32[]{:S(2)}, u32[]{:S(2)}) collective-permute-start(bf16[128,7168]{1,0:T(8,128)(2,1)} %fusion.20), channel_id=1, source_target_pairs={{0,16},{16,32},{32,48},{48,64},{64,80},{80,96},{96,112},{1,17},{17... | collective-permute-start | bytes 5505032 | tf_op jit(solution)/shard_map/ppermute | solution.py:16
  400.9 4.3 copy-start.15
  405.2 109.2 %copy-start.23 = (bf16[1,7168,256]{2,1,0:T(8,128)(2,1)S(1)}, bf16[1,7168,256]{2,1,0:T(8,128)(2,1)}, u32[]{:S(2)}) copy-start(bf16[1,7168,256]{2,1,0:T(8,128)(2,1)} %all-gather.9.cloned.1.call-done) | copy-start | bytes 11010052
  407.7 118.1 %collective-permute-start.13 = (bf16[128,7168]{1,0:T(8,128)(2,1)}, bf16[128,7168]{1,0:T(8,128)(2,1)}, u32[]{:S(2)}, u32[]{:S(2)}) collective-permute-start(bf16[128,7168]{1,0:T(8,128)(2,1)} %fusion.22), channel_id=1, source_target_pairs={{16,0},{32,16},{48,32},{64,48},{80,64},{96,80},{112,96},{17,1},{33... | collective-permute-start | bytes 5505032 | tf_op jit(solution)/shard_map/ppermute | solution.py:16
  516.9 4.2 copy-start.16
  606.8 75.7 %collective-permute-start.25 = (bf16[256,448]{0,1:T(8,128)(2,1)S(1)}, bf16[256,448]{0,1:T(8,128)(2,1)S(1)}, u32[]{:S(2)}, u32[]{:S(2)}) collective-permute-start(bf16[256,448]{0,1:T(8,128)(2,1)S(1)} %bitcast.261), channel_id=1, source_target_pairs={{0,16},{16,0},{32,48},{48,32},{64,80},{80,64},{96,112},{112,96},{1... | collective-permute-start | bytes 688136 | tf_op jit(solution)/shard_map/ppermute | solution.py:10
  681.7 104.0 %collective-permute-start.16 = (bf16[448]{0:T(512)(128)(2,1)S(1)}, bf16[448]{0:T(512)(128)(2,1)S(1)}, u32[]{:S(2)}, u32[]{:S(2)}) collective-permute-start(bf16[448]{0:T(512)(128)(2,1)S(1)} %get-tuple-element.36), channel_id=1, source_target_pairs={{0,16},{16,0},{32,48},{48,32},{64,80},{80,64},{96,112},{112,96},{1... | collective-permute-start | bytes 2696 | tf_op jit(solution)/shard_map/ppermute | solution.py:10
  682.5 172.1 %collective-permute-start.26 = (bf16[256,448]{0,1:T(8,128)(2,1)S(1)}, bf16[256,448]{0,1:T(8,128)(2,1)S(1)}, u32[]{:S(2)}, u32[]{:S(2)}) collective-permute-start(bf16[256,448]{0,1:T(8,128)(2,1)S(1)} %collective-permute-done.25), channel_id=1, source_target_pairs={{0,32},{16,48},{32,0},{48,16},{64,96},{80,112},{96,64},{112,80},{1... | collective-permute-start | bytes 688136 | tf_op jit(solution)/shard_map/ppermute | solution.py:10
  779.5 78.2 %collective-permute-start.19 = (bf16[448,256]{1,0:T(8,128)(2,1)S(1)}, bf16[448,256]{1,0:T(8,128)(2,1)S(1)}, u32[]{:S(2)}, u32[]{:S(2)}) collective-permute-start(bf16[448,256]{1,0:T(8,128)(2,1)S(1)} %slice_bitcast_fusion), channel_id=1, source_target_pairs={{0,16},{16,0},{32,48},{48,32},{64,80},{80,64},{96,112},{112,96},{1... | collective-permute-start | bytes 688136 | tf_op jit(solution)/shard_map/ppermute | solution.py:10
  780.4 94.2 %copy-start.18 = (bf16[2,448,256]{2,1,0:T(8,128)(2,1)S(1)}, bf16[2,448,256]{2,1,0:T(8,128)(2,1)}, u32[]{:S(2)}) copy-start(bf16[2,448,256]{2,1,0:T(8,128)(2,1)} %reduce-scatter.8.cloned.1.call-done) | copy-start | bytes 1376260
  785.6 68.5 %collective-permute-start.17 = (bf16[448]{0:T(512)(128)(2,1)S(1)}, bf16[448]{0:T(512)(128)(2,1)S(1)}, u32[]{:S(2)}, u32[]{:S(2)}) collective-permute-start(bf16[448]{0:T(512)(128)(2,1)S(1)} %collective-permute-done.16), channel_id=1, source_target_pairs={{0,32},{16,48},{32,0},{48,16},{64,96},{80,112},{96,64},{112,80},{1... | collective-permute-start | bytes 2696 | tf_op jit(solution)/shard_map/ppermute | solution.py:10
  844.0 3.5 collective-permute-start.22
  847.6 3.5 collective-permute-start.23
  851.1 7.1 collective-permute-start.24
  854.1 5.1 collective-permute-start.18
  854.7 13.9 %collective-permute-start.27 = (bf16[256,448]{0,1:T(8,128)(2,1)S(1)}, bf16[256,448]{0,1:T(8,128)(2,1)S(1)}, u32[]{:S(2)}, u32[]{:S(2)}) collective-permute-start(bf16[256,448]{0,1:T(8,128)(2,1)S(1)} %collective-permute-done.26), channel_id=1, source_target_pairs={{0,64},{16,80},{32,96},{48,112},{64,0},{80,16},{96,32},{112,48},{1... | collective-permute-start | bytes 688136 | tf_op jit(solution)/shard_map/ppermute | solution.py:10
  857.6 9.5 %collective-permute-start.20 = (bf16[448,256]{1,0:T(8,128)(2,1)S(1)}, bf16[448,256]{1,0:T(8,128)(2,1)S(1)}, u32[]{:S(2)}, u32[]{:S(2)}) collective-permute-start(bf16[448,256]{1,0:T(8,128)(2,1)S(1)} %collective-permute-done.19), channel_id=1, source_target_pairs={{0,32},{16,48},{32,0},{48,16},{64,96},{80,112},{96,64},{112,80},{1... | collective-permute-start | bytes 688136 | tf_op jit(solution)/shard_map/ppermute | solution.py:10
  867.2 7.5 collective-permute-start.21
  (17 other events, 48.0 us)
Sparse Core Ops, SparseCore 0:
  10.4 56.9 all-gather.8
  69.8 52.7 all-gather.10
  125.6 91.4 all-gather.12
  219.9 52.7 all-gather.14
  347.9 256.9 all-reduce.2
  608.6 71.8 reduce-scatter.9
  685.3 93.1 reduce-scatter.7
  782.6 60.3 reduce-scatter.11
where the time goes:
time: 890 us; the launch traced here: 883 us
  waiting for transfers between devices  658 us (74%)
  matrix products  82.5 us (9%)
  starting transfers between devices  52.4 us (6%)
  other arithmetic  40.5 us (5%)
  local copies, waits for them, and re-layouts  33.8 us (4%)
  between operations  15.5 us (2%)
    unnamed x11, waiting for transfers between devices  199 us
    ppermute x4, waiting for transfers between devices, from_behind(): return lax.ppermute(block, axis, route)  137 us
    reduce_scatter x1, waiting for transfers between devices, body(): lax.psum_scatter(paired[1], 'dp', scatter_dimension=1, tiled=True)  94.5 us
    all_gather x1, waiting for transfers between devices, body(): lax.all_gather(mirror_small[1], 'dp', axis=0, tiled=True)  78.3 us
    all_gather x1, waiting for transfers between devices, body(): lax.all_gather(mirror_small[3], 'dp', axis=1, tiled=True)  52.1 us
    ppermute x24, waiting for transfers between devices, swapped(): lax.ppermute(value, axis, [(i, i ^ 1 << distance) for i in range(lax.axis...  51.3 us
    dot_general x16, matrix products, layer(): latent = jnp.dot(normed, w_down, preferred_element_type=jnp.float32)  48.5 us
    all_gather x1, waiting for transfers between devices, body(): lax.all_gather(w_up[0], 'dp', axis=1, tiled=True)  45.5 us
  transfers between devices with their start and end apart: 36, of which 22 were waited for; matrix products, arithmetic and copies ran while one was open for 14% of the time, Pallas kernels for 0%

commit v1 on v0

v1 whole, which is shorter than its diff:
```python
import functools

import jax
import jax.numpy as jnp
from jax import lax
from jax.experimental import pallas as pl
from jax.experimental.pallas import tpu as pltpu
from jax.sharding import PartitionSpec as P

EPS = 1e-06
NX, NZ, NC = 4, 2, 2
NDP = NX * NZ * NC
CH = 512
BF = jnp.bfloat16
F32 = jnp.float32


def dp_move(value, fx=0, fz=0, fc=0):
    pairs = []
    for i in range(NDP):
        x, z, c = i // 4, (i // 2) % 2, i % 2
        pairs.append((i, ((x + fx) % NX) * 4 + (z ^ fz) * 2 + (c ^ fc)))
    return lax.ppermute(value, "dp", pairs)


def mirror(value):
    n = lax.axis_size("section")
    return lax.ppermute(value, "section", [(i, n - 1 - i) for i in range(n)])


def relay(value, distance):
    n = lax.axis_size("section")
    pairs = [(i - distance, i) for i in range(n) if 0 <= i - distance < n]
    return lax.ppermute(value, "section", pairs)


def spread(shard):
    other = dp_move(shard, fz=1)
    both = jnp.stack([shard, other])
    right = dp_move(both, fx=1)
    left = dp_move(both, fx=-1)
    far_a = dp_move(right[:, 0], fx=1)
    far_b = dp_move(left[:, 1], fx=-1)
    mine = (both, right, left, far_a, far_b)
    return mine + tuple(dp_move(p, fc=1) for p in mine)


def nt(a, b):
    return lax.dot_general(a, b, (((1,), (1,)), ((), ())), preferred_element_type=F32)


def nn(a, b):
    return lax.dot_general(a, b, (((1,), (0,)), ((), ())), preferred_element_type=F32)


def weight_copies(idx, pieces, wd, wu, sems):
    x, z, c = idx[0], idx[1], idx[2]
    rows = wd.shape[0] // NDP
    down, up = [], []
    n = 0

    def add(src, dst_ref, group, dx, dz, dc):
        nonlocal n
        place = ((x + dx) & 3) * 4 + ((z + dz) & 1) * 2 + ((c + dc) & 1)
        start = pl.multiple_of(place * rows, 64)
        group.append(pltpu.make_async_copy(src, dst_ref.at[pl.ds(start, rows), :], sems.at[n]))
        n += 1

    for dc in range(2):
        both, right, left, far_a, far_b = pieces[5 * dc : 5 * dc + 5]
        for dz in range(2):
            for ref, dx in ((both, 0), (right, 3), (left, 1)):
                add(ref.at[dz, 0], wd, down, dx, dz, dc)
                add(ref.at[dz, 1], wu, up, dx, dz, dc)
            add(far_a.at[dz], wd, down, 2, dz, dc)
            add(far_b.at[dz], wu, up, 2, dz, dc)
    return down, up


def chunks(ref):
    return ref.shape[1] // CH


def ds(k):
    return pl.ds(pl.multiple_of(k * CH, CH), CH)


def norm_scale(x_ref):
    def step(k, acc):
        xf = x_ref[:, ds(k)].astype(F32)
        sq = xf * xf
        part = sq[:, :128]
        for j in range(1, CH // 128):
            part = part + sq[:, 128 * j : 128 * (j + 1)]
        return acc + part

    acc = lax.fori_loop(0, chunks(x_ref), step, jnp.zeros((x_ref.shape[0], 128), F32))
    return lax.rsqrt(jnp.sum(acc, axis=1, keepdims=True) / x_ref.shape[1] + EPS)


def latent_of(x_ref, gain_ref, wd, nrm_ref, scale):
    def step(k, acc):
        xf = x_ref[:, ds(k)].astype(F32)
        normed = (xf * scale * gain_ref[:, ds(k)]).astype(BF)
        if nrm_ref is not None:
            nrm_ref[:, ds(k)] = normed
        return acc + nn(normed, wd[ds(k), :])

    return lax.fori_loop(0, chunks(x_ref), step, jnp.zeros((x_ref.shape[0], wd.shape[1]), F32))


def forward_kernel(idx, *refs):
    pieces = refs[:10]
    x_ref, gain_ref, lgain_ref, out_ref, wd, wu, sems = refs[10:]
    down, up = weight_copies(idx, pieces, wd, wu, sems)
    for cp in down + up:
        cp.start()
    scale = norm_scale(x_ref)
    for cp in down:
        cp.wait()
    latent = latent_of(x_ref, gain_ref, wd, None, scale)
    scale2 = lax.rsqrt(jnp.mean(latent * latent, axis=1, keepdims=True) + EPS)
    scaled = (latent * scale2 * lgain_ref[...]).astype(BF)
    for cp in up:
        cp.wait()

    def step(k, carry):
        y = x_ref[:, ds(k)].astype(F32) + nt(scaled, wu[ds(k), :])
        out_ref[:, ds(k)] = y.astype(BF)
        return carry

    lax.fori_loop(0, chunks(x_ref), step, 0)


def backward_core(x_ref, g_ref, gain_ref, lgain_ref, wd, wu, down, up, nrm_ref, dn_ref, dgain_ref, back_ref):
    scale = norm_scale(x_ref)
    for cp in down:
        cp.wait()
    latent = latent_of(x_ref, gain_ref, wd, nrm_ref, scale)
    scale2 = lax.rsqrt(jnp.mean(latent * latent, axis=1, keepdims=True) + EPS)
    n2 = latent * scale2
    lgain = lgain_ref[...]
    scaled = (n2 * lgain).astype(BF)
    for cp in up:
        cp.wait()

    def step_g(k, acc):
        return acc + nn(g_ref[:, ds(k)], wu[ds(k), :])

    rows = x_ref.shape[0]
    width = x_ref.shape[1]
    dsc = lax.fori_loop(0, chunks(x_ref), step_g, jnp.zeros((rows, wd.shape[1]), F32))
    dq = dsc.astype(BF).astype(F32)
    dlg = jnp.sum(dq * n2, axis=0, keepdims=True)
    dn2 = dq * lgain
    dlat = (scale2 * (dn2 - n2 * jnp.mean(dn2 * n2, axis=1, keepdims=True))).astype(BF)

    def step_n(k, acc):
        dn_bf = nt(dlat, wd[ds(k), :]).astype(BF)
        dn_ref[:, ds(k)] = dn_bf
        n1 = x_ref[:, ds(k)].astype(F32) * scale
        prod = dn_bf.astype(F32) * n1
        dgain_ref[:, ds(k)] = dgain_ref[:, ds(k)] + jnp.sum(prod, axis=0, keepdims=True)
        prod = prod * gain_ref[:, ds(k)]
        part = prod[:, :128]
        for j in range(1, CH // 128):
            part = part + prod[:, 128 * j : 128 * (j + 1)]
        return acc + part

    acc = lax.fori_loop(0, chunks(x_ref), step_n, jnp.zeros((rows, 128), F32))
    coeff = jnp.sum(acc, axis=1, keepdims=True) / width
    lean = scale * scale * coeff

    def step_x(k, carry):
        dx = dn_ref[:, ds(k)].astype(F32) * (gain_ref[:, ds(k)] * scale) - x_ref[:, ds(k)].astype(F32) * lean
        back_ref[:, ds(k)] = (g_ref[:, ds(k)].astype(F32) + dx).astype(BF)
        return carry

    lax.fori_loop(0, chunks(x_ref), step_x, 0)
    return scaled, dlat, dlg


def backward_first_kernel(idx, *refs):
    pieces = refs[:10]
    (x_ref, g_ref, gain_ref, lgain_ref, back_ref, nrm_ref, sc_ref, dlat_ref, dgain_ref, dlg_ref,
     wd, wu, dn_ref, sems) = refs[10:]
    down, up = weight_copies(idx, pieces, wd, wu, sems)
    for cp in down + up:
        cp.start()
    dgain_ref[...] = jnp.zeros(dgain_ref.shape, F32)
    scaled, dlat, dlg = backward_core(
        x_ref, g_ref, gain_ref, lgain_ref, wd, wu, down, up, nrm_ref, dn_ref, dgain_ref, back_ref
    )
    sc_ref[...] = scaled
    dlat_ref[...] = dlat
    dlg_ref[...] = dlg


def backward_last_kernel(idx, *refs):
    pieces = refs[:10]
    (x_ref, g_ref, gain_ref, lgain_ref, nrm0_ref, g0_ref, sc0_ref, dlat0_ref, dgain0_ref, dlg0_ref,
     back_ref, keep_ref, send_ref,
     wd, wu, dn_ref, nrm_ref, dgain_ref, grads, small, sems, out_sems) = refs[10:]
    down, up = weight_copies(idx, pieces, wd, wu, sems)
    for cp in down + up:
        cp.start()
    dgain_ref[...] = dgain0_ref[...]
    scaled, dlat, dlg = backward_core(
        x_ref, g_ref, gain_ref, lgain_ref, wd, wu, down, up, nrm_ref, dn_ref, dgain_ref, back_ref
    )
    rank = wd.shape[1]
    half = rank // 2
    span = x_ref.shape[1] // (NX * NZ)
    dlat_t = jnp.concatenate([dlat0_ref[...], dlat], axis=0).astype(F32).T.astype(BF)
    sc_t = jnp.concatenate([sc0_ref[...], scaled], axis=0).astype(F32).T.astype(BF)

    def step(k, carry):
        n_all = jnp.concatenate([nrm0_ref[:, ds(k)], nrm_ref[:, ds(k)]], axis=0)
        grads[0, :, ds(k)] = nn(dlat_t, n_all).astype(BF)
        g_all = jnp.concatenate([g0_ref[:, ds(k)], g_ref[:, ds(k)]], axis=0)
        grads[1, :, ds(k)] = nn(sc_t, g_all).astype(BF)
        return carry

    lax.fori_loop(0, chunks(x_ref), step, 0)
    small[...] = jnp.zeros(small.shape, BF)
    small[0:1, :] = dgain_ref[...].astype(BF)
    dlg_all = (dlg0_ref[...] + dlg).astype(BF)
    for j in range(NX * NZ):
        small[1:2, j * span : j * span + rank] = dlg_all
    x, z, c = idx[0], idx[1], idx[2]
    copies = []
    for side, out in ((0, keep_ref), (1, send_ref)):
        row = pl.multiple_of(((c + side) & 1) * half, half)
        for dx in range(NX):
            for dz in range(NZ):
                lane = pl.multiple_of((((x + dx) & 3) * 2 + ((z + dz) & 1)) * span, 128)
                for m in range(2):
                    copies.append((
                        grads.at[m, pl.ds(row, half), pl.ds(lane, span)],
                        out.at[dx, dz, pl.ds(m * half, half), :],
                    ))
                copies.append((small.at[:, pl.ds(lane, span)], out.at[dx, dz, pl.ds(rank, 16), :]))
    started = [pltpu.make_async_copy(a, b, out_sems.at[n]) for n, (a, b) in enumerate(copies)]
    for cp in started:
        cp.start()
    for cp in started:
        cp.wait()


SMEM = functools.partial(pl.BlockSpec, memory_space=pltpu.SMEM)
VMEM = functools.partial(pl.BlockSpec, memory_space=pltpu.VMEM)
ANY = functools.partial(pl.BlockSpec, memory_space=pl.ANY)


def weight_scratch(width, rank):
    return [pltpu.VMEM((width, rank), BF), pltpu.VMEM((width, rank), BF)]


def forward(idx, pieces, x, gain, lgain):
    t, width = x.shape
    rank = lgain.shape[1]
    return pl.pallas_call(
        forward_kernel,
        out_shape=jax.ShapeDtypeStruct(x.shape, BF),
        in_specs=[SMEM()] + [ANY()] * 10 + [VMEM()] * 3,
        out_specs=VMEM(),
        scratch_shapes=weight_scratch(width, rank) + [pltpu.SemaphoreType.DMA((32,))],
        compiler_params=pltpu.CompilerParams(vmem_limit_bytes=32 << 20),
        cost_estimate=pl.CostEstimate(flops=4 * t * width * rank, transcendentals=0, bytes_accessed=4 * width * (t + rank)),
        name="forward",
    )(idx, *pieces, x, gain, lgain)


def backward_first(idx, pieces, x, g, gain, lgain):
    t, width = x.shape
    rank = lgain.shape[1]
    act = jax.ShapeDtypeStruct(x.shape, BF)
    lat = jax.ShapeDtypeStruct((t, rank), BF)
    return pl.pallas_call(
        backward_first_kernel,
        out_shape=(act, act, lat, lat, jax.ShapeDtypeStruct((1, width), F32), jax.ShapeDtypeStruct((1, rank), F32)),
        in_specs=[SMEM()] + [ANY()] * 10 + [VMEM()] * 4,
        out_specs=(VMEM(),) * 6,
        scratch_shapes=weight_scratch(width, rank) + [pltpu.VMEM(x.shape, BF), pltpu.SemaphoreType.DMA((32,))],
        compiler_params=pltpu.CompilerParams(vmem_limit_bytes=40 << 20),
        cost_estimate=pl.CostEstimate(flops=6 * t * width * rank, transcendentals=0, bytes_accessed=4 * width * (2 * t + rank)),
        name="backward_first",
    )(idx, *pieces, x, g, gain, lgain)


def backward_last(idx, pieces, x, g, gain, lgain, first, g0):
    t, width = x.shape
    rank = lgain.shape[1]
    act = jax.ShapeDtypeStruct(x.shape, BF)
    span = width // (NX * NZ)
    block = jax.ShapeDtypeStruct((NX, NZ, rank + 16, span), BF)
    _, nrm0, sc0, dlat0, dgain0, dlg0 = first
    return pl.pallas_call(
        backward_last_kernel,
        out_shape=(act, block, block),
        in_specs=[SMEM()] + [ANY()] * 10 + [VMEM()] * 10,
        out_specs=(VMEM(), ANY(), ANY()),
        scratch_shapes=weight_scratch(width, rank)
        + [
            pltpu.VMEM(x.shape, BF),
            pltpu.VMEM(x.shape, BF),
            pltpu.VMEM((1, width), F32),
            pltpu.VMEM((2, rank, width), BF),
            pltpu.VMEM((16, width), BF),
            pltpu.SemaphoreType.DMA((32,)),
            pltpu.SemaphoreType.DMA((NX * NZ * 6,)),
        ],
        compiler_params=pltpu.CompilerParams(vmem_limit_bytes=48 << 20),
        cost_estimate=pl.CostEstimate(flops=14 * t * width * rank, transcendentals=0, bytes_accessed=4 * width * (4 * t + 2 * rank)),
        name="backward_last",
    )(idx, *pieces, x, g, gain, lgain, nrm0, g0, sc0, dlat0, dgain0, dlg0)


def gather_sums(keep, send):
    half = 128
    recv = dp_move(send, fc=1)

    def both(dx):
        return keep[dx].astype(F32) + recv[dx].astype(F32)

    far = both(2).astype(BF)
    got_a = dp_move(far[:, :half], fx=1).astype(F32)
    got_b = dp_move(far[:, half:], fx=-1).astype(F32)
    rows = keep.shape[2]
    got_a = jnp.pad(got_a, ((0, 0), (0, rows - half), (0, 0)))
    got_b = jnp.pad(got_b, ((0, 0), (half, 0), (0, 0)))
    from_left = dp_move((both(1) + got_a).astype(BF), fx=1)
    from_right = dp_move((both(3) + got_b).astype(BF), fx=-1)
    total = both(0) + from_left.astype(F32) + from_right.astype(F32)
    across = dp_move(total[1].astype(BF), fz=1)
    return total[0] + across.astype(F32)


def body(enter_a, enter_b, cotan_a, cotan_b, saved_a, saved_b, norm_gain, w_down, latent_gain, w_up):
    place = lax.axis_index("dp")
    core = place % 2
    idx = jnp.stack([place // 4, (place // 2) % 2, core]).astype(jnp.int32)
    width = norm_gain.shape[1]
    rank = latent_gain.shape[1]
    cols = w_up.shape[2]

    shard = jnp.stack([w_down[0], w_up[0].T])
    gains = jnp.concatenate([norm_gain[0], latent_gain[0]]).reshape(-1, 128)
    own = spread(shard)
    other = spread(mirror(shard))
    gains_m = mirror(gains).reshape(1, -1)
    gain_a, lgain_a = norm_gain, latent_gain
    gain_b, lgain_b = gains_m[:, :width], gains_m[:, width:]

    first_a = backward_first(idx, own, saved_a[0, 0], cotan_a[0], gain_a, lgain_a)
    ga = relay(first_a[0], -1)
    xa = relay(forward(idx, own, enter_a[0], gain_a, lgain_a), 1)
    first_b = backward_first(idx, other, saved_b[0, 0], cotan_b[0], gain_b, lgain_b)
    gb = relay(first_b[0], 1)
    xb = relay(forward(idx, other, enter_b[0], gain_b, lgain_b), -1)

    back_a, keep_a, send_a = backward_last(idx, own, saved_a[1, 0], ga, gain_a, lgain_a, first_a, cotan_a[0])
    back_b, keep_b, send_b = backward_last(idx, other, saved_b[1, 0], gb, gain_b, lgain_b, first_b, cotan_b[0])
    sum_b = gather_sums(keep_b, send_b)
    sum_a = gather_sums(keep_a, send_a)
    total = sum_a + mirror(sum_b.astype(BF)).astype(F32)

    out_a = forward(idx, own, xa, gain_a, lgain_a)
    out_b = forward(idx, other, xb, gain_b, lgain_b)

    mats = total[:rank].reshape(2, rank // 2, 2, cols)
    mine = jnp.where(core == 0, mats[:, :, 0], mats[:, :, 1])
    yours = jnp.where(core == 0, mats[:, :, 1], mats[:, :, 0])
    got = dp_move(yours, fc=1)
    grads = jnp.where(
        core == 0, jnp.concatenate([mine, got], axis=1), jnp.concatenate([got, mine], axis=1)
    )
    row = total[rank].reshape(2, cols)
    grad_gain = jnp.where(core == 0, row[0], row[1])
    grad_lgain = lax.dynamic_slice(total[rank + 1, :rank], (place * (rank // NDP),), (rank // NDP,))
    return (
        out_a[None],
        out_b[None],
        back_a[None],
        back_b[None],
        grad_gain[None],
        grads[0].T[None],
        grad_lgain[None],
        grads[1][None],
    )


def solution(mesh):
    act = P("section", "dp", None)
    placed = (
        act,
        act,
        act,
        act,
        P(None, "section", "dp", None),
        P(None, "section", "dp", None),
        P("section", None),
        P("section", "dp", None),
        P("section", None),
        P("section", None, "dp"),
    )
    return jax.shard_map(
        body,
        mesh=mesh,
        in_specs=placed,
        out_specs=(act, act, act, act, P("section", "dp"), act, P("section", "dp"), P("section", None, "dp")),
        check_vma=False,
    )
```

time: 890 us -> 499 us (0.56)
  waiting for transfers between devices: 658 us -> 212 us
  Pallas kernels: 0 us -> 175 us
  matrix products: 82.5 us -> 0 us
  other arithmetic: 40.5 us -> 16.6 us
  between operations: 15.5 us -> 1.42 us
    unnamed x11 -> x0, waiting for transfers between devices: 199 us -> none
    all_gather x4 -> x0, waiting for transfers between devices: 176 us -> none  [the longest x1 78.3 us: body(): lax.all_gather(mirror_small[1], 'dp', axis=0, tiled=True)]
    pallas_call x0 -> x8, Pallas kernels: none -> 175 us  [the longest x4 70.5 us: forward(): pl.pallas_call(forward_kernel, out_shape=jax.ShapeDtypeStruct(x.shape, BF...]
    reduce_scatter x1 -> x0, waiting for transfers between devices: 94.5 us -> none  [body(): lax.psum_scatter(paired[1], 'dp', scatter_dimension=1, tiled=True)]
    dot_general x28 -> x0, matrix products: 82.5 us -> none  [the longest x16 48.5 us: layer(): latent = jnp.dot(normed, w_down, preferred_element_type=jnp.float32)]
    ppermute x28 -> x40, waiting for transfers between devices: 188 us -> 212 us  [the longest x33 141 us: dp_move(): return lax.ppermute(value, 'dp', pairs)]
    another operation x1, local copies, waits for them, and re-layouts: 18.5 us -> 0.06 us  [spread(): both = jnp.stack([shard, other])]
    reduce_sum x6 -> x0, other arithmetic: 11.8 us -> none  [layer(): jnp.mean(xf * xf, axis=-1, keepdims=True) + 1e-06]
  transfers between devices with their start and end apart: 36 -> 40, of which waited for: 22 -> 16; matrix products, arithmetic and copies ran while one was open for 14% -> 7% of each run, Pallas kernels for 0% -> 35%
where the time goes in v1:
time: 499 us; the launch traced here: 497 us
  waiting for transfers between devices  212 us (42%)
  Pallas kernels  175 us (35%)
  starting transfers between devices  53.4 us (11%)
  local copies, waits for them, and re-layouts  38.4 us (8%)
  other arithmetic  16.6 us (3%)
    ppermute x33, waiting for transfers between devices, dp_move(): return lax.ppermute(value, 'dp', pairs)  141 us
    pallas_call x4, Pallas kernels, forward(): pl.pallas_call(forward_kernel, out_shape=jax.ShapeDtypeStruct(x.shape, BF...  70.5 us
    pallas_call x2, Pallas kernels, backward_last(): pl.pallas_call(backward_last_kernel, out_shape=(act, block, block), in_sp...  59.7 us
    ppermute x4, waiting for transfers between devices, relay(): return lax.ppermute(value, 'section', pairs)  52.3 us
    pallas_call x2, Pallas kernels, backward_first(): pl.pallas_call(backward_first_kernel, out_shape=(act, act, lat, lat, jax....  44.8 us
    ppermute x33, starting transfers between devices, dp_move(): return lax.ppermute(value, 'dp', pairs)  33.7 us
    unnamed x107, local copies, waits for them, and re-layouts  19.7 us
    ppermute x3, waiting for transfers between devices, mirror(): return lax.ppermute(value, 'section', [(i, n - 1 - i) for i in range(n)])  18.6 us
  transfers between devices with their start and end apart: 40, of which 16 were waited for; matrix products, arithmetic and copies ran while one was open for 7% of the time, Pallas kernels for 35%

profile of v1, /device:TPU:0, one launch (start us, length us, event | category | flops | bytes accessed | tf_op | source)
XLA Modules:
  0.0 496.9 jit_solution(17549078878942145866)
XLA Ops:
  1.8 4.5 collective-permute-start.11
  6.3 10.5 %collective-permute-done.11 = bf16[2,448,256]{2,1,0:T(8,128)(2,1)S(1)} collective-permute-done((bf16[2,448,256]{2,1,0:T(8,128)(2,1)S(1)}, bf16[2,448,256]{2,1,0:T(8,128)(2,1)S(1)}, u32[]{:S(2)}, u32[]{:S(2)}) %collective-permute-start.11) | collective-permute-done | bytes 458784 | tf_op jit(solution)/shard_map/ppermute | solution.py:28
  16.8 3.6 collective-permute-start.12
  20.4 11.4 %collective-permute-done.12 = bf16[2,448,256]{2,1,0:T(8,128)(2,1)S(1)} collective-permute-done((bf16[2,448,256]{2,1,0:T(8,128)(2,1)S(1)}, bf16[2,448,256]{2,1,0:T(8,128)(2,1)S(1)}, u32[]{:S(2)}, u32[]{:S(2)}) %collective-permute-start.12) | collective-permute-done | bytes 458784 | tf_op jit(solution)/shard_map/ppermute | solution.py:23
  33.5 1.7 collective-permute-start.14
  35.2 4.9 collective-permute-done
  41.8 1.7 collective-permute-start.2
  43.6 3.3 collective-permute-start.22
  46.9 2.8 collective-permute-done.22
  49.7 6.8 %collective-permute-done.13 = bf16[2,2,448,256]{3,2,0,1:T(8,128)(2,1)S(1)} collective-permute-done((bf16[2,2,448,256]{3,2,0,1:T(8,128)(2,1)S(1)}, bf16[2,2,448,256]{3,2,0,1:T(8,128)(2,1)S(1)}, u32[]{:S(2)}, u32[]{:S(2)}) %collective-permute-start.13) | collective-permute-done | bytes 917536 | tf_op jit(solution)/shard_map/ppermute | solution.py:23
  57.1 15.1 %collective-permute-done.1.refs_1_ = bf16[2,2,448,256]{3,2,1,0:T(8,128)(2,1)S(1)} collective-permute-done((bf16[2,2,448,256]{3,2,1,0:T(8,128)(2,1)S(1)}, bf16[2,2,448,256]{3,2,1,0:T(8,128)(2,1)S(1)}, u32[]{:S(2)}, u32[]{:S(2)}) %collective-permute-start.1) | collective-permute-done | bytes 917536 | tf_op jit(solution)/shard_map/ppermute | solution.py:23
  73.7 1.7 collective-permute-start.16
  77.1 5.1 %collective-permute-done.15.refs_3_ = bf16[2,448,256]{2,1,0:T(8,128)(2,1)S(1)} collective-permute-done((bf16[2,448,256]{2,1,0:T(8,128)(2,1)S(1)}, bf16[2,448,256]{2,1,0:T(8,128)(2,1)S(1)}, u32[]{:S(2)}, u32[]{:S(2)}) %collective-permute-start.15) | collective-permute-done | bytes 458784 | tf_op jit(solution)/shard_map/ppermute | solution.py:23
  83.8 1.8 collective-permute-start.4
  87.5 2.1 slice_bitcast_fusion
  92.7 1.7 copy-done.50
  95.9 22.4 %backward_first.3 = (bf16[128,7168]{1,0:T(8,128)(2,1)S(1)}, bf16[128,7168]{1,0:T(8,128)(2,1)S(1)}, bf16[128,256]{1,0:T(8,128)(2,1)S(1)}, bf16[128,256]{1,0:T(8,1...) custom-call(s32[3]{0:T(128)S(1)} %pad_add_fusion.idx, bf16[2,2,448,256]{3,2,1,0:T(8,128)(2,1)S(1)} %copy.52.refs_0_, ...), custom_call_target="tpu_custom_call" | custom-call | flops 1409286144 | bytes 14680064 | tf_op jit(solution)/shard_map/backward_first/pallas_call | solution.py:279
  118.3 3.4 collective-permute-start.25
  123.3 22.5 %backward_first.2 = (bf16[128,7168]{1,0:T(8,128)(2,1)S(1)}, bf16[128,7168]{1,0:T(8,128)(2,1)S(1)}, bf16[128,256]{1,0:T(8,128)(2,1)S(1)}, bf16[128,256]{1,0:T(8,1...) custom-call(s32[3]{0:T(128)S(1)} %pad_add_fusion.idx, bf16[2,2,448,256]{3,2,1,0:T(8,128)(2,1)S(1)} %pad_maximum_fusion.refs_0_, ...), custom_call_target="tpu_custom_call" | custom-call | flops 1409286144 | bytes 14680064 | tf_op jit(solution)/shard_map/backward_first/pallas_call | solution.py:279
  148.5 52.3 %collective-permute-done.25.refs_11_ = bf16[128,7168]{1,0:T(8,128)(2,1)S(1)} collective-permute-done((bf16[128,7168]{1,0:T(8,128)(2,1)S(1)}, bf16[128,7168]{1,0:T(8,128)(2,1)S(1)}, u32[]{:S(2)}, u32[]{:S(2)}) %collective-permute-start.25) | collective-permute-done | bytes 1835040 | tf_op jit(solution)/shard_map/ppermute | solution.py:34
  202.0 30.2 %backward_last.3 = (bf16[128,7168]{1,0:T(8,128)(2,1)}, bf16[4,2,272,896]{3,2,1,0:T(8,128)(2,1)}, bf16[4,2,272,896]{3,2,1,0:T(8,128)(2,1)}) custom-call(s32[3]{0:T(128)S(1)} %pad_add_fusion.idx, bf16[2,2,448,256]{3,2,1,0:T(8,128)(2,1)S(1)} %copy.52.refs_0_, bf16[2,2,448,256]{3,2,1,0:T(8,128)(2,1)S(1)} %copy.53.refs_1_, ...), custom_call_target="tpu_custom_call" | custom-call | flops 3288334336 | bytes 29360128 | tf_op jit(solution)/shard_map/backward_last/pallas_call | solution.py:298
  233.6 29.5 %backward_last.2 = (bf16[128,7168]{1,0:T(8,128)(2,1)}, bf16[4,2,272,896]{3,2,1,0:T(8,128)(2,1)}, bf16[4,2,272,896]{3,2,1,0:T(8,128)(2,1)}) custom-call(s32[3]{0:T(128)S(1)} %pad_add_fusion.idx, bf16[2,2,448,256]{3,2,1,0:T(8,128)(2,1)S(1)} %pad_maximum_fusion.refs_0_, bf16[2,2,448,256]{3,2,1,0:T(8,128)(2,1)S(1)} %copy-done.11, ...), custom_call_target="tpu_custom_call" | custom-call | flops 3288334336 | bytes 29360128 | tf_op jit(solution)/shard_map/backward_last/pallas_call | solution.py:298
  263.7 1.6 fusion.7
  265.3 1.6 collective-permute-start.35
  267.6 2.7 collective-permute-done.26
  270.6 1.6 collective-permute-start.29
  272.7 9.0 %collective-permute-done.33 = bf16[2,128,896]{2,1,0:T(8,128)(2,1)S(1)} collective-permute-done((bf16[2,128,896]{2,1,0:T(8,128)(2,1)S(1)}, bf16[2,128,896]{2,1,0:T(8,128)(2,1)S(1)}, u32[]{:S(2)}, u32[]{:S(2)}) %collective-permute-start.33) | collective-permute-done | bytes 458784 | tf_op jit(solution)/shard_map/ppermute | solution.py:23
  281.7 2.1 fusion.1
  283.9 3.2 collective-permute-start.36
  287.1 4.4 collective-permute-done.27
  293.1 3.2 collective-permute-start.30
  296.4 16.8 %forward.4 = bf16[128,7168]{1,0:T(8,128)(2,1)} custom-call(s32[3]{0:T(128)S(1)} %pad_add_fusion.idx, bf16[2,2,448,256]{3,2,1,0:T(8,128)(2,1)S(1)} %pad_maximum_fusion.refs_0_, bf16[2,2,448,256]{3,2,1,0:T(8,128)(2,1)S(1)} %copy-done.11, bf16[2,2,448,256]{3,2,1,0:T(8,128)(2,1)S(1)} %copy-done.14, bf16[2,448,256]{2,1,0:T(8,128)(2,1)} %collective-permute-done.3.refs_3_, ...), custom_call_target="tpu_custom_call" | custom-call | flops 939524096 | bytes 11010048 | tf_op jit(solution)/shard_map/forward/pallas_call | solution.py:262
  313.2 5.7 %collective-permute-start.10 = (bf16[128,7168]{1,0:T(8,128)(2,1)}, bf16[128,7168]{1,0:T(8,128)(2,1)}, u32[]{:S(2)}, u32[]{:S(2)}) collective-permute-start(bf16[128,7168]{1,0:T(8,128)(2,1)} %forward.4), channel_id=1, source_target_pairs={{0,16},{16,32},{32,48},{48,64},{64,80},{80,96},{96,112},{1,17},{17... | collective-permute-start | bytes 5505032 | tf_op jit(solution)/shard_map/ppermute | solution.py:34
  318.9 17.5 %forward.6 = bf16[128,7168]{1,0:T(8,128)(2,1)} custom-call(s32[3]{0:T(128)S(1)} %pad_add_fusion.idx, bf16[2,2,448,256]{3,2,1,0:T(8,128)(2,1)S(1)} %copy.52.refs_0_, bf16[2,2,448,256]{3,2,1,0:T(8,128)(2,1)S(1)} %copy.53.refs_1_, bf16[2,2,448,256]{3,2,1,0:T(8,128)(2,1)S(1)} %copy.54.refs_2_, bf16[2,448,256]{2,1,0:T(8,128)(2,1)S(1)} %collective-permute-done.15.refs_3_, ...), custom_call_target="tpu_custom_call" | custom-call | flops 939524096 | bytes 11010048 | tf_op jit(solution)/shard_map/forward/pallas_call | solution.py:262
  337.7 1.9 fusion.2
  339.7 3.7 collective-permute-start.37
  343.4 1.6 fusion.5
  347.2 75.3 %collective-permute-done.37 = bf16[272,896]{1,0:T(8,128)(2,1)S(1)} collective-permute-done((bf16[272,896]{1,0:T(8,128)(2,1)S(1)}, bf16[272,896]{1,0:T(8,128)(2,1)S(1)}, u32[]{:S(2)}, u32[]{:S(2)}) %collective-permute-start.37) | collective-permute-done | bytes 487456 | tf_op jit(solution)/shard_map/ppermute | solution.py:23
  423.4 5.9 %collective-permute-done.31 = bf16[272,896]{1,0:T(8,128)(2,1)} collective-permute-done((bf16[272,896]{1,0:T(8,128)(2,1)}, bf16[272,896]{1,0:T(8,128)(2,1)}, u32[]{:S(2)}, u32[]{:S(2)}) %collective-permute-start.31) | collective-permute-done | bytes 487456 | tf_op jit(solution)/shard_map/ppermute | solution.py:23
  429.3 5.3 %collective-permute-done.38 = bf16[272,896]{1,0:T(8,128)(2,1)} collective-permute-done((bf16[272,896]{1,0:T(8,128)(2,1)}, bf16[272,896]{1,0:T(8,128)(2,1)}, u32[]{:S(2)}, u32[]{:S(2)}) %collective-permute-start.38) | collective-permute-done | bytes 487456 | tf_op jit(solution)/shard_map/ppermute | solution.py:28
  434.6 1.6 fusion.11
  438.2 3.1 reshape.66
  441.3 3.5 fusion.15
  444.8 1.9 copy.74
  446.7 1.9 copy.75
  448.6 1.6 select_bitcast_fusion.1
  454.9 17.7 %forward.5 = bf16[128,7168]{1,0:T(8,128)(2,1)} custom-call(s32[3]{0:T(128)S(1)} %pad_add_fusion.idx, bf16[2,2,448,256]{3,2,1,0:T(8,128)(2,1)S(1)} %pad_maximum_fusion.refs_0_, bf16[2,2,448,256]{3,2,1,0:T(8,128)(2,1)S(1)} %copy-done.12, bf16[2,2,448,256]{3,2,1,0:T(8,128)(2,1)S(1)} %copy-done.15, bf16[2,448,256]{2,1,0:T(8,128)(2,1)} %collective-permute-done.3.refs_3_, ...), custom_call_target="tpu_custom_call" | custom-call | flops 939524096 | bytes 11010048 | tf_op jit(solution)/shard_map/forward/pallas_call | solution.py:262
  472.7 18.5 %forward.7 = bf16[128,7168]{1,0:T(8,128)(2,1)} custom-call(s32[3]{0:T(128)S(1)} %pad_add_fusion.idx, bf16[2,2,448,256]{3,2,1,0:T(8,128)(2,1)S(1)} %copy.52.refs_0_, bf16[2,2,448,256]{3,2,1,0:T(8,128)(2,1)S(1)} %copy.53.refs_1_, bf16[2,2,448,256]{3,2,1,0:T(8,128)(2,1)S(1)} %copy-done.1, bf16[2,448,256]{2,1,0:T(8,128)(2,1)S(1)} %collective-permute-done.15.refs_3_, ...), custom_call_target="tpu_custom_call" | custom-call | flops 939524096 | bytes 11010048 | tf_op jit(solution)/shard_map/forward/pallas_call | solution.py:262
  (189 shorter events, 43.3 us)
Async XLA Ops:
  1.7 41.8 %copy-start.33 = (f32[1,7168]{1,0:T(1,128)S(1)}, f32[1,7168]{1,0:T(1,128)}, u32[]{:S(2)}) copy-start(f32[1,7168]{1,0:T(1,128)} %refs_12_.7) | copy-start | bytes 86020
  1.8 41.8 %copy-start.34 = (f32[1,256]{1,0:T(1,128)S(1)}, f32[1,256]{1,0:T(1,128)}, u32[]{:S(2)}) copy-start(f32[1,256]{1,0:T(1,128)} %refs_13_.3) | copy-start | bytes 3076
  1.8 15.0 %collective-permute-start.11 = (bf16[2,448,256]{2,1,0:T(8,128)(2,1)S(1)}, bf16[2,448,256]{2,1,0:T(8,128)(2,1)S(1)}, u32[]{:S(2)}, u32[]{:S(2)}) collective-permute-start(bf16[2,448,256]{2,1,0:T(8,128)(2,1)S(1)} %get-tuple-element.67), channel_id=1, source_target_pairs={{0,112},{16,96},{32,80},{48,64},{64,48},{80,32},{96,16},{112,0},{1... | collective-permute-start | bytes 1376264 | tf_op jit(solution)/shard_map/ppermute | solution.py:28
  16.8 15.0 %collective-permute-start.12 = (bf16[2,448,256]{2,1,0:T(8,128)(2,1)S(1)}, bf16[2,448,256]{2,1,0:T(8,128)(2,1)S(1)}, u32[]{:S(2)}, u32[]{:S(2)}) collective-permute-start(bf16[2,448,256]{2,1,0:T(8,128)(2,1)S(1)} %collective-permute-done.11), channel_id=1, source_target_pairs={{0,2},{1,3},{2,0},{3,1},{4,6},{5,7},{6,4},{7,5},{8,10},{9,11},{10,... | collective-permute-start | bytes 1376264 | tf_op jit(solution)/shard_map/ppermute | solution.py:23
  20.4 19.7 %collective-permute-start = (bf16[2,448,256]{2,1,0:T(8,128)(2,1)S(1)}, bf16[2,448,256]{2,1,0:T(8,128)(2,1)S(1)}, u32[]{:S(2)}, u32[]{:S(2)}) collective-permute-start(bf16[2,448,256]{2,1,0:T(8,128)(2,1)S(1)} %get-tuple-element.67), channel_id=1, source_target_pairs={{0,2},{1,3},{2,0},{3,1},{4,6},{5,7},{6,4},{7,5},{8,10},{9,11},{10,... | collective-permute-start | bytes 1376264 | tf_op jit(solution)/shard_map/ppermute | solution.py:23
  31.9 24.6 %collective-permute-start.13 = (bf16[2,2,448,256]{3,2,0,1:T(8,128)(2,1)S(1)}, bf16[2,2,448,256]{3,2,0,1:T(8,128)(2,1)S(1)}, u32[]{:S(2)}, u32[]{:S(2)}) collective-permute-start(bf16[2,2,448,256]{3,2,0,1:T(8,128)(2,1)S(1)} %pad_maximum_fusion.1), channel_id=1, source_target_pairs={{0,4},{1,5},{2,6},{3,7},{4,8},{5,9},{6,10},{7,11},{8,12},{9,13},{1... | collective-permute-start | bytes 2752520 | tf_op jit(solution)/shard_map/ppermute | solution.py:23
  33.5 23.3 %collective-permute-start.14 = (bf16[2,2,448,256]{3,2,0,1:T(8,128)(2,1)S(1)}, bf16[2,2,448,256]{3,2,0,1:T(8,128)(2,1)S(1)}, u32[]{:S(2)}, u32[]{:S(2)}) collective-permute-start(bf16[2,2,448,256]{3,2,0,1:T(8,128)(2,1)S(1)} %pad_maximum_fusion.1), channel_id=1, source_target_pairs={{0,12},{1,13},{2,14},{3,15},{4,0},{5,1},{6,2},{7,3},{8,4},{9,5},{1... | collective-permute-start | bytes 2752520 | tf_op jit(solution)/shard_map/ppermute | solution.py:23
  40.2 47.3 %copy-start.39 = (bf16[2,1,128,7168]{3,2,1,0:T(8,128)(2,1)S(1)}, bf16[2,1,128,7168]{3,2,1,0:T(8,128)(2,1)}, u32[]{:S(2)}) copy-start(bf16[2,1,128,7168]{3,2,1,0:T(8,128)(2,1)} %param.15) | copy-start | bytes 11010052
  40.2 31.9 %collective-permute-start.1 = (bf16[2,2,448,256]{3,2,1,0:T(8,128)(2,1)S(1)}, bf16[2,2,448,256]{3,2,1,0:T(8,128)(2,1)S(1)}, u32[]{:S(2)}, u32[]{:S(2)}) collective-permute-start(bf16[2,2,448,256]{3,2,1,0:T(8,128)(2,1)S(1)} %pad_maximum_fusion.refs_0_), channel_id=1, source_target_pairs={{0,4},{1,5},{2,6},{3,7},{4,8},{5,9},{6,10},{7,11},{8,12},{9,13},{1... | collective-permute-start | bytes 2752520 | tf_op jit(solution)/shard_map/ppermute | solution.py:23
  41.8 31.9 %collective-permute-start.2 = (bf16[2,2,448,256]{3,2,1,0:T(8,128)(2,1)S(1)}, bf16[2,2,448,256]{3,2,1,0:T(8,128)(2,1)S(1)}, u32[]{:S(2)}, u32[]{:S(2)}) collective-permute-start(bf16[2,2,448,256]{3,2,1,0:T(8,128)(2,1)S(1)} %pad_maximum_fusion.refs_0_), channel_id=1, source_target_pairs={{0,12},{1,13},{2,14},{3,15},{4,0},{5,1},{6,2},{7,3},{8,4},{9,5},{1... | collective-permute-start | bytes 2752520 | tf_op jit(solution)/shard_map/ppermute | solution.py:23
  43.6 6.1 %collective-permute-start.22 = (f32[58,128]{1,0:T(8,128)S(1)}, f32[58,128]{1,0:T(8,128)S(1)}, u32[]{:S(2)}, u32[]{:S(2)}) collective-permute-start(f32[58,128]{1,0:T(8,128)S(1)} %maximum_bitcast_fusion), channel_id=1, source_target_pairs={{0,112},{16,96},{32,80},{48,64},{64,48},{80,32},{96,16},{112,0},{1... | collective-permute-start | bytes 89096 | tf_op jit(solution)/shard_map/ppermute | solution.py:28
  49.7 27.4 %collective-permute-start.17 = (bf16[2,2,448,256]{3,2,0,1:T(8,128)(2,1)S(1)}, bf16[2,2,448,256]{3,2,0,1:T(8,128)(2,1)S(1)}, u32[]{:S(2)}, u32[]{:S(2)}) collective-permute-start(bf16[2,2,448,256]{3,2,0,1:T(8,128)(2,1)S(1)} %pad_maximum_fusion.1), channel_id=1, source_target_pairs={{0,1},{1,0},{2,3},{3,2},{4,5},{5,4},{6,7},{7,6},{8,9},{9,8},{10,11... | collective-permute-start | bytes 2752520 | tf_op jit(solution)/shard_map/ppermute | solution.py:23
  56.5 29.2 %collective-permute-start.18 = (bf16[2,2,448,256]{3,2,0,1:T(8,128)(2,1)S(1)}, bf16[2,2,448,256]{3,2,0,1:T(8,128)(2,1)S(1)}, u32[]{:S(2)}, u32[]{:S(2)}) collective-permute-start(bf16[2,2,448,256]{3,2,0,1:T(8,128)(2,1)S(1)} %collective-permute-done.13), channel_id=1, source_target_pairs={{0,1},{1,0},{2,3},{3,2},{4,5},{5,4},{6,7},{7,6},{8,9},{9,8},{10,11... | collective-permute-start | bytes 2752520 | tf_op jit(solution)/shard_map/ppermute | solution.py:23
  56.8 29.0 %collective-permute-start.19 = (bf16[2,2,448,256]{3,2,0,1:T(8,128)(2,1)S(1)}, bf16[2,2,448,256]{3,2,0,1:T(8,128)(2,1)S(1)}, u32[]{:S(2)}, u32[]{:S(2)}) collective-permute-start(bf16[2,2,448,256]{3,2,0,1:T(8,128)(2,1)S(1)} %collective-permute-done.14), channel_id=1, source_target_pairs={{0,1},{1,0},{2,3},{3,2},{4,5},{5,4},{6,7},{7,6},{8,9},{9,8},{10,11... | collective-permute-start | bytes 2752520 | tf_op jit(solution)/shard_map/ppermute | solution.py:23
  72.2 10.1 %collective-permute-start.15 = (bf16[2,448,256]{2,1,0:T(8,128)(2,1)S(1)}, bf16[2,448,256]{2,1,0:T(8,128)(2,1)S(1)}, u32[]{:S(2)}, u32[]{:S(2)}) collective-permute-start(bf16[2,448,256]{2,1,0:T(8,128)(2,1)S(1)} %slice_bitcast_fusion.7), channel_id=1, source_target_pairs={{0,4},{1,5},{2,6},{3,7},{4,8},{5,9},{6,10},{7,11},{8,12},{9,13},{1... | collective-permute-start | bytes 1376264 | tf_op jit(solution)/shard_map/ppermute | solution.py:23
  73.7 10.2 %collective-permute-start.16 = (bf16[2,448,256]{2,1,0:T(8,128)(2,1)S(1)}, bf16[2,448,256]{2,1,0:T(8,128)(2,1)}, u32[]{:S(2)}, u32[]{:S(2)}) collective-permute-start(bf16[2,448,256]{2,1,0:T(8,128)(2,1)S(1)} %slice_bitcast_fusion.6), channel_id=1, source_target_pairs={{0,12},{1,13},{2,14},{3,15},{4,0},{5,1},{6,2},{7,3},{8,4},{9,5},{1... | collective-permute-start | bytes 1376264 | tf_op jit(solution)/shard_map/ppermute | solution.py:23
  77.0 41.3 %collective-permute-start.5 = (bf16[2,2,448,256]{3,2,1,0:T(8,128)(2,1)S(1)}, bf16[2,2,448,256]{3,2,1,0:T(8,128)(2,1)}, u32[]{:S(2)}, u32[]{:S(2)}) collective-permute-start(bf16[2,2,448,256]{3,2,1,0:T(8,128)(2,1)S(1)} %pad_maximum_fusion.refs_0_), channel_id=1, source_target_pairs={{0,1},{1,0},{2,3},{3,2},{4,5},{5,4},{6,7},{7,6},{8,9},{9,8},{10,11... | collective-permute-start | bytes 2752520 | tf_op jit(solution)/shard_map/ppermute | solution.py:23
  82.3 12.2 %collective-permute-start.3 = (bf16[2,448,256]{2,1,0:T(8,128)(2,1)}, bf16[2,448,256]{2,1,0:T(8,128)(2,1)}, u32[]{:S(2)}, u32[]{:S(2)}) collective-permute-start(bf16[2,448,256]{2,1,0:T(8,128)(2,1)} %slice_bitcast_fusion.9), channel_id=1, source_target_pairs={{0,4},{1,5},{2,6},{3,7},{4,8},{5,9},{6,10},{7,11},{8,12},{9,13},{1... | collective-permute-start | bytes 1376264 | tf_op jit(solution)/shard_map/ppermute | solution.py:23
  83.8 11.3 %collective-permute-start.4 = (bf16[2,448,256]{2,1,0:T(8,128)(2,1)}, bf16[2,448,256]{2,1,0:T(8,128)(2,1)}, u32[]{:S(2)}, u32[]{:S(2)}) collective-permute-start(bf16[2,448,256]{2,1,0:T(8,128)(2,1)} %slice_bitcast_fusion.8), channel_id=1, source_target_pairs={{0,12},{1,13},{2,14},{3,15},{4,0},{5,1},{6,2},{7,3},{8,4},{9,5},{1... | collective-permute-start | bytes 1376264 | tf_op jit(solution)/shard_map/ppermute | solution.py:23
  85.7 9.7 %collective-permute-start.20 = (bf16[2,448,256]{2,1,0:T(8,128)(2,1)S(1)}, bf16[2,448,256]{2,1,0:T(8,128)(2,1)}, u32[]{:S(2)}, u32[]{:S(2)}) collective-permute-start(bf16[2,448,256]{2,1,0:T(8,128)(2,1)S(1)} %collective-permute-done.15.refs_3_), channel_id=1, source_target_pairs={{0,1},{1,0},{2,3},{3,2},{4,5},{5,4},{6,7},{7,6},{8,9},{9,8},{10,11... | collective-permute-start | bytes 1376264 | tf_op jit(solution)/shard_map/ppermute | solution.py:23
  87.5 8.1 %collective-permute-start.21 = (bf16[2,448,256]{2,1,0:T(8,128)(2,1)}, bf16[2,448,256]{2,1,0:T(8,128)(2,1)}, u32[]{:S(2)}, u32[]{:S(2)}) collective-permute-start(bf16[2,448,256]{2,1,0:T(8,128)(2,1)} %collective-permute-done.16.refs_4_), channel_id=1, source_target_pairs={{0,1},{1,0},{2,3},{3,2},{4,5},{5,4},{6,7},{7,6},{8,9},{9,8},{10,11... | collective-permute-start | bytes 1376264 | tf_op jit(solution)/shard_map/ppermute | solution.py:23
  92.5 226.4 %copy-start = (bf16[2,2,448,256]{3,2,1,0:T(8,128)(2,1)}, bf16[2,2,448,256]{3,2,1,0:T(8,128)(2,1)S(1)}, u32[]{:S(2)}) copy-start(bf16[2,2,448,256]{3,2,1,0:T(8,128)(2,1)S(1)} %copy.54.refs_2_) | copy-start | bytes 2752516
  92.6 226.2 %copy-start.2 = (bf16[2,2,448,256]{3,2,1,0:T(8,128)(2,1)}, bf16[2,2,448,256]{3,2,1,0:T(8,128)(2,1)S(1)}, u32[]{:S(2)}) copy-start(bf16[2,2,448,256]{3,2,1,0:T(8,128)(2,1)S(1)} %copy.55.refs_5_) | copy-start | bytes 2752516
  94.6 28.6 %collective-permute-start.6 = (bf16[2,2,448,256]{3,2,1,0:T(8,128)(2,1)S(1)}, bf16[2,2,448,256]{3,2,1,0:T(8,128)(2,1)S(1)}, u32[]{:S(2)}, u32[]{:S(2)}) collective-permute-start(bf16[2,2,448,256]{3,2,1,0:T(8,128)(2,1)S(1)} %copy-done.11), channel_id=1, source_target_pairs={{0,1},{1,0},{2,3},{3,2},{4,5},{5,4},{6,7},{7,6},{8,9},{9,8},{10,11... | collective-permute-start | bytes 2752520 | tf_op jit(solution)/shard_map/ppermute | solution.py:23
  95.1 28.1 %collective-permute-start.7 = (bf16[2,2,448,256]{3,2,1,0:T(8,128)(2,1)S(1)}, bf16[2,2,448,256]{3,2,1,0:T(8,128)(2,1)S(1)}, u32[]{:S(2)}, u32[]{:S(2)}) collective-permute-start(bf16[2,2,448,256]{3,2,1,0:T(8,128)(2,1)S(1)} %copy-done.14), channel_id=1, source_target_pairs={{0,1},{1,0},{2,3},{3,2},{4,5},{5,4},{6,7},{7,6},{8,9},{9,8},{10,11... | collective-permute-start | bytes 2752520 | tf_op jit(solution)/shard_map/ppermute | solution.py:23
  95.4 27.8 %collective-permute-start.8 = (bf16[2,448,256]{2,1,0:T(8,128)(2,1)}, bf16[2,448,256]{2,1,0:T(8,128)(2,1)S(1)}, u32[]{:S(2)}, u32[]{:S(2)}) collective-permute-start(bf16[2,448,256]{2,1,0:T(8,128)(2,1)} %collective-permute-done.3.refs_3_), channel_id=1, source_target_pairs={{0,1},{1,0},{2,3},{3,2},{4,5},{5,4},{6,7},{7,6},{8,9},{9,8},{10,11... | collective-permute-start | bytes 1376264 | tf_op jit(solution)/shard_map/ppermute | solution.py:23
  95.7 27.6 %collective-permute-start.9 = (bf16[2,448,256]{2,1,0:T(8,128)(2,1)}, bf16[2,448,256]{2,1,0:T(8,128)(2,1)S(1)}, u32[]{:S(2)}, u32[]{:S(2)}) collective-permute-start(bf16[2,448,256]{2,1,0:T(8,128)(2,1)} %collective-permute-done.4.refs_4_), channel_id=1, source_target_pairs={{0,1},{1,0},{2,3},{3,2},{4,5},{5,4},{6,7},{7,6},{8,9},{9,8},{10,11... | collective-permute-start | bytes 1376264 | tf_op jit(solution)/shard_map/ppermute | solution.py:23
  118.3 82.5 %collective-permute-start.25 = (bf16[128,7168]{1,0:T(8,128)(2,1)S(1)}, bf16[128,7168]{1,0:T(8,128)(2,1)S(1)}, u32[]{:S(2)}, u32[]{:S(2)}) collective-permute-start(bf16[128,7168]{1,0:T(8,128)(2,1)S(1)} %get-tuple-element.33), channel_id=1, source_target_pairs={{0,16},{16,32},{32,48},{48,64},{64,80},{80,96},{96,112},{1,17},{17... | collective-permute-start | bytes 5505032 | tf_op jit(solution)/shard_map/ppermute | solution.py:34
  147.0 85.3 %collective-permute-start.24 = (bf16[128,7168]{1,0:T(8,128)(2,1)S(1)}, bf16[128,7168]{1,0:T(8,128)(2,1)S(1)}, u32[]{:S(2)}, u32[]{:S(2)}) collective-permute-start(bf16[128,7168]{1,0:T(8,128)(2,1)S(1)} %get-tuple-element.26), channel_id=1, source_target_pairs={{16,0},{32,16},{48,32},{64,48},{80,64},{96,80},{112,96},{17,1},{33... | collective-permute-start | bytes 5505032 | tf_op jit(solution)/shard_map/ppermute | solution.py:34
  202.0 31.6 %copy-start.24 = (bf16[2,448,256]{2,1,0:T(8,128)(2,1)S(1)}, bf16[2,448,256]{2,1,0:T(8,128)(2,1)}, u32[]{:S(2)}) copy-start(bf16[2,448,256]{2,1,0:T(8,128)(2,1)} %copy-done.23) | copy-start | bytes 1376260
  202.0 31.6 %copy-start.27 = (bf16[2,448,256]{2,1,0:T(8,128)(2,1)S(1)}, bf16[2,448,256]{2,1,0:T(8,128)(2,1)}, u32[]{:S(2)}) copy-start(bf16[2,448,256]{2,1,0:T(8,128)(2,1)} %copy-done.26) | copy-start | bytes 1376260
  232.3 31.4 %collective-permute-start.32 = (bf16[4,2,272,896]{3,2,1,0:T(8,128)(2,1)}, bf16[4,2,272,896]{3,2,1,0:T(8,128)(2,1)}, u32[]{:S(2)}, u32[]{:S(2)}) collective-permute-start(bf16[4,2,272,896]{3,2,1,0:T(8,128)(2,1)} %get-tuple-element.43), channel_id=1, source_target_pairs={{0,1},{1,0},{2,3},{3,2},{4,5},{5,4},{6,7},{7,6},{8,9},{9,8},{10,11... | collective-permute-start | bytes 11698184 | tf_op jit(solution)/shard_map/ppermute | solution.py:23
  233.6 30.1 %copy-start.36 = (bf16[4,2,272,896]{3,2,1,0:T(8,128)(2,1)S(1)}, bf16[4,2,272,896]{3,2,1,0:T(8,128)(2,1)}, u32[]{:S(2)}) copy-start(bf16[4,2,272,896]{3,2,1,0:T(8,128)(2,1)} %get-tuple-element.42) | copy-start | bytes 11698180
  263.1 7.1 %collective-permute-start.26 = (bf16[4,2,272,896]{3,2,1,0:T(8,128)(2,1)}, bf16[4,2,272,896]{3,2,1,0:T(8,128)(2,1)S(1)}, u32[]{:S(2)}, u32[]{:S(2)}) collective-permute-start(bf16[4,2,272,896]{3,2,1,0:T(8,128)(2,1)} %get-tuple-element.41), channel_id=1, source_target_pairs={{0,1},{1,0},{2,3},{3,2},{4,5},{5,4},{6,7},{7,6},{8,9},{9,8},{10,11... | collective-permute-start | bytes 11698184 | tf_op jit(solution)/shard_map/ppermute | solution.py:23
  265.3 16.4 %collective-permute-start.35 = (bf16[2,144,896]{2,1,0:T(8,128)(2,1)S(1)}, bf16[2,144,896]{2,1,0:T(8,128)(2,1)S(1)}, u32[]{:S(2)}, u32[]{:S(2)}) collective-permute-start(bf16[2,144,896]{2,1,0:T(8,128)(2,1)S(1)} %slice.196), channel_id=1, source_target_pairs={{0,12},{1,13},{2,14},{3,15},{4,0},{5,1},{6,2},{7,3},{8,4},{9,5},{1... | collective-permute-start | bytes 1548296 | tf_op jit(solution)/shard_map/ppermute | solution.py:23
  267.0 14.7 %collective-permute-start.33 = (bf16[2,128,896]{2,1,0:T(8,128)(2,1)S(1)}, bf16[2,128,896]{2,1,0:T(8,128)(2,1)S(1)}, u32[]{:S(2)}, u32[]{:S(2)}) collective-permute-start(bf16[2,128,896]{2,1,0:T(8,128)(2,1)S(1)} %slice.194), channel_id=1, source_target_pairs={{0,4},{1,5},{2,6},{3,7},{4,8},{5,9},{6,10},{7,11},{8,12},{9,13},{1... | collective-permute-start | bytes 1376264 | tf_op jit(solution)/shard_map/ppermute | solution.py:23
  270.6 20.9 %collective-permute-start.29 = (bf16[2,144,896]{2,1,0:T(8,128)(2,1)S(1)}, bf16[2,144,896]{2,1,0:T(8,128)(2,1)S(1)}, u32[]{:S(2)}, u32[]{:S(2)}) collective-permute-start(bf16[2,144,896]{2,1,0:T(8,128)(2,1)S(1)} %slice.188), channel_id=1, source_target_pairs={{0,12},{1,13},{2,14},{3,15},{4,0},{5,1},{6,2},{7,3},{8,4},{9,5},{1... | collective-permute-start | bytes 1548296 | tf_op jit(solution)/shard_map/ppermute | solution.py:23
  272.2 19.3 %collective-permute-start.27 = (bf16[2,128,896]{2,1,0:T(8,128)(2,1)S(1)}, bf16[2,128,896]{2,1,0:T(8,128)(2,1)S(1)}, u32[]{:S(2)}, u32[]{:S(2)}) collective-permute-start(bf16[2,128,896]{2,1,0:T(8,128)(2,1)S(1)} %slice.186), channel_id=1, source_target_pairs={{0,4},{1,5},{2,6},{3,7},{4,8},{5,9},{6,10},{7,11},{8,12},{9,13},{1... | collective-permute-start | bytes 1376264 | tf_op jit(solution)/shard_map/ppermute | solution.py:23
  283.8 52.6 %collective-permute-start.34 = (bf16[2,272,896]{2,1,0:T(8,128)(2,1)S(1)}, bf16[2,272,896]{2,1,0:T(8,128)(2,1)S(1)}, u32[]{:S(2)}, u32[]{:S(2)}) collective-permute-start(bf16[2,272,896]{2,1,0:T(8,128)(2,1)S(1)} %get-tuple-element.52), channel_id=1, source_target_pairs={{0,4},{1,5},{2,6},{3,7},{4,8},{5,9},{6,10},{7,11},{8,12},{9,13},{1... | collective-permute-start | bytes 2924552 | tf_op jit(solution)/shard_map/ppermute | solution.py:23
  283.9 53.8 %collective-permute-start.36 = (bf16[2,272,896]{2,1,0:T(8,128)(2,1)S(1)}, bf16[2,272,896]{2,1,0:T(8,128)(2,1)S(1)}, u32[]{:S(2)}, u32[]{:S(2)}) collective-permute-start(bf16[2,272,896]{2,1,0:T(8,128)(2,1)S(1)} %get-tuple-element.53), channel_id=1, source_target_pairs={{0,12},{1,13},{2,14},{3,15},{4,0},{5,1},{6,2},{7,3},{8,4},{9,5},{1... | collective-permute-start | bytes 2924552 | tf_op jit(solution)/shard_map/ppermute | solution.py:23
  293.1 50.3 %collective-permute-start.28 = (bf16[2,272,896]{2,1,0:T(8,128)(2,1)}, bf16[2,272,896]{2,1,0:T(8,128)(2,1)S(1)}, u32[]{:S(2)}, u32[]{:S(2)}) collective-permute-start(bf16[2,272,896]{2,1,0:T(8,128)(2,1)} %get-tuple-element.54), channel_id=1, source_target_pairs={{0,4},{1,5},{2,6},{3,7},{4,8},{5,9},{6,10},{7,11},{8,12},{9,13},{1... | collective-permute-start | bytes 2924552 | tf_op jit(solution)/shard_map/ppermute | solution.py:23
  293.1 50.3 %collective-permute-start.30 = (bf16[2,272,896]{2,1,0:T(8,128)(2,1)S(1)}, bf16[2,272,896]{2,1,0:T(8,128)(2,1)}, u32[]{:S(2)}, u32[]{:S(2)}) collective-permute-start(bf16[2,272,896]{2,1,0:T(8,128)(2,1)S(1)} %get-tuple-element.55), channel_id=1, source_target_pairs={{0,12},{1,13},{2,14},{3,15},{4,0},{5,1},{6,2},{7,3},{8,4},{9,5},{1... | collective-permute-start | bytes 2924552 | tf_op jit(solution)/shard_map/ppermute | solution.py:23
  313.2 137.1 %collective-permute-start.10 = (bf16[128,7168]{1,0:T(8,128)(2,1)}, bf16[128,7168]{1,0:T(8,128)(2,1)}, u32[]{:S(2)}, u32[]{:S(2)}) collective-permute-start(bf16[128,7168]{1,0:T(8,128)(2,1)} %forward.4), channel_id=1, source_target_pairs={{0,16},{16,32},{32,48},{48,64},{64,80},{80,96},{96,112},{1,17},{17... | collective-permute-start | bytes 5505032 | tf_op jit(solution)/shard_map/ppermute | solution.py:34
  336.4 136.2 %collective-permute-start.23 = (bf16[128,7168]{1,0:T(8,128)(2,1)}, bf16[128,7168]{1,0:T(8,128)(2,1)}, u32[]{:S(2)}, u32[]{:S(2)}) collective-permute-start(bf16[128,7168]{1,0:T(8,128)(2,1)} %forward.6), channel_id=1, source_target_pairs={{16,0},{32,16},{48,32},{64,48},{80,64},{96,80},{112,96},{17,1},{33... | collective-permute-start | bytes 5505032 | tf_op jit(solution)/shard_map/ppermute | solution.py:34
  339.7 82.8 %collective-permute-start.37 = (bf16[272,896]{1,0:T(8,128)(2,1)S(1)}, bf16[272,896]{1,0:T(8,128)(2,1)S(1)}, u32[]{:S(2)}, u32[]{:S(2)}) collective-permute-start(bf16[272,896]{1,0:T(8,128)(2,1)S(1)} %fusion.13), channel_id=1, source_target_pairs={{0,2},{1,3},{2,0},{3,1},{4,6},{5,7},{6,4},{7,5},{8,10},{9,11},{10,... | collective-permute-start | bytes 1462280 | tf_op jit(solution)/shard_map/ppermute | solution.py:23
  347.2 82.1 %collective-permute-start.31 = (bf16[272,896]{1,0:T(8,128)(2,1)}, bf16[272,896]{1,0:T(8,128)(2,1)}, u32[]{:S(2)}, u32[]{:S(2)}) collective-permute-start(bf16[272,896]{1,0:T(8,128)(2,1)} %fusion.12), channel_id=1, source_target_pairs={{0,2},{1,3},{2,0},{3,1},{4,6},{5,7},{6,4},{7,5},{8,10},{9,11},{10,... | collective-permute-start | bytes 1462280 | tf_op jit(solution)/shard_map/ppermute | solution.py:23
  423.4 11.2 %collective-permute-start.38 = (bf16[272,896]{1,0:T(8,128)(2,1)}, bf16[272,896]{1,0:T(8,128)(2,1)}, u32[]{:S(2)}, u32[]{:S(2)}) collective-permute-start(bf16[272,896]{1,0:T(8,128)(2,1)} %fusion.9), channel_id=1, source_target_pairs={{0,112},{16,96},{32,80},{48,64},{64,48},{80,32},{96,16},{112,0},{1... | collective-permute-start | bytes 1462280 | tf_op jit(solution)/shard_map/ppermute | solution.py:28
  450.2 43.7 %collective-permute-start.39 = (f32[2,128,448]{1,0,2:T(2,128)S(1)}, f32[2,128,448]{1,0,2:T(2,128)S(1)}, u32[]{:S(2)}, u32[]{:S(2)}) collective-permute-start(f32[2,128,448]{1,0,2:T(2,128)S(1)} %get-tuple-element.65), channel_id=1, source_target_pairs={{0,1},{1,0},{2,3},{3,2},{4,5},{5,4},{6,7},{7,6},{8,9},{9,8},{10,11... | collective-permute-start | bytes 1376264 | tf_op jit(solution)/shard_map/ppermute | solution.py:23
  (43 other events, 474.7 us)

commit v2 on v1

v2 whole, which is shorter than its diff:
```python
import functools

import jax
import jax.numpy as jnp
from jax import lax
from jax.experimental import pallas as pl
from jax.experimental.pallas import tpu as pltpu
from jax.sharding import PartitionSpec as P

EPS = 1e-06
LATE = 1
NX, NZ, NC = 4, 2, 2
NDP = NX * NZ * NC
CH = 1024
BF = jnp.bfloat16
F32 = jnp.float32


def dp_move(value, fx=0, fz=0, fc=0):
    pairs = []
    for i in range(NDP):
        x, z, c = i // 4, (i // 2) % 2, i % 2
        pairs.append((i, ((x + fx) % NX) * 4 + (z ^ fz) * 2 + (c ^ fc)))
    return lax.ppermute(value, "dp", pairs)


def mirror(value, fz=0):
    n = lax.axis_size("section")
    pairs = [
        (s * NDP + i, (n - 1 - s) * NDP + (i ^ (fz * NC))) for s in range(n) for i in range(NDP)
    ]
    return lax.ppermute(value, ("section", "dp"), pairs)


def relay(value, distance, fc=0):
    n = lax.axis_size("section")
    pairs = [
        ((s - distance) * NDP + i, s * NDP + (i ^ fc))
        for s in range(n)
        if 0 <= s - distance < n
        for i in range(NDP)
    ]
    return lax.ppermute(value, ("section", "dp"), pairs)


def after(value, *others):
    return lax.optimization_barrier((value, *others))[0]


def ring(near):
    return near, dp_move(near, fx=1), dp_move(near, fx=-1)


def far_halves(group):
    near, right, left = group
    return group + (dp_move(right[..., 0, :, :], fx=1), dp_move(left[..., 1, :, :], fx=-1))


def other_core(group):
    return tuple(dp_move(p, fc=1) for p in group)


def nt(a, b):
    return lax.dot_general(a, b, (((1,), (1,)), ((), ())), preferred_element_type=F32)


def nn(a, b):
    return lax.dot_general(a, b, (((1,), (0,)), ((), ())), preferred_element_type=F32)


def place_pieces(idx, pieces, wd, wu):
    x, z, c = idx[0], idx[1], idx[2]
    rows = wd.shape[0] // NDP

    def put(dst_ref, value, dx, dz, dc):
        place = ((x + dx) & 3) * 4 + ((z + dz) & 1) * 2 + ((c + dc) & 1)
        dst_ref[pl.ds(pl.multiple_of(place * rows, 64), rows), :] = value

    many = len(pieces) == 5 * NC
    for n in range(NZ * NC):
        dc, dz = n // NZ, n % NZ
        group = pieces[5 * dc : 5 * dc + 5] if many else pieces[5 * n : 5 * n + 5]
        at = (dz,) if many else ()
        for ref, dx in ((group[0], 0), (group[1], 3), (group[2], 1)):
            put(wd, ref[at + (0,)], dx, dz, dc)
            put(wu, ref[at + (1,)], dx, dz, dc)
        put(wd, group[3][at] if many else group[3][...], 2, dz, dc)
        put(wu, group[4][at] if many else group[4][...], 2, dz, dc)


def chunks(ref):
    return ref.shape[1] // CH


def ds(k):
    return pl.ds(pl.multiple_of(k * CH, CH), CH)


def norm_scale(x_ref):
    def step(k, acc):
        xf = x_ref[:, ds(k)].astype(F32)
        sq = xf * xf
        part = sq[:, :128]
        for j in range(1, CH // 128):
            part = part + sq[:, 128 * j : 128 * (j + 1)]
        return acc + part

    acc = lax.fori_loop(0, chunks(x_ref), step, jnp.zeros((x_ref.shape[0], 128), F32))
    return lax.rsqrt(jnp.sum(acc, axis=1, keepdims=True) / x_ref.shape[1] + EPS)


def latent_of(x_ref, gain_ref, wd, nrm_ref, scale):
    def step(k, acc):
        xf = x_ref[:, ds(k)].astype(F32)
        normed = (xf * scale * gain_ref[:, ds(k)]).astype(BF)
        if nrm_ref is not None:
            nrm_ref[:, ds(k)] = normed
        return acc + nn(normed, wd[ds(k), :])

    return lax.fori_loop(0, chunks(x_ref), step, jnp.zeros((x_ref.shape[0], wd.shape[1]), F32))


def forward_kernel(x_ref, gain_ref, lgain_ref, wd, wu, out_ref):
    scale = norm_scale(x_ref)
    latent = latent_of(x_ref, gain_ref, wd, None, scale)
    scale2 = lax.rsqrt(jnp.mean(latent * latent, axis=1, keepdims=True) + EPS)
    scaled = (latent * scale2 * lgain_ref[...]).astype(BF)

    def step(k, carry):
        y = x_ref[:, ds(k)].astype(F32) + nt(scaled, wu[ds(k), :])
        out_ref[:, ds(k)] = y.astype(BF)
        return carry

    lax.fori_loop(0, chunks(x_ref), step, 0)


def backward_core(x_ref, g_ref, gain_ref, lgain_ref, wd, wu, nrm_ref, dn_ref, dgain_ref, back_ref):
    scale = norm_scale(x_ref)
    latent = latent_of(x_ref, gain_ref, wd, nrm_ref, scale)
    scale2 = lax.rsqrt(jnp.mean(latent * latent, axis=1, keepdims=True) + EPS)
    n2 = latent * scale2
    lgain = lgain_ref[...]
    scaled = (n2 * lgain).astype(BF)

    def step_g(k, acc):
        return acc + nn(g_ref[:, ds(k)], wu[ds(k), :])

    rows = x_ref.shape[0]
    width = x_ref.shape[1]
    dsc = lax.fori_loop(0, chunks(x_ref), step_g, jnp.zeros((rows, wd.shape[1]), F32))
    dq = dsc.astype(BF).astype(F32)
    dlg = jnp.sum(dq * n2, axis=0, keepdims=True)
    dn2 = dq * lgain
    dlat = (scale2 * (dn2 - n2 * jnp.mean(dn2 * n2, axis=1, keepdims=True))).astype(BF)

    def step_n(k, acc):
        dn_bf = nt(dlat, wd[ds(k), :]).astype(BF)
        dn_ref[:, ds(k)] = dn_bf
        n1 = x_ref[:, ds(k)].astype(F32) * scale
        prod = dn_bf.astype(F32) * n1
        dgain_ref[:, ds(k)] = dgain_ref[:, ds(k)] + jnp.sum(prod, axis=0, keepdims=True)
        prod = prod * gain_ref[:, ds(k)]
        part = prod[:, :128]
        for j in range(1, CH // 128):
            part = part + prod[:, 128 * j : 128 * (j + 1)]
        return acc + part

    acc = lax.fori_loop(0, chunks(x_ref), step_n, jnp.zeros((rows, 128), F32))
    coeff = jnp.sum(acc, axis=1, keepdims=True) / width
    lean = scale * scale * coeff

    def step_x(k, carry):
        dx = dn_ref[:, ds(k)].astype(F32) * (gain_ref[:, ds(k)] * scale) - x_ref[:, ds(k)].astype(F32) * lean
        back_ref[:, ds(k)] = (g_ref[:, ds(k)].astype(F32) + dx).astype(BF)
        return carry

    lax.fori_loop(0, chunks(x_ref), step_x, 0)
    return scaled, dlat, dlg


def backward_first_kernel(idx, *refs):
    (x_ref, g_ref, gain_ref, lgain_ref, back_ref, nrm_ref, sc_ref, dlat_ref, dgain_ref, dlg_ref,
     wd, wu, dn_ref) = refs[-13:]
    place_pieces(idx, refs[:-13], wd, wu)
    dgain_ref[...] = jnp.zeros(dgain_ref.shape, F32)
    scaled, dlat, dlg = backward_core(
        x_ref, g_ref, gain_ref, lgain_ref, wd, wu, nrm_ref, dn_ref, dgain_ref, back_ref
    )
    sc_ref[...] = scaled
    dlat_ref[...] = dlat
    dlg_ref[...] = dlg


def backward_last_kernel(idx, x_ref, g_ref, gain_ref, lgain_ref, wd, wu, nrm0_ref, g0_ref, sc0_ref, dlat0_ref,
                         dgain0_ref, dlg0_ref, back_ref, *refs):
    keep, send, (dn_ref, nrm_ref, dgain_ref) = refs[:NX], refs[NX : 2 * NX], refs[2 * NX :]
    dgain_ref[...] = dgain0_ref[...]
    scaled, dlat, dlg = backward_core(
        x_ref, g_ref, gain_ref, lgain_ref, wd, wu, nrm_ref, dn_ref, dgain_ref, back_ref
    )
    rank = wd.shape[1]
    half = rank // 2
    span = x_ref.shape[1] // (NX * NZ)
    x, z, c = idx[0], idx[1], idx[2]

    def rows_of(first, second):
        whole = jnp.concatenate([first, second], axis=0).astype(F32).T
        low, high = whole[:half], whole[half:]
        return jnp.where(c == 0, whole, jnp.concatenate([high, low], axis=0)).astype(BF)

    dlat_t = rows_of(dlat0_ref[...], dlat)
    sc_t = rows_of(sc0_ref[...], scaled)
    dlg_all = jnp.concatenate([dlg0_ref[...] + dlg, jnp.zeros((1, span - rank), F32)], axis=1)
    spare = jnp.zeros((14, span), F32)
    for dx in (2, 1, 3, 0):
        for dz in range(NZ):
            lanes = pl.ds(pl.multiple_of((((x + dx) & 3) * NZ + ((z + dz) & 1)) * span, 128), span)
            n_all = jnp.concatenate([nrm0_ref[:, lanes], nrm_ref[:, lanes]], axis=0)
            g_all = jnp.concatenate([g0_ref[:, lanes], g_ref[:, lanes]], axis=0)
            for m, grad in ((0, nn(dlat_t, n_all).astype(BF)), (1, nn(sc_t, g_all).astype(BF))):
                keep[dx][dz, m * half : (m + 1) * half, :] = grad[:half]
                send[dx][dz, m * half : (m + 1) * half, :] = grad[half:]
            small = jnp.concatenate([dgain_ref[:, lanes], dlg_all, spare], axis=0).astype(BF)
            keep[dx][dz, rank : rank + 16, :] = small
            send[dx][dz, rank : rank + 16, :] = small


SMEM = functools.partial(pl.BlockSpec, memory_space=pltpu.SMEM)
VMEM = functools.partial(pl.BlockSpec, memory_space=pltpu.VMEM)


def forward(whole, x, gain, lgain, work=1):
    t, width = x.shape
    rank = lgain.shape[1]
    return pl.pallas_call(
        forward_kernel,
        out_shape=jax.ShapeDtypeStruct(x.shape, BF),
        in_specs=[VMEM()] * 5,
        out_specs=VMEM(),
        compiler_params=pltpu.CompilerParams(vmem_limit_bytes=6 << 20),
        cost_estimate=pl.CostEstimate(flops=4 * t * width * rank, transcendentals=0, bytes_accessed=4 * work * width * (t + rank)),
        name="forward",
    )(x, gain, lgain, *whole)


def backward_first(idx, pieces, x, g, gain, lgain):
    t, width = x.shape
    rank = lgain.shape[1]
    act = jax.ShapeDtypeStruct(x.shape, BF)
    lat = jax.ShapeDtypeStruct((t, rank), BF)
    mat = jax.ShapeDtypeStruct((width, rank), BF)
    return pl.pallas_call(
        backward_first_kernel,
        out_shape=(act, act, lat, lat, jax.ShapeDtypeStruct((1, width), F32), jax.ShapeDtypeStruct((1, rank), F32), mat, mat),
        in_specs=[SMEM()] + [VMEM()] * (len(pieces) + 4),
        out_specs=(VMEM(),) * 8,
        scratch_shapes=[pltpu.VMEM(x.shape, BF)],
        compiler_params=pltpu.CompilerParams(vmem_limit_bytes=8 << 20),
        cost_estimate=pl.CostEstimate(flops=6 * t * width * rank, transcendentals=0, bytes_accessed=4 * width * (2 * t + rank)),
        name="backward_first",
    )(idx, *pieces, x, g, gain, lgain)


def backward_last(idx, x, g, gain, lgain, first, g0):
    t, width = x.shape
    rank = lgain.shape[1]
    act = jax.ShapeDtypeStruct(x.shape, BF)
    span = width // (NX * NZ)
    block = jax.ShapeDtypeStruct((NZ, rank + 16, span), BF)
    _, nrm0, sc0, dlat0, dgain0, dlg0, wd, wu = first
    out = pl.pallas_call(
        backward_last_kernel,
        out_shape=(act,) + (block,) * (2 * NX),
        in_specs=[SMEM()] + [VMEM()] * 12,
        out_specs=(VMEM(),) * (1 + 2 * NX),
        scratch_shapes=[
            pltpu.VMEM(x.shape, BF),
            pltpu.VMEM(x.shape, BF),
            pltpu.VMEM((1, width), F32),
        ],
        compiler_params=pltpu.CompilerParams(vmem_limit_bytes=12 << 20),
        cost_estimate=pl.CostEstimate(flops=14 * t * width * rank, transcendentals=0, bytes_accessed=4 * width * (4 * t + 2 * rank)),
        name="backward_last",
    )(idx, x, g, gain, lgain, wd, wu, nrm0, g0, sc0, dlat0, dgain0, dlg0)
    return out[0], out[1 : 1 + NX], out[1 + NX :]


def pair_sums(keep, send, *others):
    half = (keep[0].shape[1] - 16) // 2
    recv = {dx: dp_move(send[dx], fc=1) for dx in (2, 1, 3, 0)}
    far = (keep[2].astype(F32) + recv[2].astype(F32)).astype(BF)
    far = after(far, *others)
    return dp_move(far[:, :half], fx=1), dp_move(far[:, half:], fx=-1), keep, recv


def ring_sums(parts):
    got_a, got_b, keep, recv = parts
    half = got_a.shape[1]
    rows = keep[0].shape[1]

    def both(dx):
        return keep[dx].astype(F32) + recv[dx].astype(F32)

    got_a = jnp.pad(got_a.astype(F32), ((0, 0), (0, rows - half), (0, 0)))
    got_b = jnp.pad(got_b.astype(F32), ((0, 0), (half, 0), (0, 0)))
    from_left = dp_move((both(1) + got_a).astype(BF), fx=1)
    from_right = dp_move((both(3) + got_b).astype(BF), fx=-1)
    return both(0) + from_left.astype(F32) + from_right.astype(F32)


def split_kernel(idx, own_ref, a_ref, b_ref, c_ref, mine_ref, yours_ref, row_ref, lrow_ref):
    total = own_ref[...] + a_ref[...].astype(F32) + b_ref[...].astype(F32) + c_ref[...].astype(F32)
    cols = yours_ref.shape[1]
    rows = yours_ref.shape[0]
    turned = pltpu.roll(total, cols, 1)
    first = idx[2] == 0
    mine = jnp.where(first, total, turned)
    mine_ref[...] = mine[:rows, : mine_ref.shape[1]]
    yours_ref[...] = jnp.where(first, turned, total)[:rows, :cols]
    row_ref[...] = mine[rows : rows + 1, :cols]
    lrow_ref[...] = total[rows + 1 : rows + 2, :rows]


def split_columns(idx, own, a, b, c, rank, cols):
    wide = -(-cols // 128) * 128
    return pl.pallas_call(
        split_kernel,
        out_shape=(
            jax.ShapeDtypeStruct((rank, wide), F32),
            jax.ShapeDtypeStruct((rank, cols), F32),
            jax.ShapeDtypeStruct((1, cols), F32),
            jax.ShapeDtypeStruct((1, rank), F32),
        ),
        in_specs=[SMEM()] + [VMEM()] * 4,
        out_specs=(VMEM(),) * 4,
        compiler_params=pltpu.CompilerParams(vmem_limit_bytes=16 << 20),
        name="split_columns",
    )(idx, own, a, b, c)


def join_kernel(idx, mine_ref, got_ref, down_ref, up_ref):
    rank, cols = got_ref.shape
    half = rank // 2
    first = idx[2] == 0
    wide = mine_ref.shape[1]
    got = jnp.concatenate([got_ref[...], jnp.zeros((rank, wide - cols), F32)], axis=1)
    mine = mine_ref[...]

    def whole(m):
        a, b = mine[m * half : (m + 1) * half], got[m * half : (m + 1) * half]
        return jnp.concatenate([jnp.where(first, a, b), jnp.where(first, b, a)], axis=0)

    down_ref[...] = whole(0).T[:cols]
    up_ref[...] = whole(1)[:, :cols]


def join_halves(idx, mine, got):
    rank, cols = got.shape
    return pl.pallas_call(
        join_kernel,
        out_shape=(jax.ShapeDtypeStruct((cols, rank), F32), jax.ShapeDtypeStruct((rank, cols), F32)),
        in_specs=[SMEM()] + [VMEM()] * 2,
        out_specs=(VMEM(),) * 2,
        compiler_params=pltpu.CompilerParams(vmem_limit_bytes=16 << 20),
        name="join_halves",
    )(idx, mine, got)


def body(enter_a, enter_b, cotan_a, cotan_b, saved_a, saved_b, norm_gain, w_down, latent_gain, w_up):
    place = lax.axis_index("dp")
    idx = (place.astype(jnp.int32) >> jnp.array([2, 1, 0], jnp.int32)) & jnp.array([3, 1, 1], jnp.int32)
    width = norm_gain.shape[1]
    rank = latent_gain.shape[1]
    cols = w_up.shape[2]

    shard = after(jnp.stack([w_down[0], w_up[0].T]), idx)
    across = dp_move(shard, fz=1)
    near_own = ring(shard)
    near_across = ring(after(across, near_own[1], near_own[2]))
    shard_m = after(shard, *near_across[1:])
    mirrored = mirror(shard_m)
    mirrored_z = mirror(shard_m, fz=1)
    near_own = far_halves(near_own)
    near_across = far_halves(near_across)
    pieces_a = near_own + near_across
    pieces_a = pieces_a + other_core(near_own) + other_core(near_across)
    gains = jnp.concatenate([norm_gain[0], latent_gain[0]]).reshape(-1, 128)
    gains_m = mirror(after(gains, *near_across[1:])).reshape(1, -1)
    gain_a, lgain_a = norm_gain, latent_gain
    gain_b, lgain_b = gains_m[:, :width], gains_m[:, width:]
    both_m = jnp.stack([mirrored, mirrored_z])
    near_m = ring(after(both_m, *near_own[3:], *near_across[3:]))

    first_a = backward_first(idx, pieces_a, saved_a[0, 0], cotan_a[0], gain_a, lgain_a)
    ga = relay(first_a[0], -1)
    near_m = far_halves(lax.optimization_barrier((*near_m, first_a[2]))[:3])
    pieces_b = near_m + other_core(near_m)
    first_b = backward_first(idx, pieces_b, saved_b[0, 0], cotan_b[0], gain_b, lgain_b)
    gb = relay(first_b[0], 1)
    ya = forward(first_a[6:], enter_a[0], gain_a, lgain_a)
    yb = forward(first_b[6:], enter_b[0], gain_b, lgain_b)
    xa = relay(ya, 1, fc=1)
    xb = relay(yb, -1, fc=1)

    back_a, keep_a, send_a = backward_last(idx, saved_a[1, 0], after(ga, ya, yb), gain_a, lgain_a, first_a, cotan_a[0])
    half_a = pair_sums(keep_a, send_a)
    gb = after(gb, ya, yb, half_a[0], half_a[1])
    back_b, keep_b, send_b = backward_last(idx, saved_b[1, 0], gb, gain_b, lgain_b, first_b, cotan_b[0])
    sums_a = ring_sums(half_a)
    sums_b = ring_sums(pair_sums(keep_b, send_b, sums_a))
    xa = dp_move(after(xa, sums_b), fc=1)
    xb = dp_move(after(xb, sums_b), fc=1)
    got_z = dp_move(sums_a[1].astype(BF), fz=1)
    got_m = mirror(sums_b[0].astype(BF))
    got_mz = mirror(sums_b[1].astype(BF), fz=1)
    mine, yours, row, lrow = split_columns(idx, sums_a[0], got_z, got_m, got_mz, rank, cols)
    out_a = forward(first_a[6:], xa, gain_a, lgain_a, LATE)
    out_b = forward(first_b[6:], xb, gain_b, lgain_b, LATE)
    yours, out_a, out_b = lax.optimization_barrier((yours, out_a, out_b))
    grad_down, grad_up = join_halves(idx, mine, dp_move(yours, fc=1))
    grad_lgain = lax.dynamic_slice(lrow, (jnp.uint32(0), place.astype(jnp.uint32) * (rank // NDP)), (1, rank // NDP))
    return (
        out_a[None],
        out_b[None],
        back_a[None],
        back_b[None],
        row,
        grad_down[None],
        grad_lgain,
        grad_up[None],
    )


def solution(mesh):
    act = P("section", "dp", None)
    placed = (
        act,
        act,
        act,
        act,
        P(None, "section", "dp", None),
        P(None, "section", "dp", None),
        P("section", None),
        P("section", "dp", None),
        P("section", None),
        P("section", None, "dp"),
    )
    return jax.shard_map(
        body,
        mesh=mesh,
        in_specs=placed,
        out_specs=(act, act, act, act, P("section", "dp"), act, P("section", "dp"), P("section", None, "dp")),
        check_vma=False,
    )
```

time: 499 us -> 348 us (0.70)
  Pallas kernels: 175 us -> 65.4 us
  local copies, waits for them, and re-layouts: 38.4 us -> 4.25 us
  starting transfers between devices: 53.4 us -> 67.7 us
  other arithmetic: 16.6 us -> 4.64 us
  waiting for transfers between devices: 212 us -> 201 us
    pallas_call x4, Pallas kernels: 70.5 us -> 20.8 us  [forward(): pl.pallas_call(forward_kernel, out_shape=jax.ShapeDtypeStruct(x.shape, BF...]
    ppermute x33 -> x48, waiting for transfers between devices: 141 us -> 106 us  [dp_move(): return lax.ppermute(value, 'dp', pairs)]
    pallas_call x2 -> x4, Pallas kernels: 59.7 us -> 26.8 us  [the longest x2 23.8 us: backward_last(): pl.pallas_call(backward_last_kernel, out_shape=(act,) + (block,) * (2 * N...]
    pallas_call x2, Pallas kernels: 44.8 us -> 17.8 us  [backward_first(): pl.pallas_call(backward_first_kernel, out_shape=(act, act, lat, lat, jax....]
    ppermute x7 -> x9, waiting for transfers between devices: 70.9 us -> 95 us  [the longest x4 83.2 us: relay(): return lax.ppermute(value, ('section', 'dp'), pairs)]
    unnamed x107 -> x18, local copies, waits for them, and re-layouts: 19.7 us -> 2.34 us
    ppermute x33 -> x48, starting transfers between devices: 33.7 us -> 43.8 us  [dp_move(): return lax.ppermute(value, 'dp', pairs)]
    slice x8 -> x4, local copies, waits for them, and re-layouts: 6.05 us -> 0.16 us  [the longest x2 0.09 us: pair_sums(): far[:, half:]]
  transfers between devices with their start and end apart: 40 -> 57, of which waited for: 16 -> 23; matrix products, arithmetic and copies ran while one was open for 7% -> 1% of each run, Pallas kernels for 35% -> 13%
where the time goes in v2:
time: 348 us; the launch traced here: 344 us
  waiting for transfers between devices  201 us (58%)
  starting transfers between devices  67.7 us (19%)
  Pallas kernels  65.4 us (19%)
  other arithmetic  4.64 us (1%)
  local copies, waits for them, and re-layouts  4.25 us (1%)
    ppermute x48, waiting for transfers between devices, dp_move(): return lax.ppermute(value, 'dp', pairs)  106 us
    ppermute x4, waiting for transfers between devices, relay(): return lax.ppermute(value, ('section', 'dp'), pairs)  83.2 us
    ppermute x48, starting transfers between devices, dp_move(): return lax.ppermute(value, 'dp', pairs)  43.8 us
    pallas_call x2, Pallas kernels, backward_last(): pl.pallas_call(backward_last_kernel, out_shape=(act,) + (block,) * (2 * N...  23.8 us
    pallas_call x4, Pallas kernels, forward(): pl.pallas_call(forward_kernel, out_shape=jax.ShapeDtypeStruct(x.shape, BF...  20.8 us
    pallas_call x2, Pallas kernels, backward_first(): pl.pallas_call(backward_first_kernel, out_shape=(act, act, lat, lat, jax....  17.8 us
    ppermute x5, starting transfers between devices, mirror(): return lax.ppermute(value, ('section', 'dp'), pairs)  14.9 us
    ppermute x5, waiting for transfers between devices, mirror(): return lax.ppermute(value, ('section', 'dp'), pairs)  11.8 us
  transfers between devices with their start and end apart: 57, of which 23 were waited for; matrix products, arithmetic and copies ran while one was open for 1% of the time, Pallas kernels for 13%

profile of v2, /device:TPU:0, one launch (start us, length us, event | category | flops | bytes accessed | tf_op | source)
XLA Modules:
  0.0 344.5 jit_solution(7013134595579006382)
XLA Ops:
  2.6 1.6 collective-permute-start
  4.2 1.7 collective-permute-start.1
  5.8 4.0 %collective-permute-start.4 = (bf16[2,448,256]{2,1,0:T(8,128)(2,1)S(1)}, bf16[2,448,256]{2,1,0:T(8,128)(2,1)S(1)}, u32[]{:S(2)}, u32[]{:S(2)}) collective-permute-start(bf16[2,448,256]{2,1,0:T(8,128)(2,1)S(1)} %pad_maximum_fusion.1.refs_0_), channel_id=1, source_target_pairs={{0,2},{1,3},{2,0},{3,1},{4,6},{5,7},{6,4},{7,5},{8,10},{9,11},{10,... | collective-permute-start | bytes 1376264 | tf_op jit(solution)/shard_map/ppermute | solution.py:24
  9.8 6.2 %collective-permute-done.refs_1_ = bf16[2,448,256]{2,1,0:T(8,128)(2,1)S(1)} collective-permute-done((bf16[2,448,256]{2,1,0:T(8,128)(2,1)S(1)}, bf16[2,448,256]{2,1,0:T(8,128)(2,1)S(1)}, u32[]{:S(2)}, u32[]{:S(2)}) %collective-permute-start) | collective-permute-done | bytes 458784 | tf_op jit(solution)/shard_map/ppermute | solution.py:24
  16.1 3.6 %collective-permute-done.4.refs_5_ = bf16[2,448,256]{2,1,0:T(8,128)(2,1)S(1)} collective-permute-done((bf16[2,448,256]{2,1,0:T(8,128)(2,1)S(1)}, bf16[2,448,256]{2,1,0:T(8,128)(2,1)S(1)}, u32[]{:S(2)}, u32[]{:S(2)}) %collective-permute-start.4) | collective-permute-done | bytes 458784 | tf_op jit(solution)/shard_map/ppermute | solution.py:24
  20.0 3.0 collective-permute-start.6
  23.1 3.3 collective-permute-start.3
  26.4 8.0 %collective-permute-done.5.refs_6_ = bf16[2,448,256]{2,1,0:T(8,128)(2,1)S(1)} collective-permute-done((bf16[2,448,256]{2,1,0:T(8,128)(2,1)S(1)}, bf16[2,448,256]{2,1,0:T(8,128)(2,1)S(1)}, u32[]{:S(2)}, u32[]{:S(2)}) %collective-permute-start.5) | collective-permute-done | bytes 458784 | tf_op jit(solution)/shard_map/ppermute | solution.py:24
  34.4 5.6 %collective-permute-start.22 = (bf16[2,448,256]{2,1,0:T(8,128)(2,1)S(1)}, bf16[2,448,256]{2,1,0:T(8,128)(2,1)S(1)}, u32[]{:S(2)}, u32[]{:S(2)}) collective-permute-start(bf16[2,448,256]{2,1,0:T(8,128)(2,1)S(1)} %pad_maximum_fusion.1.refs_0_), channel_id=1, source_target_pairs={{0,114},{1,115},{2,112},{3,113},{4,118},{5,119},{6,116},{7,117},{8... | collective-permute-start | bytes 1376264 | tf_op jit(solution)/shard_map/ppermute | solution.py:32
  40.5 3.0 collective-permute-start.8
  43.6 5.6 %collective-permute-done.7.refs_8_ = bf16[448,256]{1,0:T(8,128)(2,1)S(1)} collective-permute-done((bf16[448,256]{1,0:T(8,128)(2,1)S(1)}, bf16[448,256]{1,0:T(8,128)(2,1)S(1)}, u32[]{:S(2)}, u32[]{:S(2)}) %collective-permute-start.7) | collective-permute-done | bytes 229408 | tf_op jit(solution)/shard_map/ppermute | solution.py:24
  49.7 1.7 collective-permute-done.22
  51.4 8.9 %collective-permute-done.21 = bf16[2,448,256]{2,1,0:T(8,128)(2,1)S(1)} collective-permute-done((bf16[2,448,256]{2,1,0:T(8,128)(2,1)S(1)}, bf16[2,448,256]{2,1,0:T(8,128)(2,1)S(1)}, u32[]{:S(2)}, u32[]{:S(2)}) %collective-permute-start.21) | collective-permute-done | bytes 458784 | tf_op jit(solution)/shard_map/ppermute | solution.py:32
  62.0 3.2 collective-permute-start.24
  65.5 9.0 %backward_first.2 = (bf16[128,7168]{1,0:T(8,128)(2,1)S(1)}, bf16[128,7168]{1,0:T(8,128)(2,1)S(1)}, bf16[128,256]{1,0:T(8,128)(2,1)S(1)}, bf16[128,256]{1,0:T(8,1...) custom-call(s32[3]{0:T(128)S(1)} %shift-right-arithmetic_and_fusion., ...), custom_call_target="tpu_custom_call" | custom-call | flops 1409286144 | bytes 14680064 | tf_op jit(solution)/shard_map/backward_first/pallas_call | solution.py:252
  74.5 11.3 %collective-permute-done.23 = bf16[2,2,448,256]{3,2,0,1:T(8,128)(2,1)S(1)} collective-permute-done((bf16[2,2,448,256]{3,2,0,1:T(8,128)(2,1)S(1)}, bf16[2,2,448,256]{3,2,0,1:T(8,128)(2,1)S(1)}, u32[]{:S(2)}, u32[]{:S(2)}) %collective-permute-start.23) | collective-permute-done | bytes 917536 | tf_op jit(solution)/shard_map/ppermute | solution.py:24
  86.0 3.3 collective-permute-start.26
  89.2 4.6 %collective-permute-start.20 = (f32[58,128]{1,0:T(8,128)S(1)}, f32[58,128]{1,0:T(8,128)S(1)}, u32[]{:S(2)}, u32[]{:S(2)}) collective-permute-start(f32[58,128]{1,0:T(8,128)S(1)} %maximum_bitcast_fusion), channel_id=1, source_target_pairs={{0,112},{1,113},{2,114},{3,115},{4,116},{5,117},{6,118},{7,119},{8... | collective-permute-start | bytes 89096 | tf_op jit(solution)/shard_map/ppermute | solution.py:32
  93.8 1.4 collective-permute-start.19
  95.7 4.3 %collective-permute-done.25.refs_3_ = bf16[2,448,256]{2,1,0:T(8,128)(2,1)S(1)} collective-permute-done((bf16[2,448,256]{2,1,0:T(8,128)(2,1)S(1)}, bf16[2,448,256]{2,1,0:T(8,128)(2,1)S(1)}, u32[]{:S(2)}, u32[]{:S(2)}) %collective-permute-start.25) | collective-permute-done | bytes 458784 | tf_op jit(solution)/shard_map/ppermute | solution.py:24
  101.0 4.6 %forward.4 = bf16[128,7168]{1,0:T(8,128)(2,1)S(1)} custom-call(bf16[128,7168]{1,0:T(8,128)(2,1)S(1)} %bitcast.60, f32[1,7168]{1,0:T(1,128)S(1)} %copy-done.4, f32[1,256]{1,0:T(1,128)S(1)} %copy-done.5, bf16[7168,256]{1,0:T(8,128)(2,1)S(1)} %get-tuple-element.67.wd, bf16[7168,256]{1,0:T(8,128)(2,1)S(1)} %get-tuple-element.68.wu), custom_call_target="tpu_custom_call" | custom-call | flops 939524096 | bytes 11010048 | tf_op jit(solution)/shard_map/forward/pallas_call | solution.py:235
  106.0 1.3 copy-done.1
  107.3 8.9 %backward_first.3 = (bf16[128,7168]{1,0:T(8,128)(2,1)S(1)}, bf16[128,7168]{1,0:T(8,128)(2,1)S(1)}, bf16[128,256]{1,0:T(8,128)(2,1)S(1)}, bf16[128,256]{1,0:T(8,1...) custom-call(s32[3]{0:T(128)S(1)} %shift-right-arithmetic_and_fusion., ...), custom_call_target="tpu_custom_call" | custom-call | flops 1409286144 | bytes 14680064 | tf_op jit(solution)/shard_map/backward_first/pallas_call | solution.py:252
  116.2 4.6 %forward.5 = bf16[128,7168]{1,0:T(8,128)(2,1)S(1)} custom-call(bf16[128,7168]{1,0:T(8,128)(2,1)S(1)} %bitcast.61, f32[1,7168]{1,0:T(1,128)S(1)} %slice.87.refs_12_.gain_ref, f32[1,256]{1,0:T(1,128)S(1)} %slice.88.refs_13_.lgain_ref, bf16[7168,256]{1,0:T(8,128)(2,1)S(1)} %get-tuple-element.76.wd, bf16[7168,256]{1,0:T(8,128)(2,1)S(1)} %get-tuple-element.77.wu), custom_call_target="tpu_custom_call" | custom-call | flops 939524096 | bytes 11010048 | tf_op jit(solution)/shard_map/forward/pallas_call | solution.py:235
  120.8 16.6 %collective-permute-done.19.g_ref = bf16[128,7168]{1,0:T(8,128)(2,1)S(1)} collective-permute-done((bf16[128,7168]{1,0:T(8,128)(2,1)S(1)}, bf16[128,7168]{1,0:T(8,128)(2,1)S(1)}, u32[]{:S(2)}, u32[]{:S(2)}) %collective-permute-start.19) | collective-permute-done | bytes 1835040 | tf_op jit(solution)/shard_map/ppermute | solution.py:43
  137.5 11.9 %backward_last.2 = (bf16[128,7168]{1,0:T(8,128)(2,1)}, bf16[2,272,896]{2,1,0:T(8,128)(2,1)S(1)}, bf16[2,272,896]{2,1,0:T(8,128)(2,1)S(1)}, bf16[2,272,896]{2,1,0...) custom-call(s32[3]{0:T(128)S(1)} %shift-right-arithmetic_and_fusion., ...), custom_call_target="tpu_custom_call" | custom-call | flops 3288334336 | bytes 29360128 | tf_op jit(solution)/shard_map/backward_last/pallas_call | solution.py:271
  149.3 2.7 collective-permute-start.41
  153.1 3.3 collective-permute-start.38
  156.4 10.5 %collective-permute-done.35 = bf16[2,128,896]{2,1,0:T(8,128)(2,1)S(1)} collective-permute-done((bf16[2,128,896]{2,1,0:T(8,128)(2,1)S(1)}, bf16[2,128,896]{2,1,0:T(8,128)(2,1)S(1)}, u32[]{:S(2)}, u32[]{:S(2)}) %collective-permute-start.35) | collective-permute-done | bytes 458784 | tf_op jit(solution)/shard_map/ppermute | solution.py:24
  167.8 4.0 %collective-permute-start.39 = (bf16[2,272,896]{2,1,0:T(8,128)(2,1)S(1)}, bf16[2,272,896]{2,1,0:T(8,128)(2,1)S(1)}, u32[]{:S(2)}, u32[]{:S(2)}) collective-permute-start(bf16[2,272,896]{2,1,0:T(8,128)(2,1)S(1)} %add_convert_fusion.3), channel_id=1, source_target_pairs={{0,12},{1,13},{2,14},{3,15},{4,0},{5,1},{6,2},{7,3},{8,4},{9,5},{1... | collective-permute-start | bytes 2924552 | tf_op jit(solution)/shard_map/ppermute | solution.py:24
  171.8 20.1 %collective-permute-done.41.g_ref = bf16[128,7168]{1,0:T(8,128)(2,1)S(1)} collective-permute-done((bf16[128,7168]{1,0:T(8,128)(2,1)S(1)}, bf16[128,7168]{1,0:T(8,128)(2,1)S(1)}, u32[]{:S(2)}, u32[]{:S(2)}) %collective-permute-start.41) | collective-permute-done | bytes 1835040 | tf_op jit(solution)/shard_map/ppermute | solution.py:43
  191.9 11.9 %backward_last.3 = (bf16[128,7168]{1,0:T(8,128)(2,1)}, bf16[2,272,896]{2,1,0:T(8,128)(2,1)S(1)}, bf16[2,272,896]{2,1,0:T(8,128)(2,1)S(1)}, bf16[2,272,896]{2,1,0...) custom-call(s32[3]{0:T(128)S(1)} %shift-right-arithmetic_and_fusion., ...), custom_call_target="tpu_custom_call" | custom-call | flops 3288334336 | bytes 29360128 | tf_op jit(solution)/shard_map/backward_last/pallas_call | solution.py:271
  204.7 1.6 collective-permute-done.44
  206.7 3.3 collective-permute-start.48
  210.0 3.7 %collective-permute-start.52 = (bf16[128,7168]{1,0:T(8,128)(2,1)S(1)}, bf16[128,7168]{1,0:T(8,128)(2,1)S(1)}, u32[]{:S(2)}, u32[]{:S(2)}) collective-permute-start(bf16[128,7168]{1,0:T(8,128)(2,1)S(1)} %forward.4), channel_id=1, source_target_pairs={{0,17},{1,16},{2,19},{3,18},{4,21},{5,20},{6,23},{7,22},{8,25},{9,... | collective-permute-start | bytes 5505032 | tf_op jit(solution)/shard_map/ppermute | solution.py:43
  213.7 1.3 collective-permute-start.54
  215.0 5.4 %collective-permute-done.45 = bf16[2,128,896]{2,1,0:T(8,128)(2,1)S(1)} collective-permute-done((bf16[2,128,896]{2,1,0:T(8,128)(2,1)S(1)}, bf16[2,128,896]{2,1,0:T(8,128)(2,1)S(1)}, u32[]{:S(2)}, u32[]{:S(2)}) %collective-permute-start.45) | collective-permute-done | bytes 458784 | tf_op jit(solution)/shard_map/ppermute | solution.py:24
  221.3 3.8 %collective-permute-start.49 = (bf16[2,272,896]{2,1,0:T(8,128)(2,1)S(1)}, bf16[2,272,896]{2,1,0:T(8,128)(2,1)S(1)}, u32[]{:S(2)}, u32[]{:S(2)}) collective-permute-start(bf16[2,272,896]{2,1,0:T(8,128)(2,1)S(1)} %add_convert_fusion), channel_id=1, source_target_pairs={{0,12},{1,13},{2,14},{3,15},{4,0},{5,1},{6,2},{7,3},{8,4},{9,5},{1... | collective-permute-start | bytes 2924552 | tf_op jit(solution)/shard_map/ppermute | solution.py:24
  225.1 20.9 %collective-permute-done.46 = bf16[2,272,896]{2,1,0:T(8,128)(2,1)S(1)} collective-permute-done((bf16[2,272,896]{2,1,0:T(8,128)(2,1)S(1)}, bf16[2,272,896]{2,1,0:T(8,128)(2,1)S(1)}, u32[]{:S(2)}, u32[]{:S(2)}) %collective-permute-start.46) | collective-permute-done | bytes 974880 | tf_op jit(solution)/shard_map/ppermute | solution.py:24
  246.5 46.5 %collective-permute-done.52 = bf16[128,7168]{1,0:T(8,128)(2,1)S(1)} collective-permute-done((bf16[128,7168]{1,0:T(8,128)(2,1)S(1)}, bf16[128,7168]{1,0:T(8,128)(2,1)S(1)}, u32[]{:S(2)}, u32[]{:S(2)}) %collective-permute-start.52) | collective-permute-done | bytes 1835040 | tf_op jit(solution)/shard_map/ppermute | solution.py:43
  293.6 1.8 collective-permute-start.40
  296.8 3.3 collective-permute-start.51
  300.1 26.2 %collective-permute-done.40.a_ref = bf16[272,896]{1,0:T(8,128)(2,1)S(1)} collective-permute-done((bf16[272,896]{1,0:T(8,128)(2,1)S(1)}, bf16[272,896]{1,0:T(8,128)(2,1)S(1)}, u32[]{:S(2)}, u32[]{:S(2)}) %collective-permute-start.40) | collective-permute-done | bytes 487456 | tf_op jit(solution)/shard_map/ppermute | solution.py:24
  327.0 1.5 split_columns.1
  328.5 5.8 %forward.6 = bf16[128,7168]{1,0:T(8,128)(2,1)} custom-call(bf16[128,7168]{1,0:T(8,128)(2,1)S(1)} %collective-permute-done.53.x_ref, f32[1,7168]{1,0:T(1,128)S(1)} %copy-done.4, f32[1,256]{1,0:T(1,128)S(1)} %copy-done.5, bf16[7168,256]{1,0:T(8,128)(2,1)S(1)} %get-tuple-element.67.wd, bf16[7168,256]{1,0:T(8,128)(2,1)S(1)} %get-tuple-element.68.wu), custom_call_target="tpu_custom_call" | custom-call | flops 939524096 | bytes 11010048 | tf_op jit(solution)/shard_map/forward/pallas_call | solution.py:235
  334.3 5.8 %forward.7 = bf16[128,7168]{1,0:T(8,128)(2,1)} custom-call(bf16[128,7168]{1,0:T(8,128)(2,1)S(1)} %collective-permute-done.55.x_ref, f32[1,7168]{1,0:T(1,128)S(1)} %slice.87.refs_12_.gain_ref, f32[1,256]{1,0:T(1,128)S(1)} %slice.88.refs_13_.lgain_ref, bf16[7168,256]{1,0:T(8,128)(2,1)S(1)} %get-tuple-element.76.wd, bf16[7168,256]{1,0:T(8,128)(2,1)S(1)} %get-tuple-element.77.wu), custom_call_target="tpu_custom_call" | custom-call | flops 939524096 | bytes 11010048 | tf_op jit(solution)/shard_map/forward/pallas_call | solution.py:235
  340.7 1.3 collective-permute-done.56.got_ref
  342.0 1.5 join_halves.1
  (130 shorter events, 16.1 us)
Async XLA Ops:
  2.6 13.4 %collective-permute-start = (bf16[2,448,256]{2,1,0:T(8,128)(2,1)S(1)}, bf16[2,448,256]{2,1,0:T(8,128)(2,1)S(1)}, u32[]{:S(2)}, u32[]{:S(2)}) collective-permute-start(bf16[2,448,256]{2,1,0:T(8,128)(2,1)S(1)} %pad_maximum_fusion.1.refs_0_), channel_id=1, source_target_pairs={{0,4},{1,5},{2,6},{3,7},{4,8},{5,9},{6,10},{7,11},{8,12},{9,13},{1... | collective-permute-start | bytes 1376264 | tf_op jit(solution)/shard_map/ppermute | solution.py:24
  4.2 12.0 %collective-permute-start.1 = (bf16[2,448,256]{2,1,0:T(8,128)(2,1)S(1)}, bf16[2,448,256]{2,1,0:T(8,128)(2,1)S(1)}, u32[]{:S(2)}, u32[]{:S(2)}) collective-permute-start(bf16[2,448,256]{2,1,0:T(8,128)(2,1)S(1)} %pad_maximum_fusion.1.refs_0_), channel_id=1, source_target_pairs={{0,12},{1,13},{2,14},{3,15},{4,0},{5,1},{6,2},{7,3},{8,4},{9,5},{1... | collective-permute-start | bytes 1376264 | tf_op jit(solution)/shard_map/ppermute | solution.py:24
  5.8 13.9 %collective-permute-start.4 = (bf16[2,448,256]{2,1,0:T(8,128)(2,1)S(1)}, bf16[2,448,256]{2,1,0:T(8,128)(2,1)S(1)}, u32[]{:S(2)}, u32[]{:S(2)}) collective-permute-start(bf16[2,448,256]{2,1,0:T(8,128)(2,1)S(1)} %pad_maximum_fusion.1.refs_0_), channel_id=1, source_target_pairs={{0,2},{1,3},{2,0},{3,1},{4,6},{5,7},{6,4},{7,5},{8,10},{9,11},{10,... | collective-permute-start | bytes 1376264 | tf_op jit(solution)/shard_map/ppermute | solution.py:24
  9.8 30.3 %collective-permute-start.9 = (bf16[2,448,256]{2,1,0:T(8,128)(2,1)S(1)}, bf16[2,448,256]{2,1,0:T(8,128)(2,1)S(1)}, u32[]{:S(2)}, u32[]{:S(2)}) collective-permute-start(bf16[2,448,256]{2,1,0:T(8,128)(2,1)S(1)} %pad_maximum_fusion.1.refs_0_), channel_id=1, source_target_pairs={{0,1},{1,0},{2,3},{3,2},{4,5},{5,4},{6,7},{7,6},{8,9},{9,8},{10,11... | collective-permute-start | bytes 1376264 | tf_op jit(solution)/shard_map/ppermute | solution.py:24
  19.7 14.7 %collective-permute-start.5 = (bf16[2,448,256]{2,1,0:T(8,128)(2,1)S(1)}, bf16[2,448,256]{2,1,0:T(8,128)(2,1)S(1)}, u32[]{:S(2)}, u32[]{:S(2)}) collective-permute-start(bf16[2,448,256]{2,1,0:T(8,128)(2,1)S(1)} %collective-permute-done.4.refs_5_), channel_id=1, source_target_pairs={{0,4},{1,5},{2,6},{3,7},{4,8},{5,9},{6,10},{7,11},{8,12},{9,13},{1... | collective-permute-start | bytes 1376264 | tf_op jit(solution)/shard_map/ppermute | solution.py:24
  20.0 14.4 %collective-permute-start.6 = (bf16[2,448,256]{2,1,0:T(8,128)(2,1)S(1)}, bf16[2,448,256]{2,1,0:T(8,128)(2,1)S(1)}, u32[]{:S(2)}, u32[]{:S(2)}) collective-permute-start(bf16[2,448,256]{2,1,0:T(8,128)(2,1)S(1)} %collective-permute-done.4.refs_5_), channel_id=1, source_target_pairs={{0,12},{1,13},{2,14},{3,15},{4,0},{5,1},{6,2},{7,3},{8,4},{9,5},{1... | collective-permute-start | bytes 1376264 | tf_op jit(solution)/shard_map/ppermute | solution.py:24
  23.0 17.2 %collective-permute-start.2 = (bf16[448,256]{1,0:T(8,128)(2,1)S(1)}, bf16[448,256]{1,0:T(8,128)(2,1)S(1)}, u32[]{:S(2)}, u32[]{:S(2)}) collective-permute-start(bf16[448,256]{1,0:T(8,128)(2,1)S(1)} %slice_bitcast_fusion.12), channel_id=1, source_target_pairs={{0,4},{1,5},{2,6},{3,7},{4,8},{5,9},{6,10},{7,11},{8,12},{9,13},{1... | collective-permute-start | bytes 688136 | tf_op jit(solution)/shard_map/ppermute | solution.py:24
  23.1 17.4 %collective-permute-start.3 = (bf16[448,256]{1,0:T(8,128)(2,1)S(1)}, bf16[448,256]{1,0:T(8,128)(2,1)S(1)}, u32[]{:S(2)}, u32[]{:S(2)}) collective-permute-start(bf16[448,256]{1,0:T(8,128)(2,1)S(1)} %slice_bitcast_fusion.11), channel_id=1, source_target_pairs={{0,12},{1,13},{2,14},{3,15},{4,0},{5,1},{6,2},{7,3},{8,4},{9,5},{1... | collective-permute-start | bytes 688136 | tf_op jit(solution)/shard_map/ppermute | solution.py:24
  34.4 9.2 %collective-permute-start.10 = (bf16[2,448,256]{2,1,0:T(8,128)(2,1)S(1)}, bf16[2,448,256]{2,1,0:T(8,128)(2,1)S(1)}, u32[]{:S(2)}, u32[]{:S(2)}) collective-permute-start(bf16[2,448,256]{2,1,0:T(8,128)(2,1)S(1)} %collective-permute-done.refs_1_), channel_id=1, source_target_pairs={{0,1},{1,0},{2,3},{3,2},{4,5},{5,4},{6,7},{7,6},{8,9},{9,8},{10,11... | collective-permute-start | bytes 1376264 | tf_op jit(solution)/shard_map/ppermute | solution.py:24
  34.4 17.0 %collective-permute-start.22 = (bf16[2,448,256]{2,1,0:T(8,128)(2,1)S(1)}, bf16[2,448,256]{2,1,0:T(8,128)(2,1)S(1)}, u32[]{:S(2)}, u32[]{:S(2)}) collective-permute-start(bf16[2,448,256]{2,1,0:T(8,128)(2,1)S(1)} %pad_maximum_fusion.1.refs_0_), channel_id=1, source_target_pairs={{0,114},{1,115},{2,112},{3,113},{4,118},{5,119},{6,116},{7,117},{8... | collective-permute-start | bytes 1376264 | tf_op jit(solution)/shard_map/ppermute | solution.py:32
  40.1 20.3 %collective-permute-start.21 = (bf16[2,448,256]{2,1,0:T(8,128)(2,1)S(1)}, bf16[2,448,256]{2,1,0:T(8,128)(2,1)S(1)}, u32[]{:S(2)}, u32[]{:S(2)}) collective-permute-start(bf16[2,448,256]{2,1,0:T(8,128)(2,1)S(1)} %pad_maximum_fusion.1.refs_0_), channel_id=1, source_target_pairs={{0,112},{1,113},{2,114},{3,115},{4,116},{5,117},{6,118},{7,119},{8... | collective-permute-start | bytes 1376264 | tf_op jit(solution)/shard_map/ppermute | solution.py:32
  40.2 9.0 %collective-permute-start.7 = (bf16[448,256]{1,0:T(8,128)(2,1)S(1)}, bf16[448,256]{1,0:T(8,128)(2,1)S(1)}, u32[]{:S(2)}, u32[]{:S(2)}) collective-permute-start(bf16[448,256]{1,0:T(8,128)(2,1)S(1)} %slice_bitcast_fusion.10), channel_id=1, source_target_pairs={{0,4},{1,5},{2,6},{3,7},{4,8},{5,9},{6,10},{7,11},{8,12},{9,13},{1... | collective-permute-start | bytes 688136 | tf_op jit(solution)/shard_map/ppermute | solution.py:24
  40.5 8.6 %collective-permute-start.8 = (bf16[448,256]{1,0:T(8,128)(2,1)S(1)}, bf16[448,256]{1,0:T(8,128)(2,1)S(1)}, u32[]{:S(2)}, u32[]{:S(2)}) collective-permute-start(bf16[448,256]{1,0:T(8,128)(2,1)S(1)} %slice_bitcast_fusion.9), channel_id=1, source_target_pairs={{0,12},{1,13},{2,14},{3,15},{4,0},{5,1},{6,2},{7,3},{8,4},{9,5},{1... | collective-permute-start | bytes 688136 | tf_op jit(solution)/shard_map/ppermute | solution.py:24
  43.6 16.9 %collective-permute-start.11 = (bf16[2,448,256]{2,1,0:T(8,128)(2,1)S(1)}, bf16[2,448,256]{2,1,0:T(8,128)(2,1)S(1)}, u32[]{:S(2)}, u32[]{:S(2)}) collective-permute-start(bf16[2,448,256]{2,1,0:T(8,128)(2,1)S(1)} %collective-permute-done.1.refs_2_), channel_id=1, source_target_pairs={{0,1},{1,0},{2,3},{3,2},{4,5},{5,4},{6,7},{7,6},{8,9},{9,8},{10,11... | collective-permute-start | bytes 1376264 | tf_op jit(solution)/shard_map/ppermute | solution.py:24
  49.2 12.8 %collective-permute-start.14 = (bf16[2,448,256]{2,1,0:T(8,128)(2,1)S(1)}, bf16[2,448,256]{2,1,0:T(8,128)(2,1)S(1)}, u32[]{:S(2)}, u32[]{:S(2)}) collective-permute-start(bf16[2,448,256]{2,1,0:T(8,128)(2,1)S(1)} %collective-permute-done.4.refs_5_), channel_id=1, source_target_pairs={{0,1},{1,0},{2,3},{3,2},{4,5},{5,4},{6,7},{7,6},{8,9},{9,8},{10,11... | collective-permute-start | bytes 1376264 | tf_op jit(solution)/shard_map/ppermute | solution.py:24
  49.2 12.8 %collective-permute-start.15 = (bf16[2,448,256]{2,1,0:T(8,128)(2,1)S(1)}, bf16[2,448,256]{2,1,0:T(8,128)(2,1)S(1)}, u32[]{:S(2)}, u32[]{:S(2)}) collective-permute-start(bf16[2,448,256]{2,1,0:T(8,128)(2,1)S(1)} %collective-permute-done.5.refs_6_), channel_id=1, source_target_pairs={{0,1},{1,0},{2,3},{3,2},{4,5},{5,4},{6,7},{7,6},{8,9},{9,8},{10,11... | collective-permute-start | bytes 1376264 | tf_op jit(solution)/shard_map/ppermute | solution.py:24
  51.4 9.6 %collective-permute-start.12 = (bf16[448,256]{1,0:T(8,128)(2,1)S(1)}, bf16[448,256]{1,0:T(8,128)(2,1)S(1)}, u32[]{:S(2)}, u32[]{:S(2)}) collective-permute-start(bf16[448,256]{1,0:T(8,128)(2,1)S(1)} %collective-permute-done.2.refs_3_), channel_id=1, source_target_pairs={{0,1},{1,0},{2,3},{3,2},{4,5},{5,4},{6,7},{7,6},{8,9},{9,8},{10,11... | collective-permute-start | bytes 688136 | tf_op jit(solution)/shard_map/ppermute | solution.py:24
  61.9 23.8 %collective-permute-start.23 = (bf16[2,2,448,256]{3,2,0,1:T(8,128)(2,1)S(1)}, bf16[2,2,448,256]{3,2,0,1:T(8,128)(2,1)S(1)}, u32[]{:S(2)}, u32[]{:S(2)}) collective-permute-start(bf16[2,2,448,256]{3,2,0,1:T(8,128)(2,1)S(1)} %pad_maximum_fusion), channel_id=1, source_target_pairs={{0,4},{1,5},{2,6},{3,7},{4,8},{5,9},{6,10},{7,11},{8,12},{9,13},{1... | collective-permute-start | bytes 2752520 | tf_op jit(solution)/shard_map/ppermute | solution.py:24
  62.0 23.8 %collective-permute-start.24 = (bf16[2,2,448,256]{3,2,0,1:T(8,128)(2,1)S(1)}, bf16[2,2,448,256]{3,2,0,1:T(8,128)(2,1)S(1)}, u32[]{:S(2)}, u32[]{:S(2)}) collective-permute-start(bf16[2,2,448,256]{3,2,0,1:T(8,128)(2,1)S(1)} %pad_maximum_fusion), channel_id=1, source_target_pairs={{0,12},{1,13},{2,14},{3,15},{4,0},{5,1},{6,2},{7,3},{8,4},{9,5},{1... | collective-permute-start | bytes 2752520 | tf_op jit(solution)/shard_map/ppermute | solution.py:24
  85.8 14.8 %collective-permute-start.27 = (bf16[2,2,448,256]{3,2,0,1:T(8,128)(2,1)S(1)}, bf16[2,2,448,256]{3,2,0,1:T(8,128)(2,1)S(1)}, u32[]{:S(2)}, u32[]{:S(2)}) collective-permute-start(bf16[2,2,448,256]{3,2,0,1:T(8,128)(2,1)S(1)} %pad_maximum_fusion), channel_id=1, source_target_pairs={{0,1},{1,0},{2,3},{3,2},{4,5},{5,4},{6,7},{7,6},{8,9},{9,8},{10,11... | collective-permute-start | bytes 2752520 | tf_op jit(solution)/shard_map/ppermute | solution.py:24
  85.8 14.2 %collective-permute-start.25 = (bf16[2,448,256]{2,1,0:T(8,128)(2,1)S(1)}, bf16[2,448,256]{2,1,0:T(8,128)(2,1)S(1)}, u32[]{:S(2)}, u32[]{:S(2)}) collective-permute-start(bf16[2,448,256]{2,1,0:T(8,128)(2,1)S(1)} %slice_bitcast_fusion.8), channel_id=1, source_target_pairs={{0,4},{1,5},{2,6},{3,7},{4,8},{5,9},{6,10},{7,11},{8,12},{9,13},{1... | collective-permute-start | bytes 1376264 | tf_op jit(solution)/shard_map/ppermute | solution.py:24
  86.0 14.1 %collective-permute-start.26 = (bf16[2,448,256]{2,1,0:T(8,128)(2,1)S(1)}, bf16[2,448,256]{2,1,0:T(8,128)(2,1)S(1)}, u32[]{:S(2)}, u32[]{:S(2)}) collective-permute-start(bf16[2,448,256]{2,1,0:T(8,128)(2,1)S(1)} %slice_bitcast_fusion.7), channel_id=1, source_target_pairs={{0,12},{1,13},{2,14},{3,15},{4,0},{5,1},{6,2},{7,3},{8,4},{9,5},{1... | collective-permute-start | bytes 1376264 | tf_op jit(solution)/shard_map/ppermute | solution.py:24
  89.2 6.5 %collective-permute-start.20 = (f32[58,128]{1,0:T(8,128)S(1)}, f32[58,128]{1,0:T(8,128)S(1)}, u32[]{:S(2)}, u32[]{:S(2)}) collective-permute-start(f32[58,128]{1,0:T(8,128)S(1)} %maximum_bitcast_fusion), channel_id=1, source_target_pairs={{0,112},{1,113},{2,114},{3,115},{4,116},{5,117},{6,118},{7,119},{8... | collective-permute-start | bytes 89096 | tf_op jit(solution)/shard_map/ppermute | solution.py:32
  93.8 43.6 %collective-permute-start.19 = (bf16[128,7168]{1,0:T(8,128)(2,1)S(1)}, bf16[128,7168]{1,0:T(8,128)(2,1)S(1)}, u32[]{:S(2)}, u32[]{:S(2)}) collective-permute-start(bf16[128,7168]{1,0:T(8,128)(2,1)S(1)} %get-tuple-element.66), channel_id=1, source_target_pairs={{16,0},{17,1},{18,2},{19,3},{20,4},{21,5},{22,6},{23,7},{24,8},{25... | collective-permute-start | bytes 5505032 | tf_op jit(solution)/shard_map/ppermute | solution.py:43
  95.7 10.1 %collective-permute-start.28 = (bf16[2,2,448,256]{3,2,0,1:T(8,128)(2,1)S(1)}, bf16[2,2,448,256]{3,2,0,1:T(8,128)(2,1)S(1)}, u32[]{:S(2)}, u32[]{:S(2)}) collective-permute-start(bf16[2,2,448,256]{3,2,0,1:T(8,128)(2,1)S(1)} %collective-permute-done.23), channel_id=1, source_target_pairs={{0,1},{1,0},{2,3},{3,2},{4,5},{5,4},{6,7},{7,6},{8,9},{9,8},{10,11... | collective-permute-start | bytes 2752520 | tf_op jit(solution)/shard_map/ppermute | solution.py:24
  100.0 5.8 %collective-permute-start.29 = (bf16[2,2,448,256]{3,2,0,1:T(8,128)(2,1)S(1)}, bf16[2,2,448,256]{3,2,0,1:T(8,128)(2,1)S(1)}, u32[]{:S(2)}, u32[]{:S(2)}) collective-permute-start(bf16[2,2,448,256]{3,2,0,1:T(8,128)(2,1)S(1)} %collective-permute-done.24), channel_id=1, source_target_pairs={{0,1},{1,0},{2,3},{3,2},{4,5},{5,4},{6,7},{7,6},{8,9},{9,8},{10,11... | collective-permute-start | bytes 2752520 | tf_op jit(solution)/shard_map/ppermute | solution.py:24
  100.1 5.9 %collective-permute-start.30 = (bf16[2,448,256]{2,1,0:T(8,128)(2,1)S(1)}, bf16[2,448,256]{2,1,0:T(8,128)(2,1)S(1)}, u32[]{:S(2)}, u32[]{:S(2)}) collective-permute-start(bf16[2,448,256]{2,1,0:T(8,128)(2,1)S(1)} %collective-permute-done.25.refs_3_), channel_id=1, source_target_pairs={{0,1},{1,0},{2,3},{3,2},{4,5},{5,4},{6,7},{7,6},{8,9},{9,8},{10,11... | collective-permute-start | bytes 1376264 | tf_op jit(solution)/shard_map/ppermute | solution.py:24
  100.6 5.4 %collective-permute-start.31 = (bf16[2,448,256]{2,1,0:T(8,128)(2,1)S(1)}, bf16[2,448,256]{2,1,0:T(8,128)(2,1)S(1)}, u32[]{:S(2)}, u32[]{:S(2)}) collective-permute-start(bf16[2,448,256]{2,1,0:T(8,128)(2,1)S(1)} %collective-permute-done.26.refs_4_), channel_id=1, source_target_pairs={{0,1},{1,0},{2,3},{3,2},{4,5},{5,4},{6,7},{7,6},{8,9},{9,8},{10,11... | collective-permute-start | bytes 1376264 | tf_op jit(solution)/shard_map/ppermute | solution.py:24
  149.3 42.5 %collective-permute-start.41 = (bf16[128,7168]{1,0:T(8,128)(2,1)S(1)}, bf16[128,7168]{1,0:T(8,128)(2,1)S(1)}, u32[]{:S(2)}, u32[]{:S(2)}) collective-permute-start(bf16[128,7168]{1,0:T(8,128)(2,1)S(1)} %get-tuple-element.91), channel_id=1, source_target_pairs={{0,16},{1,17},{2,18},{3,19},{4,20},{5,21},{6,22},{7,23},{8,24},{9,... | collective-permute-start | bytes 5505032 | tf_op jit(solution)/shard_map/ppermute | solution.py:43
  152.4 14.9 %collective-permute-start.37 = (bf16[2,272,896]{2,1,0:T(8,128)(2,1)S(1)}, bf16[2,272,896]{2,1,0:T(8,128)(2,1)S(1)}, u32[]{:S(2)}, u32[]{:S(2)}) collective-permute-start(bf16[2,272,896]{2,1,0:T(8,128)(2,1)S(1)} %get-tuple-element.90), channel_id=1, source_target_pairs={{0,1},{1,0},{2,3},{3,2},{4,5},{5,4},{6,7},{7,6},{8,9},{9,8},{10,11... | collective-permute-start | bytes 2924552 | tf_op jit(solution)/shard_map/ppermute | solution.py:24
  152.9 13.9 %collective-permute-start.35 = (bf16[2,128,896]{2,1,0:T(8,128)(2,1)S(1)}, bf16[2,128,896]{2,1,0:T(8,128)(2,1)S(1)}, u32[]{:S(2)}, u32[]{:S(2)}) collective-permute-start(bf16[2,128,896]{2,1,0:T(8,128)(2,1)S(1)} %slice.89), channel_id=1, source_target_pairs={{0,4},{1,5},{2,6},{3,7},{4,8},{5,9},{6,10},{7,11},{8,12},{9,13},{1... | collective-permute-start | bytes 1376264 | tf_op jit(solution)/shard_map/ppermute | solution.py:24
  153.1 14.4 %collective-permute-start.38 = (bf16[2,144,896]{2,1,0:T(8,128)(2,1)S(1)}, bf16[2,144,896]{2,1,0:T(8,128)(2,1)S(1)}, u32[]{:S(2)}, u32[]{:S(2)}) collective-permute-start(bf16[2,144,896]{2,1,0:T(8,128)(2,1)S(1)} %slice.90), channel_id=1, source_target_pairs={{0,12},{1,13},{2,14},{3,15},{4,0},{5,1},{6,2},{7,3},{8,4},{9,5},{1... | collective-permute-start | bytes 1548296 | tf_op jit(solution)/shard_map/ppermute | solution.py:24
  156.4 47.9 %collective-permute-start.32 = (bf16[2,272,896]{2,1,0:T(8,128)(2,1)S(1)}, bf16[2,272,896]{2,1,0:T(8,128)(2,1)S(1)}, u32[]{:S(2)}, u32[]{:S(2)}) collective-permute-start(bf16[2,272,896]{2,1,0:T(8,128)(2,1)S(1)} %get-tuple-element.84), channel_id=1, source_target_pairs={{0,1},{1,0},{2,3},{3,2},{4,5},{5,4},{6,7},{7,6},{8,9},{9,8},{10,11... | collective-permute-start | bytes 2924552 | tf_op jit(solution)/shard_map/ppermute | solution.py:24
  167.2 37.1 %collective-permute-start.36 = (bf16[2,272,896]{2,1,0:T(8,128)(2,1)S(1)}, bf16[2,272,896]{2,1,0:T(8,128)(2,1)S(1)}, u32[]{:S(2)}, u32[]{:S(2)}) collective-permute-start(bf16[2,272,896]{2,1,0:T(8,128)(2,1)S(1)} %add_convert_fusion.4), channel_id=1, source_target_pairs={{0,4},{1,5},{2,6},{3,7},{4,8},{5,9},{6,10},{7,11},{8,12},{9,13},{1... | collective-permute-start | bytes 2924552 | tf_op jit(solution)/shard_map/ppermute | solution.py:24
  167.8 36.5 %collective-permute-start.39 = (bf16[2,272,896]{2,1,0:T(8,128)(2,1)S(1)}, bf16[2,272,896]{2,1,0:T(8,128)(2,1)S(1)}, u32[]{:S(2)}, u32[]{:S(2)}) collective-permute-start(bf16[2,272,896]{2,1,0:T(8,128)(2,1)S(1)} %add_convert_fusion.3), channel_id=1, source_target_pairs={{0,12},{1,13},{2,14},{3,15},{4,0},{5,1},{6,2},{7,3},{8,4},{9,5},{1... | collective-permute-start | bytes 2924552 | tf_op jit(solution)/shard_map/ppermute | solution.py:24
  203.8 17.0 %collective-permute-start.47 = (bf16[2,272,896]{2,1,0:T(8,128)(2,1)S(1)}, bf16[2,272,896]{2,1,0:T(8,128)(2,1)S(1)}, u32[]{:S(2)}, u32[]{:S(2)}) collective-permute-start(bf16[2,272,896]{2,1,0:T(8,128)(2,1)S(1)} %get-tuple-element.106), channel_id=1, source_target_pairs={{0,1},{1,0},{2,3},{3,2},{4,5},{5,4},{6,7},{7,6},{8,9},{9,8},{10,11... | collective-permute-start | bytes 2924552 | tf_op jit(solution)/shard_map/ppermute | solution.py:24
  204.3 9.4 %collective-permute-start.43 = (bf16[2,272,896]{2,1,0:T(8,128)(2,1)S(1)}, bf16[2,272,896]{2,1,0:T(8,128)(2,1)S(1)}, u32[]{:S(2)}, u32[]{:S(2)}) collective-permute-start(bf16[2,272,896]{2,1,0:T(8,128)(2,1)S(1)} %get-tuple-element.101), channel_id=1, source_target_pairs={{0,1},{1,0},{2,3},{3,2},{4,5},{5,4},{6,7},{7,6},{8,9},{9,8},{10,11... | collective-permute-start | bytes 2924552 | tf_op jit(solution)/shard_map/ppermute | solution.py:24
  206.6 13.8 %collective-permute-start.45 = (bf16[2,128,896]{2,1,0:T(8,128)(2,1)S(1)}, bf16[2,128,896]{2,1,0:T(8,128)(2,1)S(1)}, u32[]{:S(2)}, u32[]{:S(2)}) collective-permute-start(bf16[2,128,896]{2,1,0:T(8,128)(2,1)S(1)} %slice.79), channel_id=1, source_target_pairs={{0,4},{1,5},{2,6},{3,7},{4,8},{5,9},{6,10},{7,11},{8,12},{9,13},{1... | collective-permute-start | bytes 1376264 | tf_op jit(solution)/shard_map/ppermute | solution.py:24
  206.7 14.3 %collective-permute-start.48 = (bf16[2,144,896]{2,1,0:T(8,128)(2,1)S(1)}, bf16[2,144,896]{2,1,0:T(8,128)(2,1)S(1)}, u32[]{:S(2)}, u32[]{:S(2)}) collective-permute-start(bf16[2,144,896]{2,1,0:T(8,128)(2,1)S(1)} %slice.80), channel_id=1, source_target_pairs={{0,12},{1,13},{2,14},{3,15},{4,0},{5,1},{6,2},{7,3},{8,4},{9,5},{1... | collective-permute-start | bytes 1548296 | tf_op jit(solution)/shard_map/ppermute | solution.py:24
  210.0 83.0 %collective-permute-start.52 = (bf16[128,7168]{1,0:T(8,128)(2,1)S(1)}, bf16[128,7168]{1,0:T(8,128)(2,1)S(1)}, u32[]{:S(2)}, u32[]{:S(2)}) collective-permute-start(bf16[128,7168]{1,0:T(8,128)(2,1)S(1)} %forward.4), channel_id=1, source_target_pairs={{0,17},{1,16},{2,19},{3,18},{4,21},{5,20},{6,23},{7,22},{8,25},{9,... | collective-permute-start | bytes 5505032 | tf_op jit(solution)/shard_map/ppermute | solution.py:43
  213.7 79.7 %collective-permute-start.54 = (bf16[128,7168]{1,0:T(8,128)(2,1)S(1)}, bf16[128,7168]{1,0:T(8,128)(2,1)S(1)}, u32[]{:S(2)}, u32[]{:S(2)}) collective-permute-start(bf16[128,7168]{1,0:T(8,128)(2,1)S(1)} %forward.5), channel_id=1, source_target_pairs={{16,1},{17,0},{18,3},{19,2},{20,5},{21,4},{22,7},{23,6},{24,9},{25... | collective-permute-start | bytes 5505032 | tf_op jit(solution)/shard_map/ppermute | solution.py:43
  220.8 25.3 %collective-permute-start.46 = (bf16[2,272,896]{2,1,0:T(8,128)(2,1)S(1)}, bf16[2,272,896]{2,1,0:T(8,128)(2,1)S(1)}, u32[]{:S(2)}, u32[]{:S(2)}) collective-permute-start(bf16[2,272,896]{2,1,0:T(8,128)(2,1)S(1)} %add_convert_fusion.1), channel_id=1, source_target_pairs={{0,4},{1,5},{2,6},{3,7},{4,8},{5,9},{6,10},{7,11},{8,12},{9,13},{1... | collective-permute-start | bytes 2924552 | tf_op jit(solution)/shard_map/ppermute | solution.py:24
  221.3 24.7 %collective-permute-start.49 = (bf16[2,272,896]{2,1,0:T(8,128)(2,1)S(1)}, bf16[2,272,896]{2,1,0:T(8,128)(2,1)S(1)}, u32[]{:S(2)}, u32[]{:S(2)}) collective-permute-start(bf16[2,272,896]{2,1,0:T(8,128)(2,1)S(1)} %add_convert_fusion), channel_id=1, source_target_pairs={{0,12},{1,13},{2,14},{3,15},{4,0},{5,1},{6,2},{7,3},{8,4},{9,5},{1... | collective-permute-start | bytes 2924552 | tf_op jit(solution)/shard_map/ppermute | solution.py:24
  293.0 35.4 %collective-permute-start.53 = (bf16[128,7168]{1,0:T(8,128)(2,1)S(1)}, bf16[128,7168]{1,0:T(8,128)(2,1)S(1)}, u32[]{:S(2)}, u32[]{:S(2)}) collective-permute-start(bf16[128,7168]{1,0:T(8,128)(2,1)S(1)} %collective-permute-done.52), channel_id=1, source_target_pairs={{0,1},{1,0},{2,3},{3,2},{4,5},{5,4},{6,7},{7,6},{8,9},{9,8},{10,11... | collective-permute-start | bytes 5505032 | tf_op jit(solution)/shard_map/ppermute | solution.py:24
  293.4 40.9 %collective-permute-start.55 = (bf16[128,7168]{1,0:T(8,128)(2,1)S(1)}, bf16[128,7168]{1,0:T(8,128)(2,1)S(1)}, u32[]{:S(2)}, u32[]{:S(2)}) collective-permute-start(bf16[128,7168]{1,0:T(8,128)(2,1)S(1)} %collective-permute-done.54), channel_id=1, source_target_pairs={{0,1},{1,0},{2,3},{3,2},{4,5},{5,4},{6,7},{7,6},{8,9},{9,8},{10,11... | collective-permute-start | bytes 5505032 | tf_op jit(solution)/shard_map/ppermute | solution.py:24
  293.6 32.7 %collective-permute-start.40 = (bf16[272,896]{1,0:T(8,128)(2,1)S(1)}, bf16[272,896]{1,0:T(8,128)(2,1)S(1)}, u32[]{:S(2)}, u32[]{:S(2)}) collective-permute-start(bf16[272,896]{1,0:T(8,128)(2,1)S(1)} %fusion), channel_id=1, source_target_pairs={{0,2},{1,3},{2,0},{3,1},{4,6},{5,7},{6,4},{7,5},{8,10},{9,11},{10,... | collective-permute-start | bytes 1462280 | tf_op jit(solution)/shard_map/ppermute | solution.py:24
  295.5 30.8 %collective-permute-start.50 = (bf16[272,896]{1,0:T(8,128)(2,1)S(1)}, bf16[272,896]{1,0:T(8,128)(2,1)S(1)}, u32[]{:S(2)}, u32[]{:S(2)}) collective-permute-start(bf16[272,896]{1,0:T(8,128)(2,1)S(1)} %get-tuple-element.133), channel_id=1, source_target_pairs={{0,112},{1,113},{2,114},{3,115},{4,116},{5,117},{6,118},{7,119},{8... | collective-permute-start | bytes 1462280 | tf_op jit(solution)/shard_map/ppermute | solution.py:32
  296.8 30.2 %collective-permute-start.51 = (bf16[272,896]{1,0:T(8,128)(2,1)S(1)}, bf16[272,896]{1,0:T(8,128)(2,1)S(1)}, u32[]{:S(2)}, u32[]{:S(2)}) collective-permute-start(bf16[272,896]{1,0:T(8,128)(2,1)S(1)} %get-tuple-element.132), channel_id=1, source_target_pairs={{0,114},{1,115},{2,112},{3,113},{4,118},{5,119},{6,116},{7,117},{8... | collective-permute-start | bytes 1462280 | tf_op jit(solution)/shard_map/ppermute | solution.py:32
  (17 other events, 162.7 us)

commit v3 on v2

--- a/solution.py
+++ b/solution.py
@@ -8,10 +8,9 @@
 from jax.sharding import PartitionSpec as P
 
 EPS = 1e-06
-LATE = 1
 NX, NZ, NC = 4, 2, 2
 NDP = NX * NZ * NC
-CH = 1024
+CH = 1792
 BF = jnp.bfloat16
 F32 = jnp.float32
 
@@ -43,6 +42,11 @@
     return lax.ppermute(value, ("section", "dp"), pairs)
 
 
+def halves(value):
+    half = value.shape[0] // 2
+    return value[:half], value[half:]
+
+
 def after(value, *others):
     return lax.optimization_barrier((value, *others))[0]
 
@@ -76,16 +80,14 @@
         place = ((x + dx) & 3) * 4 + ((z + dz) & 1) * 2 + ((c + dc) & 1)
         dst_ref[pl.ds(pl.multiple_of(place * rows, 64), rows), :] = value
 
-    many = len(pieces) == 5 * NC
     for n in range(NZ * NC):
         dc, dz = n // NZ, n % NZ
-        group = pieces[5 * dc : 5 * dc + 5] if many else pieces[5 * n : 5 * n + 5]
-        at = (dz,) if many else ()
-        for ref, dx in ((group[0], 0), (group[1], 3), (group[2], 1)):
-            put(wd, ref[at + (0,)], dx, dz, dc)
-            put(wu, ref[at + (1,)], dx, dz, dc)
-        put(wd, group[3][at] if many else group[3][...], 2, dz, dc)
-        put(wu, group[4][at] if many else group[4][...], 2, dz, dc)
+        near, right, left, far_a, far_b = pieces[5 * dc : 5 * dc + 5]
+        for ref, dx in ((near, 0), (right, 3), (left, 1)):
+            put(wd, ref[dz, 0], dx, dz, dc)
+            put(wu, ref[dz, 1], dx, dz, dc)
+        put(wd, far_a[dz], 2, dz, dc)
+        put(wu, far_b[dz], 2, dz, dc)
 
 
 def chunks(ref):
@@ -121,6 +123,8 @@
 
 
 def forward_kernel(x_ref, gain_ref, lgain_ref, wd, wu, out_ref):
+    count = out_ref.shape[0]
+    x_ref = x_ref.at[x_ref.shape[0] - count :, :]
     scale = norm_scale(x_ref)
     latent = latent_of(x_ref, gain_ref, wd, None, scale)
     scale2 = lax.rsqrt(jnp.mean(latent * latent, axis=1, keepdims=True) + EPS)
@@ -179,12 +183,17 @@
 
 
 def backward_first_kernel(idx, *refs):
+    pieces, refs = refs[:10], refs[10:]
+    if len(refs) > 13:
+        rider_ref, refs = refs[0], refs[1:]
+        count = rider_ref.shape[0]
+        refs[4][count:, :] = rider_ref[...]
     (x_ref, g_ref, gain_ref, lgain_ref, back_ref, nrm_ref, sc_ref, dlat_ref, dgain_ref, dlg_ref,
-     wd, wu, dn_ref) = refs[-13:]
-    place_pieces(idx, refs[:-13], wd, wu)
+     wd, wu, dn_ref) = refs
+    place_pieces(idx, pieces, wd, wu)
     dgain_ref[...] = jnp.zeros(dgain_ref.shape, F32)
     scaled, dlat, dlg = backward_core(
-        x_ref, g_ref, gain_ref, lgain_ref, wd, wu, nrm_ref, dn_ref, dgain_ref, back_ref
+        x_ref, g_ref, gain_ref, lgain_ref, wd, wu, nrm_ref, dn_ref, dgain_ref, back_ref.at[: x_ref.shape[0], :]
     )
     sc_ref[...] = scaled
     dlat_ref[...] = dlat
@@ -195,6 +204,7 @@
                          dgain0_ref, dlg0_ref, back_ref, *refs):
     keep, send, (dn_ref, nrm_ref, dgain_ref) = refs[:NX], refs[NX : 2 * NX], refs[2 * NX :]
     dgain_ref[...] = dgain0_ref[...]
+    g_ref = g_ref.at[: x_ref.shape[0], :]
     scaled, dlat, dlg = backward_core(
         x_ref, g_ref, gain_ref, lgain_ref, wd, wu, nrm_ref, dn_ref, dgain_ref, back_ref
     )
@@ -229,21 +239,21 @@
 VMEM = functools.partial(pl.BlockSpec, memory_space=pltpu.VMEM)
 
 
-def forward(whole, x, gain, lgain, work=1):
-    t, width = x.shape
+def forward(whole, x, gain, lgain, t):
+    width = x.shape[1]
     rank = lgain.shape[1]
     return pl.pallas_call(
         forward_kernel,
-        out_shape=jax.ShapeDtypeStruct(x.shape, BF),
+        out_shape=jax.ShapeDtypeStruct((t, width), BF),
         in_specs=[VMEM()] * 5,
         out_specs=VMEM(),
         compiler_params=pltpu.CompilerParams(vmem_limit_bytes=6 << 20),
-        cost_estimate=pl.CostEstimate(flops=4 * t * width * rank, transcendentals=0, bytes_accessed=4 * work * width * (t + rank)),
+        cost_estimate=pl.CostEstimate(flops=t * width * rank, transcendentals=0, bytes_accessed=width * t),
         name="forward",
     )(x, gain, lgain, *whole)
 
 
-def backward_first(idx, pieces, x, g, gain, lgain):
+def backward_first(idx, pieces, x, g, gain, lgain, rider=()):
     t, width = x.shape
     rank = lgain.shape[1]
     act = jax.ShapeDtypeStruct(x.shape, BF)
@@ -251,14 +261,14 @@
     mat = jax.ShapeDtypeStruct((width, rank), BF)
     return pl.pallas_call(
         backward_first_kernel,
-        out_shape=(act, act, lat, lat, jax.ShapeDtypeStruct((1, width), F32), jax.ShapeDtypeStruct((1, rank), F32), mat, mat),
-        in_specs=[SMEM()] + [VMEM()] * (len(pieces) + 4),
+        out_shape=(jax.ShapeDtypeStruct((t * (1 + len(rider)), width), BF), act, lat, lat, jax.ShapeDtypeStruct((1, width), F32), jax.ShapeDtypeStruct((1, rank), F32), mat, mat),
+        in_specs=[SMEM()] + [VMEM()] * (len(pieces) + len(rider) + 4),
         out_specs=(VMEM(),) * 8,
         scratch_shapes=[pltpu.VMEM(x.shape, BF)],
         compiler_params=pltpu.CompilerParams(vmem_limit_bytes=8 << 20),
         cost_estimate=pl.CostEstimate(flops=6 * t * width * rank, transcendentals=0, bytes_accessed=4 * width * (2 * t + rank)),
         name="backward_first",
-    )(idx, *pieces, x, g, gain, lgain)
+    )(idx, *pieces, *rider, x, g, gain, lgain)
 
 
 def backward_last(idx, x, g, gain, lgain, first, g0):
@@ -279,7 +289,7 @@
             pltpu.VMEM((1, width), F32),
         ],
         compiler_params=pltpu.CompilerParams(vmem_limit_bytes=12 << 20),
-        cost_estimate=pl.CostEstimate(flops=14 * t * width * rank, transcendentals=0, bytes_accessed=4 * width * (4 * t + 2 * rank)),
+        cost_estimate=pl.CostEstimate(flops=t * width * rank, transcendentals=0, bytes_accessed=width * t),
         name="backward_last",
     )(idx, x, g, gain, lgain, wd, wu, nrm0, g0, sc0, dlat0, dgain0, dlg0)
     return out[0], out[1 : 1 + NX], out[1 + NX :]
@@ -293,7 +303,7 @@
     return dp_move(far[:, :half], fx=1), dp_move(far[:, half:], fx=-1), keep, recv
 
 
-def ring_sums(parts):
+def ring_sums(parts, *others):
     got_a, got_b, keep, recv = parts
     half = got_a.shape[1]
     rows = keep[0].shape[1]
@@ -303,9 +313,20 @@
 
     got_a = jnp.pad(got_a.astype(F32), ((0, 0), (0, rows - half), (0, 0)))
     got_b = jnp.pad(got_b.astype(F32), ((0, 0), (half, 0), (0, 0)))
-    from_left = dp_move((both(1) + got_a).astype(BF), fx=1)
-    from_right = dp_move((both(3) + got_b).astype(BF), fx=-1)
+    to_right, to_left = lax.optimization_barrier(
+        ((both(1) + got_a).astype(BF), (both(3) + got_b).astype(BF), *others)
+    )[:2]
+    from_left = dp_move(to_right, fx=1)
+    from_right = dp_move(to_left, fx=-1)
     return both(0) + from_left.astype(F32) + from_right.astype(F32)
+
+
+def direct_sums(keep, send):
+    pairs = [k.astype(F32) + dp_move(b, fc=1).astype(F32) for k, b in zip(keep, send)]
+    total = pairs[0]
+    for dx in (2, 1, 3):
+        total = total + dp_move(pairs[dx].astype(BF), fx=dx).astype(F32)
+    return total
 
 
 def split_kernel(idx, own_ref, a_ref, b_ref, c_ref, mine_ref, yours_ref, row_ref, lrow_ref):
@@ -375,48 +396,46 @@
 
     shard = after(jnp.stack([w_down[0], w_up[0].T]), idx)
     across = dp_move(shard, fz=1)
-    near_own = ring(shard)
-    near_across = ring(after(across, near_own[1], near_own[2]))
-    shard_m = after(shard, *near_across[1:])
+    near_own = ring(jnp.stack([shard, across]))
+    shard_m = after(shard, across)
     mirrored = mirror(shard_m)
     mirrored_z = mirror(shard_m, fz=1)
-    near_own = far_halves(near_own)
-    near_across = far_halves(near_across)
-    pieces_a = near_own + near_across
-    pieces_a = pieces_a + other_core(near_own) + other_core(near_across)
     gains = jnp.concatenate([norm_gain[0], latent_gain[0]]).reshape(-1, 128)
-    gains_m = mirror(after(gains, *near_across[1:])).reshape(1, -1)
+    gains = mirror(after(gains, across))
+    near_own = far_halves(lax.optimization_barrier((*near_own, gains))[:3])
+    pieces_a = near_own + other_core(near_own)
+    gains_m = gains.reshape(1, -1)
     gain_a, lgain_a = norm_gain, latent_gain
     gain_b, lgain_b = gains_m[:, :width], gains_m[:, width:]
     both_m = jnp.stack([mirrored, mirrored_z])
-    near_m = ring(after(both_m, *near_own[3:], *near_across[3:]))
+    near_m = ring(after(both_m, *near_own[3:]))
 
     first_a = backward_first(idx, pieces_a, saved_a[0, 0], cotan_a[0], gain_a, lgain_a)
-    ga = relay(first_a[0], -1)
+    ga = [relay(h, -1) for h in halves(first_a[0])]
     near_m = far_halves(lax.optimization_barrier((*near_m, first_a[2]))[:3])
     pieces_b = near_m + other_core(near_m)
-    first_b = backward_first(idx, pieces_b, saved_b[0, 0], cotan_b[0], gain_b, lgain_b)
-    gb = relay(first_b[0], 1)
-    ya = forward(first_a[6:], enter_a[0], gain_a, lgain_a)
-    yb = forward(first_b[6:], enter_b[0], gain_b, lgain_b)
-    xa = relay(ya, 1, fc=1)
-    xb = relay(yb, -1, fc=1)
-
-    back_a, keep_a, send_a = backward_last(idx, saved_a[1, 0], after(ga, ya, yb), gain_a, lgain_a, first_a, cotan_a[0])
-    half_a = pair_sums(keep_a, send_a)
-    gb = after(gb, ya, yb, half_a[0], half_a[1])
-    back_b, keep_b, send_b = backward_last(idx, saved_b[1, 0], gb, gain_b, lgain_b, first_b, cotan_b[0])
-    sums_a = ring_sums(half_a)
-    sums_b = ring_sums(pair_sums(keep_b, send_b, sums_a))
-    xa = dp_move(after(xa, sums_b), fc=1)
-    xb = dp_move(after(xb, sums_b), fc=1)
+    t = enter_a.shape[1]
+    ya = forward(first_a[6:], enter_a[0], gain_a, lgain_a, t)
+    first_b = backward_first(
+        idx, pieces_b, saved_b[0, 0], after(cotan_b[0], ga[0]), gain_b, lgain_b, [ya]
+    )
+    ahead = relay(first_b[0], 1)
+    yb = forward(first_b[6:], after(enter_b[0], ga[1]), gain_b, lgain_b, t)
+
+    ga = after(jnp.concatenate(ga), yb)
+    back_a, keep_a, send_a = backward_last(idx, saved_a[1, 0], ga, gain_a, lgain_a, first_a, cotan_a[0])
+    sums_a = direct_sums(keep_a, send_a)
     got_z = dp_move(sums_a[1].astype(BF), fz=1)
-    got_m = mirror(sums_b[0].astype(BF))
+    ahead = after(ahead, sums_a)
+    back_b, keep_b, send_b = backward_last(idx, saved_b[1, 0], ahead, gain_b, lgain_b, first_b, cotan_b[0])
+    out_a = forward(first_a[6:], ahead, gain_a, lgain_a, t)
+    sums_b = ring_sums(pair_sums(keep_b, send_b, sums_a), out_a)
+    xb = dp_move(after(relay(after(yb, ahead, got_z), -1, fc=1), sums_b), fc=1)
+    out_b = forward(first_b[6:], xb, gain_b, lgain_b, t)
+    got_m = after(mirror(sums_b[0].astype(BF)), out_b)
     got_mz = mirror(sums_b[1].astype(BF), fz=1)
     mine, yours, row, lrow = split_columns(idx, sums_a[0], got_z, got_m, got_mz, rank, cols)
-    out_a = forward(first_a[6:], xa, gain_a, lgain_a, LATE)
-    out_b = forward(first_b[6:], xb, gain_b, lgain_b, LATE)
-    yours, out_a, out_b = lax.optimization_barrier((yours, out_a, out_b))
+    yours = after(yours, out_b)
     grad_down, grad_up = join_halves(idx, mine, dp_move(yours, fc=1))
     grad_lgain = lax.dynamic_slice(lrow, (jnp.uint32(0), place.astype(jnp.uint32) * (rank // NDP)), (1, rank // NDP))
     return (

time: 348 us -> 298 us (0.86)
  waiting for transfers between devices: 201 us -> 174 us
  starting transfers between devices: 67.7 us -> 53.3 us
  Pallas kernels: 65.4 us -> 58.9 us
    ppermute x4, waiting for transfers between devices: 83.2 us -> 26 us  [relay(): return lax.ppermute(value, ('section', 'dp'), pairs)]
    ppermute x48 -> x37, waiting for transfers between devices: 106 us -> 129 us  [dp_move(): return lax.ppermute(value, 'dp', pairs)]
    ppermute x48 -> x37, starting transfers between devices: 43.8 us -> 30.7 us  [dp_move(): return lax.ppermute(value, 'dp', pairs)]
    ppermute x5, waiting for transfers between devices: 11.8 us -> 19.2 us  [mirror(): return lax.ppermute(value, ('section', 'dp'), pairs)]
    pallas_call x6, Pallas kernels: 38.6 us -> 34.9 us  [the longest x4 17.8 us: forward(): pl.pallas_call(forward_kernel, out_shape=jax.ShapeDtypeStruct((t, width),...]
  transfers between devices with their start and end apart: 57 -> 46, of which waited for: 23 -> 22; matrix products, arithmetic and copies ran while one was open for 1% -> 2% of each run, Pallas kernels for 13% -> 15%
where the time goes in v3:
time: 298 us; the launch traced here: 296 us
  waiting for transfers between devices  174 us (58%)
  Pallas kernels  58.9 us (20%)
  starting transfers between devices  53.3 us (18%)
  other arithmetic  4.83 us (2%)
  local copies, waits for them, and re-layouts  4.28 us (1%)
    ppermute x37, waiting for transfers between devices, dp_move(): return lax.ppermute(value, 'dp', pairs)  129 us
    ppermute x37, starting transfers between devices, dp_move(): return lax.ppermute(value, 'dp', pairs)  30.7 us
    ppermute x4, waiting for transfers between devices, relay(): return lax.ppermute(value, ('section', 'dp'), pairs)  26 us
    pallas_call x2, Pallas kernels, backward_last(): pl.pallas_call(backward_last_kernel, out_shape=(act,) + (block,) * (2 * N...  21 us
    ppermute x5, waiting for transfers between devices, mirror(): return lax.ppermute(value, ('section', 'dp'), pairs)  19.2 us
    pallas_call x4, Pallas kernels, forward(): pl.pallas_call(forward_kernel, out_shape=jax.ShapeDtypeStruct((t, width),...  17.8 us
    pallas_call x2, Pallas kernels, backward_first(): pl.pallas_call(backward_first_kernel, out_shape=(jax.ShapeDtypeStruct((t...  17 us
    ppermute x5, starting transfers between devices, mirror(): return lax.ppermute(value, ('section', 'dp'), pairs)  15.5 us
  transfers between devices with their start and end apart: 46, of which 22 were waited for; matrix products, arithmetic and copies ran while one was open for 2% of the time, Pallas kernels for 15%

profile of v3, /device:TPU:0, one launch (start us, length us, event | category | flops | bytes accessed | tf_op | source)
XLA Modules:
  0.0 296.1 jit_solution(4435242752912965361)
XLA Ops:
  2.6 4.0 %collective-permute-start = (bf16[2,448,256]{2,1,0:T(8,128)(2,1)S(1)}, bf16[2,448,256]{2,1,0:T(8,128)(2,1)S(1)}, u32[]{:S(2)}, u32[]{:S(2)}) collective-permute-start(bf16[2,448,256]{2,1,0:T(8,128)(2,1)S(1)} %pad_maximum_fusion.3), channel_id=1, source_target_pairs={{0,2},{1,3},{2,0},{3,1},{4,6},{5,7},{6,4},{7,5},{8,10},{9,11},{10,... | collective-permute-start | bytes 1376264 | tf_op jit(solution)/shard_map/ppermute | solution.py:23
  6.6 10.5 %collective-permute-done = bf16[2,448,256]{2,1,0:T(8,128)(2,1)S(1)} collective-permute-done((bf16[2,448,256]{2,1,0:T(8,128)(2,1)S(1)}, bf16[2,448,256]{2,1,0:T(8,128)(2,1)S(1)}, u32[]{:S(2)}, u32[]{:S(2)}) %collective-permute-start) | collective-permute-done | bytes 458784 | tf_op jit(solution)/shard_map/ppermute | solution.py:23
  17.2 2.8 collective-permute-start.4
  20.0 3.8 %collective-permute-start.5 = (f32[58,128]{1,0:T(8,128)S(1)}, f32[58,128]{1,0:T(8,128)S(1)}, u32[]{:S(2)}, u32[]{:S(2)}) collective-permute-start(f32[58,128]{1,0:T(8,128)S(1)} %maximum_bitcast_fusion), channel_id=1, source_target_pairs={{0,112},{1,113},{2,114},{3,115},{4,116},{5,117},{6,118},{7,119},{8... | collective-permute-start | bytes 89096 | tf_op jit(solution)/shard_map/ppermute | solution.py:31
  23.8 2.2 collective-permute-start.2
  26.1 3.4 %collective-permute-start.1 = (bf16[2,448,256]{2,1,0:T(8,128)(2,1)S(1)}, bf16[2,448,256]{2,1,0:T(8,128)(2,1)S(1)}, u32[]{:S(2)}, u32[]{:S(2)}) collective-permute-start(bf16[2,448,256]{2,1,0:T(8,128)(2,1)S(1)} %pad_maximum_fusion.3), channel_id=1, source_target_pairs={{0,112},{1,113},{2,114},{3,115},{4,116},{5,117},{6,118},{7,119},{8... | collective-permute-start | bytes 1376264 | tf_op jit(solution)/shard_map/ppermute | solution.py:31
  29.5 9.6 %collective-permute-done.4.refs_2_ = bf16[2,2,448,256]{3,2,1,0:T(8,128)(2,1)S(1)} collective-permute-done((bf16[2,2,448,256]{3,2,1,0:T(8,128)(2,1)S(1)}, bf16[2,2,448,256]{3,2,1,0:T(8,128)(2,1)S(1)}, u32[]{:S(2)}, u32[]{:S(2)}) %collective-permute-start.4) | collective-permute-done | bytes 917536 | tf_op jit(solution)/shard_map/ppermute | solution.py:23
  39.1 3.4 %collective-permute-done.3.refs_1_ = bf16[2,2,448,256]{3,2,1,0:T(8,128)(2,1)S(1)} collective-permute-done((bf16[2,2,448,256]{3,2,1,0:T(8,128)(2,1)S(1)}, bf16[2,2,448,256]{3,2,1,0:T(8,128)(2,1)S(1)}, u32[]{:S(2)}, u32[]{:S(2)}) %collective-permute-start.3) | collective-permute-done | bytes 917536 | tf_op jit(solution)/shard_map/ppermute | solution.py:23
  42.9 1.8 collective-permute-start.6
  45.2 2.9 collective-permute-done.1
  48.1 4.9 %collective-permute-done.7.refs_4_ = bf16[2,448,256]{2,1,0:T(8,128)(2,1)S(1)} collective-permute-done((bf16[2,448,256]{2,1,0:T(8,128)(2,1)S(1)}, bf16[2,448,256]{2,1,0:T(8,128)(2,1)S(1)}, u32[]{:S(2)}, u32[]{:S(2)}) %collective-permute-start.7) | collective-permute-done | bytes 458784 | tf_op jit(solution)/shard_map/ppermute | solution.py:23
  53.1 1.6 collective-permute-done.6.refs_3_
  55.0 1.6 collective-permute-start.9
  57.2 7.6 %backward_first.2 = (bf16[128,7168]{1,0:T(8,128)(2,1)S(1)}, bf16[128,7168]{1,0:T(8,128)(2,1)S(1)}, bf16[128,256]{1,0:T(8,128)(2,1)S(1)}, bf16[128,256]{1,0:T(8,1...) custom-call(s32[3]{0:T(128)S(1)} %shift-right-arithmetic_and_fusion., ...), custom_call_target="tpu_custom_call" | custom-call | flops 1409286144 | bytes 14680064 | tf_op jit(solution)/shard_map/backward_first/pallas_call | solution.py:262
  64.9 1.6 collective-permute-start.22
  66.4 11.4 %collective-permute-done.9 = bf16[2,2,448,256]{3,2,0,1:T(8,128)(2,1)S(1)} collective-permute-done((bf16[2,2,448,256]{3,2,0,1:T(8,128)(2,1)S(1)}, bf16[2,2,448,256]{3,2,0,1:T(8,128)(2,1)S(1)}, u32[]{:S(2)}, u32[]{:S(2)}) %collective-permute-start.9) | collective-permute-done | bytes 917536 | tf_op jit(solution)/shard_map/ppermute | solution.py:23
  77.9 2.2 collective-permute-done.8
  80.4 1.9 collective-permute-start.15
  82.3 1.4 collective-permute-start.24
  83.7 9.4 %collective-permute-done.16.refs_4_ = bf16[2,448,256]{2,1,0:T(8,128)(2,1)S(1)} collective-permute-done((bf16[2,448,256]{2,1,0:T(8,128)(2,1)S(1)}, bf16[2,448,256]{2,1,0:T(8,128)(2,1)S(1)}, u32[]{:S(2)}, u32[]{:S(2)}) %collective-permute-start.16) | collective-permute-done | bytes 458784 | tf_op jit(solution)/shard_map/ppermute | solution.py:23
  93.1 1.3 collective-permute-done.15.refs_3_
  95.6 3.8 %forward.4.refs_10_ = bf16[128,7168]{1,0:T(8,128)(2,1)S(1)} custom-call(bf16[128,7168]{1,0:T(8,128)(2,1)S(1)} %bitcast.58, f32[1,7168]{1,0:T(1,128)S(1)} %copy-done.4, f32[1,256]{1,0:T(1,128)S(1)} %copy-done.5, bf16[7168,256]{1,0:T(8,128)(2,1)S(1)} %get-tuple-element.80.wd, bf16[7168,256]{1,0:T(8,128)(2,1)S(1)} %get-tuple-element.81.wu), custom_call_target="tpu_custom_call" | custom-call | flops 234881024 | bytes 917504 | tf_op jit(solution)/shard_map/forward/pallas_call | solution.py:245
  99.9 1.3 copy-done.1
  101.2 9.5 %backward_first.3 = (bf16[256,7168]{1,0:T(8,128)(2,1)}, bf16[128,7168]{1,0:T(8,128)(2,1)S(1)}, bf16[128,256]{1,0:T(8,128)(2,1)S(1)}, bf16[128,256]{1,0:T(8,128)(...) custom-call(s32[3]{0:T(128)S(1)} %shift-right-arithmetic_and_fusion., ...), custom_call_target="tpu_custom_call" | custom-call | flops 1409286144 | bytes 14680064 | tf_op jit(solution)/shard_map/backward_first/pallas_call | solution.py:262
  110.6 2.9 collective-permute-start.23
  113.7 3.8 %forward.5 = bf16[128,7168]{1,0:T(8,128)(2,1)S(1)} custom-call(bf16[128,7168]{1,0:T(8,128)(2,1)S(1)} %bitcast.59, f32[1,7168]{1,0:T(1,128)S(1)} %slice.75.refs_13_.gain_ref, f32[1,256]{1,0:T(1,128)S(1)} %slice.76.refs_14_.lgain_ref, bf16[7168,256]{1,0:T(8,128)(2,1)S(1)} %get-tuple-element.86.wd, bf16[7168,256]{1,0:T(8,128)(2,1)S(1)} %get-tuple-element.87.wu), custom_call_target="tpu_custom_call" | custom-call | flops 234881024 | bytes 917504 | tf_op jit(solution)/shard_map/forward/pallas_call | solution.py:245
  117.6 10.5 %backward_last.2 = (bf16[128,7168]{1,0:T(8,128)(2,1)}, bf16[2,272,896]{2,1,0:T(8,128)(2,1)S(1)}, bf16[2,272,896]{2,1,0:T(8,128)(2,1)S(1)}, bf16[2,272,896]{2,1,0...) custom-call(s32[3]{0:T(128)S(1)} %shift-right-arithmetic_and_fusion., ...), custom_call_target="tpu_custom_call" | custom-call | flops 234881024 | bytes 917504 | tf_op jit(solution)/shard_map/backward_last/pallas_call | solution.py:281
  129.1 1.5 collective-permute-done.26
  133.7 2.4 collective-permute-start.31
  136.1 20.8 %collective-permute-done.27 = bf16[2,272,896]{2,1,0:T(8,128)(2,1)S(1)} collective-permute-done((bf16[2,272,896]{2,1,0:T(8,128)(2,1)S(1)}, bf16[2,272,896]{2,1,0:T(8,128)(2,1)S(1)}, u32[]{:S(2)}, u32[]{:S(2)}) %collective-permute-start.27) | collective-permute-done | bytes 974880 | tf_op jit(solution)/shard_map/ppermute | solution.py:23
  156.9 20.0 %collective-permute-done.29 = bf16[2,272,896]{2,1,0:T(8,128)(2,1)S(1)} collective-permute-done((bf16[2,272,896]{2,1,0:T(8,128)(2,1)S(1)}, bf16[2,272,896]{2,1,0:T(8,128)(2,1)S(1)}, u32[]{:S(2)}, u32[]{:S(2)}) %collective-permute-start.29) | collective-permute-done | bytes 974880 | tf_op jit(solution)/shard_map/ppermute | solution.py:23
  177.5 15.1 %collective-permute-done.23.x_ref.g_ref = bf16[256,7168]{1,0:T(8,128)(2,1)S(1)} collective-permute-done((bf16[256,7168]{1,0:T(8,128)(2,1)}, bf16[256,7168]{1,0:T(8,128)(2,1)S(1)}, u32[]{:S(2)}, u32[]{:S(2)}) %collective-permute-start.23) | collective-permute-done | bytes 3670048 | tf_op jit(solution)/shard_map/ppermute | solution.py:42
  192.6 10.5 %backward_last.3 = (bf16[128,7168]{1,0:T(8,128)(2,1)}, bf16[2,272,896]{2,1,0:T(8,128)(2,1)S(1)}, bf16[2,272,896]{2,1,0:T(8,128)(2,1)S(1)}, bf16[2,272,896]{2,1,0...) custom-call(s32[3]{0:T(128)S(1)} %shift-right-arithmetic_and_fusion., ...), custom_call_target="tpu_custom_call" | custom-call | flops 234881024 | bytes 917504 | tf_op jit(solution)/shard_map/backward_last/pallas_call | solution.py:281
  203.7 3.7 %collective-permute-start.32 = (bf16[272,896]{1,0:T(8,128)(2,1)S(1)}, bf16[272,896]{1,0:T(8,128)(2,1)S(1)}, u32[]{:S(2)}, u32[]{:S(2)}) collective-permute-start(bf16[272,896]{1,0:T(8,128)(2,1)S(1)} %fusion), channel_id=1, source_target_pairs={{0,2},{1,3},{2,0},{3,1},{4,6},{5,7},{6,4},{7,5},{8,10},{9,11},{10,... | collective-permute-start | bytes 1462280 | tf_op jit(solution)/shard_map/ppermute | solution.py:23
  208.3 2.8 collective-permute-start.39
  211.1 7.6 %collective-permute-done.32.a_ref = bf16[272,896]{1,0:T(8,128)(2,1)S(1)} collective-permute-done((bf16[272,896]{1,0:T(8,128)(2,1)S(1)}, bf16[272,896]{1,0:T(8,128)(2,1)S(1)}, u32[]{:S(2)}, u32[]{:S(2)}) %collective-permute-start.32) | collective-permute-done | bytes 487456 | tf_op jit(solution)/shard_map/ppermute | solution.py:23
  220.0 5.1 %forward.6 = bf16[128,7168]{1,0:T(8,128)(2,1)} custom-call(bf16[256,7168]{1,0:T(8,128)(2,1)S(1)} %collective-permute-done.23.x_ref.g_ref, f32[1,7168]{1,0:T(1,128)S(1)} %copy-done.4, f32[1,256]{1,0:T(1,128)S(1)} %copy-done.5, bf16[7168,256]{1,0:T(8,128)(2,1)S(1)} %get-tuple-element.80.wd, bf16[7168,256]{1,0:T(8,128)(2,1)S(1)} %get-tuple-element.81.wu), custom_call_target="tpu_custom_call" | custom-call | flops 234881024 | bytes 917504 | tf_op jit(solution)/shard_map/forward/pallas_call | solution.py:245
  226.3 2.7 collective-permute-start.41
  229.0 22.0 %collective-permute-done.40 = bf16[2,272,896]{2,1,0:T(8,128)(2,1)S(1)} collective-permute-done((bf16[2,272,896]{2,1,0:T(8,128)(2,1)S(1)}, bf16[2,272,896]{2,1,0:T(8,128)(2,1)S(1)}, u32[]{:S(2)}, u32[]{:S(2)}) %collective-permute-start.40) | collective-permute-done | bytes 974880 | tf_op jit(solution)/shard_map/ppermute | solution.py:23
  251.4 10.9 %collective-permute-done.33 = bf16[128,7168]{1,0:T(8,128)(2,1)S(1)} collective-permute-done((bf16[128,7168]{1,0:T(8,128)(2,1)S(1)}, bf16[128,7168]{1,0:T(8,128)(2,1)S(1)}, u32[]{:S(2)}, u32[]{:S(2)}) %collective-permute-start.33) | collective-permute-done | bytes 1835040 | tf_op jit(solution)/shard_map/ppermute | solution.py:42
  262.8 4.0 %collective-permute-start.43 = (bf16[272,896]{1,0:T(8,128)(2,1)S(1)}, bf16[272,896]{1,0:T(8,128)(2,1)S(1)}, u32[]{:S(2)}, u32[]{:S(2)}) collective-permute-start(bf16[272,896]{1,0:T(8,128)(2,1)S(1)} %get-tuple-element.145), channel_id=1, source_target_pairs={{0,112},{1,113},{2,114},{3,115},{4,116},{5,117},{6,118},{7,119},{8... | collective-permute-start | bytes 1462280 | tf_op jit(solution)/shard_map/ppermute | solution.py:31
  266.7 2.0 collective-permute-start.44
  268.8 5.1 %forward.7 = bf16[128,7168]{1,0:T(8,128)(2,1)} custom-call(bf16[128,7168]{1,0:T(8,128)(2,1)S(1)} %collective-permute-done.42.x_ref, f32[1,7168]{1,0:T(1,128)S(1)} %slice.75.refs_13_.gain_ref, f32[1,256]{1,0:T(1,128)S(1)} %slice.76.refs_14_.lgain_ref, bf16[7168,256]{1,0:T(8,128)(2,1)S(1)} %get-tuple-element.86.wd, bf16[7168,256]{1,0:T(8,128)(2,1)S(1)} %get-tuple-element.87.wu), custom_call_target="tpu_custom_call" | custom-call | flops 234881024 | bytes 917504 | tf_op jit(solution)/shard_map/forward/pallas_call | solution.py:245
  273.9 5.0 %collective-permute-done.43.b_ref = bf16[272,896]{1,0:T(8,128)(2,1)S(1)} collective-permute-done((bf16[272,896]{1,0:T(8,128)(2,1)S(1)}, bf16[272,896]{1,0:T(8,128)(2,1)S(1)}, u32[]{:S(2)}, u32[]{:S(2)}) %collective-permute-start.43) | collective-permute-done | bytes 487456 | tf_op jit(solution)/shard_map/ppermute | solution.py:31
  278.9 11.3 %collective-permute-done.44.c_ref = bf16[272,896]{1,0:T(8,128)(2,1)S(1)} collective-permute-done((bf16[272,896]{1,0:T(8,128)(2,1)S(1)}, bf16[272,896]{1,0:T(8,128)(2,1)S(1)}, u32[]{:S(2)}, u32[]{:S(2)}) %collective-permute-start.44) | collective-permute-done | bytes 487456 | tf_op jit(solution)/shard_map/ppermute | solution.py:31
  290.2 1.5 split_columns.1
  292.3 1.3 collective-permute-done.45.got_ref
  293.6 1.5 join_halves.1
  (107 shorter events, 16.9 us)
Async XLA Ops:
  1.8 52.9 %copy-start.6 = (bf16[2,1,128,7168]{3,2,1,0:T(8,128)(2,1)S(1)}, bf16[2,1,128,7168]{3,2,1,0:T(8,128)(2,1)}, u32[]{:S(2)}) copy-start(bf16[2,1,128,7168]{3,2,1,0:T(8,128)(2,1)} %param.16) | copy-start | bytes 11010052
  2.6 14.5 %collective-permute-start = (bf16[2,448,256]{2,1,0:T(8,128)(2,1)S(1)}, bf16[2,448,256]{2,1,0:T(8,128)(2,1)S(1)}, u32[]{:S(2)}, u32[]{:S(2)}) collective-permute-start(bf16[2,448,256]{2,1,0:T(8,128)(2,1)S(1)} %pad_maximum_fusion.3), channel_id=1, source_target_pairs={{0,2},{1,3},{2,0},{3,1},{4,6},{5,7},{6,4},{7,5},{8,10},{9,11},{10,... | collective-permute-start | bytes 1376264 | tf_op jit(solution)/shard_map/ppermute | solution.py:23
  17.2 21.9 %collective-permute-start.4 = (bf16[2,2,448,256]{3,2,1,0:T(8,128)(2,1)S(1)}, bf16[2,2,448,256]{3,2,1,0:T(8,128)(2,1)S(1)}, u32[]{:S(2)}, u32[]{:S(2)}) collective-permute-start(bf16[2,2,448,256]{3,2,1,0:T(8,128)(2,1)S(1)} %pad_maximum_fusion.2.refs_0_), channel_id=1, source_target_pairs={{0,12},{1,13},{2,14},{3,15},{4,0},{5,1},{6,2},{7,3},{8,4},{9,5},{1... | collective-permute-start | bytes 2752520 | tf_op jit(solution)/shard_map/ppermute | solution.py:23
  20.0 22.5 %collective-permute-start.3 = (bf16[2,2,448,256]{3,2,1,0:T(8,128)(2,1)S(1)}, bf16[2,2,448,256]{3,2,1,0:T(8,128)(2,1)S(1)}, u32[]{:S(2)}, u32[]{:S(2)}) collective-permute-start(bf16[2,2,448,256]{3,2,1,0:T(8,128)(2,1)S(1)} %pad_maximum_fusion.2.refs_0_), channel_id=1, source_target_pairs={{0,4},{1,5},{2,6},{3,7},{4,8},{5,9},{6,10},{7,11},{8,12},{9,13},{1... | collective-permute-start | bytes 2752520 | tf_op jit(solution)/shard_map/ppermute | solution.py:23
  20.0 9.5 %collective-permute-start.5 = (f32[58,128]{1,0:T(8,128)S(1)}, f32[58,128]{1,0:T(8,128)S(1)}, u32[]{:S(2)}, u32[]{:S(2)}) collective-permute-start(f32[58,128]{1,0:T(8,128)S(1)} %maximum_bitcast_fusion), channel_id=1, source_target_pairs={{0,112},{1,113},{2,114},{3,115},{4,116},{5,117},{6,118},{7,119},{8... | collective-permute-start | bytes 89096 | tf_op jit(solution)/shard_map/ppermute | solution.py:31
  23.8 20.9 %collective-permute-start.2 = (bf16[2,448,256]{2,1,0:T(8,128)(2,1)S(1)}, bf16[2,448,256]{2,1,0:T(8,128)(2,1)S(1)}, u32[]{:S(2)}, u32[]{:S(2)}) collective-permute-start(bf16[2,448,256]{2,1,0:T(8,128)(2,1)S(1)} %pad_maximum_fusion.3), channel_id=1, source_target_pairs={{0,114},{1,115},{2,112},{3,113},{4,118},{5,119},{6,116},{7,117},{8... | collective-permute-start | bytes 1376264 | tf_op jit(solution)/shard_map/ppermute | solution.py:31
  26.1 22.1 %collective-permute-start.1 = (bf16[2,448,256]{2,1,0:T(8,128)(2,1)S(1)}, bf16[2,448,256]{2,1,0:T(8,128)(2,1)S(1)}, u32[]{:S(2)}, u32[]{:S(2)}) collective-permute-start(bf16[2,448,256]{2,1,0:T(8,128)(2,1)S(1)} %pad_maximum_fusion.3), channel_id=1, source_target_pairs={{0,112},{1,113},{2,114},{3,115},{4,116},{5,117},{6,118},{7,119},{8... | collective-permute-start | bytes 1376264 | tf_op jit(solution)/shard_map/ppermute | solution.py:31
  42.5 10.6 %collective-permute-start.7 = (bf16[2,448,256]{2,1,0:T(8,128)(2,1)S(1)}, bf16[2,448,256]{2,1,0:T(8,128)(2,1)S(1)}, u32[]{:S(2)}, u32[]{:S(2)}) collective-permute-start(bf16[2,448,256]{2,1,0:T(8,128)(2,1)S(1)} %slice_bitcast_fusion.9), channel_id=1, source_target_pairs={{0,12},{1,13},{2,14},{3,15},{4,0},{5,1},{6,2},{7,3},{8,4},{9,5},{1... | collective-permute-start | bytes 1376264 | tf_op jit(solution)/shard_map/ppermute | solution.py:23
  42.9 11.8 %collective-permute-start.6 = (bf16[2,448,256]{2,1,0:T(8,128)(2,1)S(1)}, bf16[2,448,256]{2,1,0:T(8,128)(2,1)S(1)}, u32[]{:S(2)}, u32[]{:S(2)}) collective-permute-start(bf16[2,448,256]{2,1,0:T(8,128)(2,1)S(1)} %slice_bitcast_fusion.10), channel_id=1, source_target_pairs={{0,4},{1,5},{2,6},{3,7},{4,8},{5,9},{6,10},{7,11},{8,12},{9,13},{1... | collective-permute-start | bytes 1376264 | tf_op jit(solution)/shard_map/ppermute | solution.py:23
  44.7 12.4 %collective-permute-start.11 = (bf16[2,2,448,256]{3,2,1,0:T(8,128)(2,1)S(1)}, bf16[2,2,448,256]{3,2,1,0:T(8,128)(2,1)S(1)}, u32[]{:S(2)}, u32[]{:S(2)}) collective-permute-start(bf16[2,2,448,256]{3,2,1,0:T(8,128)(2,1)S(1)} %collective-permute-done.3.refs_1_), channel_id=1, source_target_pairs={{0,1},{1,0},{2,3},{3,2},{4,5},{5,4},{6,7},{7,6},{8,9},{9,8},{10,11... | collective-permute-start | bytes 2752520 | tf_op jit(solution)/shard_map/ppermute | solution.py:23
  44.7 12.4 %collective-permute-start.12 = (bf16[2,2,448,256]{3,2,1,0:T(8,128)(2,1)S(1)}, bf16[2,2,448,256]{3,2,1,0:T(8,128)(2,1)S(1)}, u32[]{:S(2)}, u32[]{:S(2)}) collective-permute-start(bf16[2,2,448,256]{3,2,1,0:T(8,128)(2,1)S(1)} %collective-permute-done.4.refs_2_), channel_id=1, source_target_pairs={{0,1},{1,0},{2,3},{3,2},{4,5},{5,4},{6,7},{7,6},{8,9},{9,8},{10,11... | collective-permute-start | bytes 2752520 | tf_op jit(solution)/shard_map/ppermute | solution.py:23
  48.1 9.0 %collective-permute-start.10 = (bf16[2,2,448,256]{3,2,1,0:T(8,128)(2,1)S(1)}, bf16[2,2,448,256]{3,2,1,0:T(8,128)(2,1)S(1)}, u32[]{:S(2)}, u32[]{:S(2)}) collective-permute-start(bf16[2,2,448,256]{3,2,1,0:T(8,128)(2,1)S(1)} %pad_maximum_fusion.2.refs_0_), channel_id=1, source_target_pairs={{0,1},{1,0},{2,3},{3,2},{4,5},{5,4},{6,7},{7,6},{8,9},{9,8},{10,11... | collective-permute-start | bytes 2752520 | tf_op jit(solution)/shard_map/ppermute | solution.py:23
  53.1 2.0 collective-permute-start.14
  54.7 2.0 collective-permute-start.13
  55.0 22.8 %collective-permute-start.9 = (bf16[2,2,448,256]{3,2,0,1:T(8,128)(2,1)S(1)}, bf16[2,2,448,256]{3,2,0,1:T(8,128)(2,1)S(1)}, u32[]{:S(2)}, u32[]{:S(2)}) collective-permute-start(bf16[2,2,448,256]{3,2,0,1:T(8,128)(2,1)S(1)} %pad_maximum_fusion.1), channel_id=1, source_target_pairs={{0,12},{1,13},{2,14},{3,15},{4,0},{5,1},{6,2},{7,3},{8,4},{9,5},{1... | collective-permute-start | bytes 2752520 | tf_op jit(solution)/shard_map/ppermute | solution.py:23
  56.7 23.4 %collective-permute-start.8 = (bf16[2,2,448,256]{3,2,0,1:T(8,128)(2,1)S(1)}, bf16[2,2,448,256]{3,2,0,1:T(8,128)(2,1)S(1)}, u32[]{:S(2)}, u32[]{:S(2)}) collective-permute-start(bf16[2,2,448,256]{3,2,0,1:T(8,128)(2,1)S(1)} %pad_maximum_fusion.1), channel_id=1, source_target_pairs={{0,4},{1,5},{2,6},{3,7},{4,8},{5,9},{6,10},{7,11},{8,12},{9,13},{1... | collective-permute-start | bytes 2752520 | tf_op jit(solution)/shard_map/ppermute | solution.py:23
  64.7 30.5 %copy-start.7 = (bf16[2,1,128,7168]{3,2,1,0:T(8,128)(2,1)S(1)}, bf16[2,1,128,7168]{3,2,1,0:T(8,128)(2,1)}, u32[]{:S(2)}) copy-start(bf16[2,1,128,7168]{3,2,1,0:T(8,128)(2,1)} %param.17) | copy-start | bytes 11010052
  64.9 29.6 %collective-permute-start.22 = (bf16[64,7168]{1,0:T(8,128)(2,1)S(1)}, bf16[64,7168]{1,0:T(8,128)(2,1)S(1)}, u32[]{:S(2)}, u32[]{:S(2)}) collective-permute-start(bf16[64,7168]{1,0:T(8,128)(2,1)S(1)} %get-tuple-element.143), channel_id=1, source_target_pairs={{16,0},{17,1},{18,2},{19,3},{20,4},{21,5},{22,6},{23,7},{24,8},{25... | collective-permute-start | bytes 2752520 | tf_op jit(solution)/shard_map/ppermute | solution.py:42
  80.1 14.9 %collective-permute-start.17 = (bf16[2,2,448,256]{3,2,0,1:T(8,128)(2,1)S(1)}, bf16[2,2,448,256]{3,2,0,1:T(8,128)(2,1)S(1)}, u32[]{:S(2)}, u32[]{:S(2)}) collective-permute-start(bf16[2,2,448,256]{3,2,0,1:T(8,128)(2,1)S(1)} %pad_maximum_fusion.1), channel_id=1, source_target_pairs={{0,1},{1,0},{2,3},{3,2},{4,5},{5,4},{6,7},{7,6},{8,9},{9,8},{10,11... | collective-permute-start | bytes 2752520 | tf_op jit(solution)/shard_map/ppermute | solution.py:23
  80.1 13.0 %collective-permute-start.16 = (bf16[2,448,256]{2,1,0:T(8,128)(2,1)S(1)}, bf16[2,448,256]{2,1,0:T(8,128)(2,1)S(1)}, u32[]{:S(2)}, u32[]{:S(2)}) collective-permute-start(bf16[2,448,256]{2,1,0:T(8,128)(2,1)S(1)} %slice_bitcast_fusion.7), channel_id=1, source_target_pairs={{0,12},{1,13},{2,14},{3,15},{4,0},{5,1},{6,2},{7,3},{8,4},{9,5},{1... | collective-permute-start | bytes 1376264 | tf_op jit(solution)/shard_map/ppermute | solution.py:23
  80.4 14.0 %collective-permute-start.15 = (bf16[2,448,256]{2,1,0:T(8,128)(2,1)S(1)}, bf16[2,448,256]{2,1,0:T(8,128)(2,1)S(1)}, u32[]{:S(2)}, u32[]{:S(2)}) collective-permute-start(bf16[2,448,256]{2,1,0:T(8,128)(2,1)S(1)} %slice_bitcast_fusion.8), channel_id=1, source_target_pairs={{0,4},{1,5},{2,6},{3,7},{4,8},{5,9},{6,10},{7,11},{8,12},{9,13},{1... | collective-permute-start | bytes 1376264 | tf_op jit(solution)/shard_map/ppermute | solution.py:23
  82.3 31.2 %collective-permute-start.24 = (bf16[64,7168]{1,0:T(8,128)(2,1)S(1)}, bf16[64,7168]{1,0:T(8,128)(2,1)S(1)}, u32[]{:S(2)}, u32[]{:S(2)}) collective-permute-start(bf16[64,7168]{1,0:T(8,128)(2,1)S(1)} %get-tuple-element.142), channel_id=1, source_target_pairs={{16,0},{17,1},{18,2},{19,3},{20,4},{21,5},{22,6},{23,7},{24,8},{25... | collective-permute-start | bytes 2752520 | tf_op jit(solution)/shard_map/ppermute | solution.py:42
  93.1 6.6 %collective-permute-start.18 = (bf16[2,2,448,256]{3,2,0,1:T(8,128)(2,1)S(1)}, bf16[2,2,448,256]{3,2,0,1:T(8,128)(2,1)S(1)}, u32[]{:S(2)}, u32[]{:S(2)}) collective-permute-start(bf16[2,2,448,256]{3,2,0,1:T(8,128)(2,1)S(1)} %collective-permute-done.8), channel_id=1, source_target_pairs={{0,1},{1,0},{2,3},{3,2},{4,5},{5,4},{6,7},{7,6},{8,9},{9,8},{10,11... | collective-permute-start | bytes 2752520 | tf_op jit(solution)/shard_map/ppermute | solution.py:23
  94.5 5.3 %collective-permute-start.19 = (bf16[2,2,448,256]{3,2,0,1:T(8,128)(2,1)S(1)}, bf16[2,2,448,256]{3,2,0,1:T(8,128)(2,1)S(1)}, u32[]{:S(2)}, u32[]{:S(2)}) collective-permute-start(bf16[2,2,448,256]{3,2,0,1:T(8,128)(2,1)S(1)} %collective-permute-done.9), channel_id=1, source_target_pairs={{0,1},{1,0},{2,3},{3,2},{4,5},{5,4},{6,7},{7,6},{8,9},{9,8},{10,11... | collective-permute-start | bytes 2752520 | tf_op jit(solution)/shard_map/ppermute | solution.py:23
  94.5 5.4 %collective-permute-start.21 = (bf16[2,448,256]{2,1,0:T(8,128)(2,1)S(1)}, bf16[2,448,256]{2,1,0:T(8,128)(2,1)S(1)}, u32[]{:S(2)}, u32[]{:S(2)}) collective-permute-start(bf16[2,448,256]{2,1,0:T(8,128)(2,1)S(1)} %collective-permute-done.16.refs_4_), channel_id=1, source_target_pairs={{0,1},{1,0},{2,3},{3,2},{4,5},{5,4},{6,7},{7,6},{8,9},{9,8},{10,11... | collective-permute-start | bytes 1376264 | tf_op jit(solution)/shard_map/ppermute | solution.py:23
  95.0 4.9 %collective-permute-start.20 = (bf16[2,448,256]{2,1,0:T(8,128)(2,1)S(1)}, bf16[2,448,256]{2,1,0:T(8,128)(2,1)S(1)}, u32[]{:S(2)}, u32[]{:S(2)}) collective-permute-start(bf16[2,448,256]{2,1,0:T(8,128)(2,1)S(1)} %collective-permute-done.15.refs_3_), channel_id=1, source_target_pairs={{0,1},{1,0},{2,3},{3,2},{4,5},{5,4},{6,7},{7,6},{8,9},{9,8},{10,11... | collective-permute-start | bytes 1376264 | tf_op jit(solution)/shard_map/ppermute | solution.py:23
  110.6 82.0 %collective-permute-start.23 = (bf16[256,7168]{1,0:T(8,128)(2,1)}, bf16[256,7168]{1,0:T(8,128)(2,1)S(1)}, u32[]{:S(2)}, u32[]{:S(2)}) collective-permute-start(bf16[256,7168]{1,0:T(8,128)(2,1)} %get-tuple-element.84), channel_id=1, source_target_pairs={{0,16},{1,17},{2,18},{3,19},{4,20},{5,21},{6,22},{7,23},{8,24},{9,... | collective-permute-start | bytes 11010056 | tf_op jit(solution)/shard_map/ppermute | solution.py:42
  128.1 2.6 collective-permute-start.26
  128.1 3.9 %collective-permute-start.28 = (bf16[2,272,896]{2,1,0:T(8,128)(2,1)S(1)}, bf16[2,272,896]{2,1,0:T(8,128)(2,1)S(1)}, u32[]{:S(2)}, u32[]{:S(2)}) collective-permute-start(bf16[2,272,896]{2,1,0:T(8,128)(2,1)S(1)} %get-tuple-element.98), channel_id=1, source_target_pairs={{0,1},{1,0},{2,3},{3,2},{4,5},{5,4},{6,7},{7,6},{8,9},{9,8},{10,11... | collective-permute-start | bytes 2924552 | tf_op jit(solution)/shard_map/ppermute | solution.py:23
  128.6 4.8 %collective-permute-start.30 = (bf16[2,272,896]{2,1,0:T(8,128)(2,1)S(1)}, bf16[2,272,896]{2,1,0:T(8,128)(2,1)S(1)}, u32[]{:S(2)}, u32[]{:S(2)}) collective-permute-start(bf16[2,272,896]{2,1,0:T(8,128)(2,1)S(1)} %get-tuple-element.100), channel_id=1, source_target_pairs={{0,1},{1,0},{2,3},{3,2},{4,5},{5,4},{6,7},{7,6},{8,9},{9,8},{10,11... | collective-permute-start | bytes 2924552 | tf_op jit(solution)/shard_map/ppermute | solution.py:23
  128.6 7.5 %collective-permute-start.25 = (bf16[2,272,896]{2,1,0:T(8,128)(2,1)S(1)}, bf16[2,272,896]{2,1,0:T(8,128)(2,1)S(1)}, u32[]{:S(2)}, u32[]{:S(2)}) collective-permute-start(bf16[2,272,896]{2,1,0:T(8,128)(2,1)S(1)} %get-tuple-element.94), channel_id=1, source_target_pairs={{0,1},{1,0},{2,3},{3,2},{4,5},{5,4},{6,7},{7,6},{8,9},{9,8},{10,11... | collective-permute-start | bytes 2924552 | tf_op jit(solution)/shard_map/ppermute | solution.py:23
  130.9 26.0 %collective-permute-start.27 = (bf16[2,272,896]{2,1,0:T(8,128)(2,1)S(1)}, bf16[2,272,896]{2,1,0:T(8,128)(2,1)S(1)}, u32[]{:S(2)}, u32[]{:S(2)}) collective-permute-start(bf16[2,272,896]{2,1,0:T(8,128)(2,1)S(1)} %add_convert_fusion.5), channel_id=1, source_target_pairs={{0,8},{1,9},{2,10},{3,11},{4,12},{5,13},{6,14},{7,15},{8,0},{9,1},... | collective-permute-start | bytes 2924552 | tf_op jit(solution)/shard_map/ppermute | solution.py:23
  132.3 44.7 %collective-permute-start.29 = (bf16[2,272,896]{2,1,0:T(8,128)(2,1)S(1)}, bf16[2,272,896]{2,1,0:T(8,128)(2,1)S(1)}, u32[]{:S(2)}, u32[]{:S(2)}) collective-permute-start(bf16[2,272,896]{2,1,0:T(8,128)(2,1)S(1)} %add_convert_fusion.4), channel_id=1, source_target_pairs={{0,4},{1,5},{2,6},{3,7},{4,8},{5,9},{6,10},{7,11},{8,12},{9,13},{1... | collective-permute-start | bytes 2924552 | tf_op jit(solution)/shard_map/ppermute | solution.py:23
  133.7 43.3 %collective-permute-start.31 = (bf16[2,272,896]{2,1,0:T(8,128)(2,1)S(1)}, bf16[2,272,896]{2,1,0:T(8,128)(2,1)S(1)}, u32[]{:S(2)}, u32[]{:S(2)}) collective-permute-start(bf16[2,272,896]{2,1,0:T(8,128)(2,1)S(1)} %add_convert_fusion.3), channel_id=1, source_target_pairs={{0,12},{1,13},{2,14},{3,15},{4,0},{5,1},{6,2},{7,3},{8,4},{9,5},{1... | collective-permute-start | bytes 2924552 | tf_op jit(solution)/shard_map/ppermute | solution.py:23
  203.1 4.2 %collective-permute-start.36 = (bf16[2,272,896]{2,1,0:T(8,128)(2,1)S(1)}, bf16[2,272,896]{2,1,0:T(8,128)(2,1)S(1)}, u32[]{:S(2)}, u32[]{:S(2)}) collective-permute-start(bf16[2,272,896]{2,1,0:T(8,128)(2,1)S(1)} %get-tuple-element.113), channel_id=1, source_target_pairs={{0,1},{1,0},{2,3},{3,2},{4,5},{5,4},{6,7},{7,6},{8,9},{9,8},{10,11... | collective-permute-start | bytes 2924552 | tf_op jit(solution)/shard_map/ppermute | solution.py:23
  203.1 21.9 %collective-permute-start.35 = (bf16[2,272,896]{2,1,0:T(8,128)(2,1)S(1)}, bf16[2,272,896]{2,1,0:T(8,128)(2,1)S(1)}, u32[]{:S(2)}, u32[]{:S(2)}) collective-permute-start(bf16[2,272,896]{2,1,0:T(8,128)(2,1)S(1)} %get-tuple-element.111), channel_id=1, source_target_pairs={{0,1},{1,0},{2,3},{3,2},{4,5},{5,4},{6,7},{7,6},{8,9},{9,8},{10,11... | collective-permute-start | bytes 2924552 | tf_op jit(solution)/shard_map/ppermute | solution.py:23
  203.7 15.0 %collective-permute-start.32 = (bf16[272,896]{1,0:T(8,128)(2,1)S(1)}, bf16[272,896]{1,0:T(8,128)(2,1)S(1)}, u32[]{:S(2)}, u32[]{:S(2)}) collective-permute-start(bf16[272,896]{1,0:T(8,128)(2,1)S(1)} %fusion), channel_id=1, source_target_pairs={{0,2},{1,3},{2,0},{3,1},{4,6},{5,7},{6,4},{7,5},{8,10},{9,11},{10,... | collective-permute-start | bytes 1462280 | tf_op jit(solution)/shard_map/ppermute | solution.py:23
  207.4 18.0 %collective-permute-start.38 = (bf16[2,272,896]{2,1,0:T(8,128)(2,1)S(1)}, bf16[2,272,896]{2,1,0:T(8,128)(2,1)S(1)}, u32[]{:S(2)}, u32[]{:S(2)}) collective-permute-start(bf16[2,272,896]{2,1,0:T(8,128)(2,1)S(1)} %get-tuple-element.116), channel_id=1, source_target_pairs={{0,1},{1,0},{2,3},{3,2},{4,5},{5,4},{6,7},{7,6},{8,9},{9,8},{10,11... | collective-permute-start | bytes 2924552 | tf_op jit(solution)/shard_map/ppermute | solution.py:23
  207.7 17.4 %collective-permute-start.37 = (bf16[2,128,896]{2,1,0:T(8,128)(2,1)S(1)}, bf16[2,128,896]{2,1,0:T(8,128)(2,1)S(1)}, u32[]{:S(2)}, u32[]{:S(2)}) collective-permute-start(bf16[2,128,896]{2,1,0:T(8,128)(2,1)S(1)} %slice.70), channel_id=1, source_target_pairs={{0,4},{1,5},{2,6},{3,7},{4,8},{5,9},{6,10},{7,11},{8,12},{9,13},{1... | collective-permute-start | bytes 1376264 | tf_op jit(solution)/shard_map/ppermute | solution.py:23
  208.3 17.1 %collective-permute-start.39 = (bf16[2,144,896]{2,1,0:T(8,128)(2,1)S(1)}, bf16[2,144,896]{2,1,0:T(8,128)(2,1)S(1)}, u32[]{:S(2)}, u32[]{:S(2)}) collective-permute-start(bf16[2,144,896]{2,1,0:T(8,128)(2,1)S(1)} %slice.71), channel_id=1, source_target_pairs={{0,12},{1,13},{2,14},{3,15},{4,0},{5,1},{6,2},{7,3},{8,4},{9,5},{1... | collective-permute-start | bytes 1548296 | tf_op jit(solution)/shard_map/ppermute | solution.py:23
  218.7 43.6 %collective-permute-start.33 = (bf16[128,7168]{1,0:T(8,128)(2,1)S(1)}, bf16[128,7168]{1,0:T(8,128)(2,1)S(1)}, u32[]{:S(2)}, u32[]{:S(2)}) collective-permute-start(bf16[128,7168]{1,0:T(8,128)(2,1)S(1)} %forward.5), channel_id=1, source_target_pairs={{16,1},{17,0},{18,3},{19,2},{20,5},{21,4},{22,7},{23,6},{24,9},{25... | collective-permute-start | bytes 5505032 | tf_op jit(solution)/shard_map/ppermute | solution.py:42
  225.0 4.0 %collective-permute-start.34 = (bf16[2,272,896]{2,1,0:T(8,128)(2,1)S(1)}, bf16[2,272,896]{2,1,0:T(8,128)(2,1)S(1)}, u32[]{:S(2)}, u32[]{:S(2)}) collective-permute-start(bf16[2,272,896]{2,1,0:T(8,128)(2,1)S(1)} %get-tuple-element.109), channel_id=1, source_target_pairs={{0,1},{1,0},{2,3},{3,2},{4,5},{5,4},{6,7},{7,6},{8,9},{9,8},{10,11... | collective-permute-start | bytes 2924552 | tf_op jit(solution)/shard_map/ppermute | solution.py:23
  225.7 25.3 %collective-permute-start.40 = (bf16[2,272,896]{2,1,0:T(8,128)(2,1)S(1)}, bf16[2,272,896]{2,1,0:T(8,128)(2,1)S(1)}, u32[]{:S(2)}, u32[]{:S(2)}) collective-permute-start(bf16[2,272,896]{2,1,0:T(8,128)(2,1)S(1)} %add_convert_fusion.1), channel_id=1, source_target_pairs={{0,4},{1,5},{2,6},{3,7},{4,8},{5,9},{6,10},{7,11},{8,12},{9,13},{1... | collective-permute-start | bytes 2924552 | tf_op jit(solution)/shard_map/ppermute | solution.py:23
  226.3 24.7 %collective-permute-start.41 = (bf16[2,272,896]{2,1,0:T(8,128)(2,1)S(1)}, bf16[2,272,896]{2,1,0:T(8,128)(2,1)S(1)}, u32[]{:S(2)}, u32[]{:S(2)}) collective-permute-start(bf16[2,272,896]{2,1,0:T(8,128)(2,1)S(1)} %add_convert_fusion), channel_id=1, source_target_pairs={{0,12},{1,13},{2,14},{3,15},{4,0},{5,1},{6,2},{7,3},{8,4},{9,5},{1... | collective-permute-start | bytes 2924552 | tf_op jit(solution)/shard_map/ppermute | solution.py:23
  262.3 6.5 %collective-permute-start.42 = (bf16[128,7168]{1,0:T(8,128)(2,1)S(1)}, bf16[128,7168]{1,0:T(8,128)(2,1)S(1)}, u32[]{:S(2)}, u32[]{:S(2)}) collective-permute-start(bf16[128,7168]{1,0:T(8,128)(2,1)S(1)} %collective-permute-done.33), channel_id=1, source_target_pairs={{0,1},{1,0},{2,3},{3,2},{4,5},{5,4},{6,7},{7,6},{8,9},{9,8},{10,11... | collective-permute-start | bytes 5505032 | tf_op jit(solution)/shard_map/ppermute | solution.py:23
  262.8 16.2 %collective-permute-start.43 = (bf16[272,896]{1,0:T(8,128)(2,1)S(1)}, bf16[272,896]{1,0:T(8,128)(2,1)S(1)}, u32[]{:S(2)}, u32[]{:S(2)}) collective-permute-start(bf16[272,896]{1,0:T(8,128)(2,1)S(1)} %get-tuple-element.145), channel_id=1, source_target_pairs={{0,112},{1,113},{2,114},{3,115},{4,116},{5,117},{6,118},{7,119},{8... | collective-permute-start | bytes 1462280 | tf_op jit(solution)/shard_map/ppermute | solution.py:31
  266.7 23.5 %collective-permute-start.44 = (bf16[272,896]{1,0:T(8,128)(2,1)S(1)}, bf16[272,896]{1,0:T(8,128)(2,1)S(1)}, u32[]{:S(2)}, u32[]{:S(2)}) collective-permute-start(bf16[272,896]{1,0:T(8,128)(2,1)S(1)} %get-tuple-element.144), channel_id=1, source_target_pairs={{0,114},{1,115},{2,112},{3,113},{4,118},{5,119},{6,116},{7,117},{8... | collective-permute-start | bytes 1462280 | tf_op jit(solution)/shard_map/ppermute | solution.py:31
  291.7 1.9 collective-permute-start.45
  (6 other events, 58.7 us)

commit v4 on v3

--- a/solution.py
+++ b/solution.py
@@ -372,14 +372,14 @@
         return jnp.concatenate([jnp.where(first, a, b), jnp.where(first, b, a)], axis=0)
 
     down_ref[...] = whole(0).T[:cols]
-    up_ref[...] = whole(1)[:, :cols]
+    up_ref[...] = whole(1).T[:cols]
 
 
 def join_halves(idx, mine, got):
     rank, cols = got.shape
     return pl.pallas_call(
         join_kernel,
-        out_shape=(jax.ShapeDtypeStruct((cols, rank), F32), jax.ShapeDtypeStruct((rank, cols), F32)),
+        out_shape=(jax.ShapeDtypeStruct((cols, rank), F32), jax.ShapeDtypeStruct((cols, rank), F32)),
         in_specs=[SMEM()] + [VMEM()] * 2,
         out_specs=(VMEM(),) * 2,
         compiler_params=pltpu.CompilerParams(vmem_limit_bytes=16 << 20),
@@ -396,13 +396,14 @@
 
     shard = after(jnp.stack([w_down[0], w_up[0].T]), idx)
     across = dp_move(shard, fz=1)
-    near_own = ring(jnp.stack([shard, across]))
+    gains = mirror(jnp.concatenate([norm_gain[0], latent_gain[0]]).reshape(-1, 128))
+    near = ring(shard)
+    near_z = ring(after(across, *near[1:], gains))
+    near_own = tuple(jnp.stack(pair) for pair in zip(near, near_z))
     shard_m = after(shard, across)
     mirrored = mirror(shard_m)
     mirrored_z = mirror(shard_m, fz=1)
-    gains = jnp.concatenate([norm_gain[0], latent_gain[0]]).reshape(-1, 128)
-    gains = mirror(after(gains, across))
-    near_own = far_halves(lax.optimization_barrier((*near_own, gains))[:3])
+    near_own = far_halves(near_own)
     pieces_a = near_own + other_core(near_own)
     gains_m = gains.reshape(1, -1)
     gain_a, lgain_a = norm_gain, latent_gain
@@ -446,7 +447,7 @@
         row,
         grad_down[None],
         grad_lgain,
-        grad_up[None],
+        grad_up.T[None],
     )
 
 

time: 298 us -> 291 us (0.977)
  waiting for transfers between devices: 174 us -> 165 us
    ppermute x37 -> x39, waiting for transfers between devices: 129 us -> 110 us  [dp_move(): return lax.ppermute(value, 'dp', pairs)]
    ppermute x5, waiting for transfers between devices: 19.2 us -> 29.7 us  [mirror(): return lax.ppermute(value, ('section', 'dp'), pairs)]
    ppermute x37 -> x39, starting transfers between devices: 30.7 us -> 32.7 us  [dp_move(): return lax.ppermute(value, 'dp', pairs)]
  transfers between devices with their start and end apart: 46 -> 48, of which waited for: 22 -> 23; matrix products, arithmetic and copies ran while one was open for 2% -> 2% of each run, Pallas kernels for 15% -> 16%
where the time goes in v4:
time: 291 us; the launch traced here: 289 us
  waiting for transfers between devices  165 us (57%)
  Pallas kernels  59 us (20%)
  starting transfers between devices  54.1 us (19%)
  other arithmetic  5.7 us (2%)
  local copies, waits for them, and re-layouts  3.27 us (1%)
    ppermute x39, waiting for transfers between devices, dp_move(): return lax.ppermute(value, 'dp', pairs)  110 us
    ppermute x39, starting transfers between devices, dp_move(): return lax.ppermute(value, 'dp', pairs)  32.7 us
    ppermute x5, waiting for transfers between devices, mirror(): return lax.ppermute(value, ('section', 'dp'), pairs)  29.7 us
    ppermute x4, waiting for transfers between devices, relay(): return lax.ppermute(value, ('section', 'dp'), pairs)  25.6 us
    pallas_call x2, Pallas kernels, backward_last(): pl.pallas_call(backward_last_kernel, out_shape=(act,) + (block,) * (2 * N...  21 us
    pallas_call x4, Pallas kernels, forward(): pl.pallas_call(forward_kernel, out_shape=jax.ShapeDtypeStruct((t, width),...  17.9 us
    pallas_call x2, Pallas kernels, backward_first(): pl.pallas_call(backward_first_kernel, out_shape=(jax.ShapeDtypeStruct((t...  17 us
    ppermute x5, starting transfers between devices, mirror(): return lax.ppermute(value, ('section', 'dp'), pairs)  12.7 us
  transfers between devices with their start and end apart: 48, of which 23 were waited for; matrix products, arithmetic and copies ran while one was open for 2% of the time, Pallas kernels for 16%

profile of v4, /device:TPU:0, one launch (start us, length us, event | category | flops | bytes accessed | tf_op | source)
XLA Modules:
  0.0 288.6 jit_solution(14509101226211842515)
XLA Ops:
  2.4 2.8 collective-permute-start.4
  5.3 3.9 %collective-permute-start = (bf16[2,448,256]{2,1,0:T(8,128)(2,1)S(1)}, bf16[2,448,256]{2,1,0:T(8,128)(2,1)S(1)}, u32[]{:S(2)}, u32[]{:S(2)}) collective-permute-start(bf16[2,448,256]{2,1,0:T(8,128)(2,1)S(1)} %pad_maximum_fusion.5), channel_id=1, source_target_pairs={{0,2},{1,3},{2,0},{3,1},{4,6},{5,7},{6,4},{7,5},{8,10},{9,11},{10,... | collective-permute-start | bytes 1376264 | tf_op jit(solution)/shard_map/ppermute | solution.py:23
  9.9 3.5 %collective-permute-start.5 = (f32[58,128]{1,0:T(8,128)S(1)}, f32[58,128]{1,0:T(8,128)S(1)}, u32[]{:S(2)}, u32[]{:S(2)}) collective-permute-start(f32[58,128]{1,0:T(8,128)S(1)} %maximum_bitcast_fusion), channel_id=1, source_target_pairs={{0,112},{1,113},{2,114},{3,115},{4,116},{5,117},{6,118},{7,119},{8... | collective-permute-start | bytes 89096 | tf_op jit(solution)/shard_map/ppermute | solution.py:31
  13.4 2.7 collective-permute-done.5
  16.0 2.4 collective-permute-done.3
  18.4 1.6 collective-permute-done
  20.1 3.0 %collective-permute-start.8 = (bf16[2,448,256]{2,1,0:T(8,128)(2,1)S(1)}, bf16[2,448,256]{2,1,0:T(8,128)(2,1)S(1)}, u32[]{:S(2)}, u32[]{:S(2)}) collective-permute-start(bf16[2,448,256]{2,1,0:T(8,128)(2,1)S(1)} %collective-permute-done), channel_id=1, source_target_pairs={{0,12},{1,13},{2,14},{3,15},{4,0},{5,1},{6,2},{7,3},{8,4},{9,5},{1... | collective-permute-start | bytes 1376264 | tf_op jit(solution)/shard_map/ppermute | solution.py:23
  23.0 5.9 %collective-permute-start.2 = (bf16[2,448,256]{2,1,0:T(8,128)(2,1)S(1)}, bf16[2,448,256]{2,1,0:T(8,128)(2,1)S(1)}, u32[]{:S(2)}, u32[]{:S(2)}) collective-permute-start(bf16[2,448,256]{2,1,0:T(8,128)(2,1)S(1)} %pad_maximum_fusion.5), channel_id=1, source_target_pairs={{0,114},{1,115},{2,112},{3,113},{4,118},{5,119},{6,116},{7,117},{8... | collective-permute-start | bytes 1376264 | tf_op jit(solution)/shard_map/ppermute | solution.py:31
  28.9 2.7 collective-permute-done.8
  31.7 3.8 %collective-permute-start.9 = (bf16[2,448,256]{2,1,0:T(8,128)(2,1)S(1)}, bf16[2,448,256]{2,1,0:T(8,128)(2,1)S(1)}, u32[]{:S(2)}, u32[]{:S(2)}) collective-permute-start(bf16[2,448,256]{2,1,0:T(8,128)(2,1)S(1)} %fusion.2), channel_id=1, source_target_pairs={{0,12},{1,13},{2,14},{3,15},{4,0},{5,1},{6,2},{7,3},{8,4},{9,5},{1... | collective-permute-start | bytes 1376264 | tf_op jit(solution)/shard_map/ppermute | solution.py:23
  36.0 4.4 %collective-permute-done.2 = bf16[2,448,256]{2,1,0:T(8,128)(2,1)S(1)} collective-permute-done((bf16[2,448,256]{2,1,0:T(8,128)(2,1)S(1)}, bf16[2,448,256]{2,1,0:T(8,128)(2,1)S(1)}, u32[]{:S(2)}, u32[]{:S(2)}) %collective-permute-start.2) | collective-permute-done | bytes 458784 | tf_op jit(solution)/shard_map/ppermute | solution.py:31
  40.3 6.4 %collective-permute-done.1 = bf16[2,448,256]{2,1,0:T(8,128)(2,1)S(1)} collective-permute-done((bf16[2,448,256]{2,1,0:T(8,128)(2,1)S(1)}, bf16[2,448,256]{2,1,0:T(8,128)(2,1)S(1)}, u32[]{:S(2)}, u32[]{:S(2)}) %collective-permute-start.1) | collective-permute-done | bytes 458784 | tf_op jit(solution)/shard_map/ppermute | solution.py:31
  47.7 3.0 %collective-permute-start.11 = (bf16[2,2,448,256]{3,2,0,1:T(8,128)(2,1)S(1)}, bf16[2,2,448,256]{3,2,0,1:T(8,128)(2,1)S(1)}, u32[]{:S(2)}, u32[]{:S(2)}) collective-permute-start(bf16[2,2,448,256]{3,2,0,1:T(8,128)(2,1)S(1)} %pad_maximum_fusion.3), channel_id=1, source_target_pairs={{0,12},{1,13},{2,14},{3,15},{4,0},{5,1},{6,2},{7,3},{8,4},{9,5},{1... | collective-permute-start | bytes 2752520 | tf_op jit(solution)/shard_map/ppermute | solution.py:23
  50.8 7.5 %backward_first.2 = (bf16[128,7168]{1,0:T(8,128)(2,1)S(1)}, bf16[128,7168]{1,0:T(8,128)(2,1)S(1)}, bf16[128,256]{1,0:T(8,128)(2,1)S(1)}, bf16[128,256]{1,0:T(8,1...) custom-call(s32[3]{0:T(128)S(1)} %shift-right-arithmetic_and_fusion., ...), custom_call_target="tpu_custom_call" | custom-call | flops 1409286144 | bytes 14680064 | tf_op jit(solution)/shard_map/backward_first/pallas_call | solution.py:262
  58.5 1.6 collective-permute-start.24
  60.0 10.9 %collective-permute-done.11 = bf16[2,2,448,256]{3,2,0,1:T(8,128)(2,1)S(1)} collective-permute-done((bf16[2,2,448,256]{3,2,0,1:T(8,128)(2,1)S(1)}, bf16[2,2,448,256]{3,2,0,1:T(8,128)(2,1)S(1)}, u32[]{:S(2)}, u32[]{:S(2)}) %collective-permute-start.11) | collective-permute-done | bytes 917536 | tf_op jit(solution)/shard_map/ppermute | solution.py:23
  70.9 3.4 %collective-permute-done.10 = bf16[2,2,448,256]{3,2,0,1:T(8,128)(2,1)S(1)} collective-permute-done((bf16[2,2,448,256]{3,2,0,1:T(8,128)(2,1)S(1)}, bf16[2,2,448,256]{3,2,0,1:T(8,128)(2,1)S(1)}, u32[]{:S(2)}, u32[]{:S(2)}) %collective-permute-start.10) | collective-permute-done | bytes 917536 | tf_op jit(solution)/shard_map/ppermute | solution.py:23
  75.4 1.2 collective-permute-start.17
  76.6 1.4 collective-permute-start.26
  78.0 9.4 %collective-permute-done.18.refs_4_ = bf16[2,448,256]{2,1,0:T(8,128)(2,1)S(1)} collective-permute-done((bf16[2,448,256]{2,1,0:T(8,128)(2,1)S(1)}, bf16[2,448,256]{2,1,0:T(8,128)(2,1)S(1)}, u32[]{:S(2)}, u32[]{:S(2)}) %collective-permute-start.18) | collective-permute-done | bytes 458784 | tf_op jit(solution)/shard_map/ppermute | solution.py:23
  87.4 1.9 collective-permute-done.17.refs_3_
  90.4 3.8 %forward.4.refs_10_ = bf16[128,7168]{1,0:T(8,128)(2,1)S(1)} custom-call(bf16[128,7168]{1,0:T(8,128)(2,1)S(1)} %bitcast.64, f32[1,7168]{1,0:T(1,128)S(1)} %copy-done.4, f32[1,256]{1,0:T(1,128)S(1)} %copy-done.5, bf16[7168,256]{1,0:T(8,128)(2,1)S(1)} %get-tuple-element.74.wd, bf16[7168,256]{1,0:T(8,128)(2,1)S(1)} %get-tuple-element.75.wu), custom_call_target="tpu_custom_call" | custom-call | flops 234881024 | bytes 917504 | tf_op jit(solution)/shard_map/forward/pallas_call | solution.py:245
  94.7 1.3 copy-done.1
  96.0 9.4 %backward_first.3 = (bf16[256,7168]{1,0:T(8,128)(2,1)}, bf16[128,7168]{1,0:T(8,128)(2,1)S(1)}, bf16[128,256]{1,0:T(8,128)(2,1)S(1)}, bf16[128,256]{1,0:T(8,128)(...) custom-call(s32[3]{0:T(128)S(1)} %shift-right-arithmetic_and_fusion., ...), custom_call_target="tpu_custom_call" | custom-call | flops 1409286144 | bytes 14680064 | tf_op jit(solution)/shard_map/backward_first/pallas_call | solution.py:262
  105.5 4.4 %collective-permute-start.25 = (bf16[256,7168]{1,0:T(8,128)(2,1)}, bf16[256,7168]{1,0:T(8,128)(2,1)S(1)}, u32[]{:S(2)}, u32[]{:S(2)}) collective-permute-start(bf16[256,7168]{1,0:T(8,128)(2,1)} %get-tuple-element.78), channel_id=1, source_target_pairs={{0,16},{1,17},{2,18},{3,19},{4,20},{5,21},{6,22},{7,23},{8,24},{9,... | collective-permute-start | bytes 11010056 | tf_op jit(solution)/shard_map/ppermute | solution.py:42
  110.0 3.8 %forward.5 = bf16[128,7168]{1,0:T(8,128)(2,1)S(1)} custom-call(bf16[128,7168]{1,0:T(8,128)(2,1)S(1)} %bitcast.65, f32[1,7168]{1,0:T(1,128)S(1)} %slice.79.refs_13_.gain_ref, f32[1,256]{1,0:T(1,128)S(1)} %slice.80.refs_14_.lgain_ref, bf16[7168,256]{1,0:T(8,128)(2,1)S(1)} %get-tuple-element.80.wd, bf16[7168,256]{1,0:T(8,128)(2,1)S(1)} %get-tuple-element.81.wu), custom_call_target="tpu_custom_call" | custom-call | flops 234881024 | bytes 917504 | tf_op jit(solution)/shard_map/forward/pallas_call | solution.py:245
  113.9 10.5 %backward_last.2 = (bf16[128,7168]{1,0:T(8,128)(2,1)}, bf16[2,272,896]{2,1,0:T(8,128)(2,1)S(1)}, bf16[2,272,896]{2,1,0:T(8,128)(2,1)S(1)}, bf16[2,272,896]{2,1,0...) custom-call(s32[3]{0:T(128)S(1)} %shift-right-arithmetic_and_fusion., ...), custom_call_target="tpu_custom_call" | custom-call | flops 234881024 | bytes 917504 | tf_op jit(solution)/shard_map/backward_last/pallas_call | solution.py:281
  125.4 1.5 collective-permute-done.28
  130.0 2.4 collective-permute-start.33
  132.4 20.8 %collective-permute-done.29 = bf16[2,272,896]{2,1,0:T(8,128)(2,1)S(1)} collective-permute-done((bf16[2,272,896]{2,1,0:T(8,128)(2,1)S(1)}, bf16[2,272,896]{2,1,0:T(8,128)(2,1)S(1)}, u32[]{:S(2)}, u32[]{:S(2)}) %collective-permute-start.29) | collective-permute-done | bytes 974880 | tf_op jit(solution)/shard_map/ppermute | solution.py:23
  153.2 20.0 %collective-permute-done.31 = bf16[2,272,896]{2,1,0:T(8,128)(2,1)S(1)} collective-permute-done((bf16[2,272,896]{2,1,0:T(8,128)(2,1)S(1)}, bf16[2,272,896]{2,1,0:T(8,128)(2,1)S(1)}, u32[]{:S(2)}, u32[]{:S(2)}) %collective-permute-start.31) | collective-permute-done | bytes 974880 | tf_op jit(solution)/shard_map/ppermute | solution.py:23
  173.9 15.1 %collective-permute-done.25.x_ref.g_ref = bf16[256,7168]{1,0:T(8,128)(2,1)S(1)} collective-permute-done((bf16[256,7168]{1,0:T(8,128)(2,1)}, bf16[256,7168]{1,0:T(8,128)(2,1)S(1)}, u32[]{:S(2)}, u32[]{:S(2)}) %collective-permute-start.25) | collective-permute-done | bytes 3670048 | tf_op jit(solution)/shard_map/ppermute | solution.py:42
  188.9 10.5 %backward_last.3 = (bf16[128,7168]{1,0:T(8,128)(2,1)}, bf16[2,272,896]{2,1,0:T(8,128)(2,1)S(1)}, bf16[2,272,896]{2,1,0:T(8,128)(2,1)S(1)}, bf16[2,272,896]{2,1,0...) custom-call(s32[3]{0:T(128)S(1)} %shift-right-arithmetic_and_fusion., ...), custom_call_target="tpu_custom_call" | custom-call | flops 234881024 | bytes 917504 | tf_op jit(solution)/shard_map/backward_last/pallas_call | solution.py:281
  200.6 1.4 collective-permute-done.38
  202.4 3.3 %collective-permute-start.41 = (bf16[2,144,896]{2,1,0:T(8,128)(2,1)S(1)}, bf16[2,144,896]{2,1,0:T(8,128)(2,1)S(1)}, u32[]{:S(2)}, u32[]{:S(2)}) collective-permute-start(bf16[2,144,896]{2,1,0:T(8,128)(2,1)S(1)} %slice.71), channel_id=1, source_target_pairs={{0,12},{1,13},{2,14},{3,15},{4,0},{5,1},{6,2},{7,3},{8,4},{9,5},{1... | collective-permute-start | bytes 1548296 | tf_op jit(solution)/shard_map/ppermute | solution.py:23
  205.7 8.9 %collective-permute-done.34.a_ref = bf16[272,896]{1,0:T(8,128)(2,1)S(1)} collective-permute-done((bf16[272,896]{1,0:T(8,128)(2,1)S(1)}, bf16[272,896]{1,0:T(8,128)(2,1)S(1)}, u32[]{:S(2)}, u32[]{:S(2)}) %collective-permute-start.34) | collective-permute-done | bytes 487456 | tf_op jit(solution)/shard_map/ppermute | solution.py:23
  214.6 1.3 collective-permute-start.35
  215.9 5.1 %forward.6 = bf16[128,7168]{1,0:T(8,128)(2,1)} custom-call(bf16[256,7168]{1,0:T(8,128)(2,1)S(1)} %collective-permute-done.25.x_ref.g_ref, f32[1,7168]{1,0:T(1,128)S(1)} %copy-done.4, f32[1,256]{1,0:T(1,128)S(1)} %copy-done.5, bf16[7168,256]{1,0:T(8,128)(2,1)S(1)} %get-tuple-element.74.wd, bf16[7168,256]{1,0:T(8,128)(2,1)S(1)} %get-tuple-element.75.wu), custom_call_target="tpu_custom_call" | custom-call | flops 234881024 | bytes 917504 | tf_op jit(solution)/shard_map/forward/pallas_call | solution.py:245
  221.7 3.2 %collective-permute-start.43 = (bf16[2,272,896]{2,1,0:T(8,128)(2,1)S(1)}, bf16[2,272,896]{2,1,0:T(8,128)(2,1)S(1)}, u32[]{:S(2)}, u32[]{:S(2)}) collective-permute-start(bf16[2,272,896]{2,1,0:T(8,128)(2,1)S(1)} %add_convert_fusion), channel_id=1, source_target_pairs={{0,12},{1,13},{2,14},{3,15},{4,0},{5,1},{6,2},{7,3},{8,4},{9,5},{1... | collective-permute-start | bytes 2924552 | tf_op jit(solution)/shard_map/ppermute | solution.py:23
  225.0 22.0 %collective-permute-done.42 = bf16[2,272,896]{2,1,0:T(8,128)(2,1)S(1)} collective-permute-done((bf16[2,272,896]{2,1,0:T(8,128)(2,1)S(1)}, bf16[2,272,896]{2,1,0:T(8,128)(2,1)S(1)}, u32[]{:S(2)}, u32[]{:S(2)}) %collective-permute-start.42) | collective-permute-done | bytes 974880 | tf_op jit(solution)/shard_map/ppermute | solution.py:23
  247.4 10.5 %collective-permute-done.35 = bf16[128,7168]{1,0:T(8,128)(2,1)S(1)} collective-permute-done((bf16[128,7168]{1,0:T(8,128)(2,1)S(1)}, bf16[128,7168]{1,0:T(8,128)(2,1)S(1)}, u32[]{:S(2)}, u32[]{:S(2)}) %collective-permute-start.35) | collective-permute-done | bytes 1835040 | tf_op jit(solution)/shard_map/ppermute | solution.py:42
  258.7 2.7 collective-permute-start.45
  262.2 5.1 %forward.7 = bf16[128,7168]{1,0:T(8,128)(2,1)} custom-call(bf16[128,7168]{1,0:T(8,128)(2,1)S(1)} %collective-permute-done.44.x_ref, f32[1,7168]{1,0:T(1,128)S(1)} %slice.79.refs_13_.gain_ref, f32[1,256]{1,0:T(1,128)S(1)} %slice.80.refs_14_.lgain_ref, bf16[7168,256]{1,0:T(8,128)(2,1)S(1)} %get-tuple-element.80.wd, bf16[7168,256]{1,0:T(8,128)(2,1)S(1)} %get-tuple-element.81.wu), custom_call_target="tpu_custom_call" | custom-call | flops 234881024 | bytes 917504 | tf_op jit(solution)/shard_map/forward/pallas_call | solution.py:245
  267.2 7.7 %collective-permute-done.45.b_ref = bf16[272,896]{1,0:T(8,128)(2,1)S(1)} collective-permute-done((bf16[272,896]{1,0:T(8,128)(2,1)S(1)}, bf16[272,896]{1,0:T(8,128)(2,1)S(1)}, u32[]{:S(2)}, u32[]{:S(2)}) %collective-permute-start.45) | collective-permute-done | bytes 487456 | tf_op jit(solution)/shard_map/ppermute | solution.py:31
  274.9 8.6 %collective-permute-done.46.c_ref = bf16[272,896]{1,0:T(8,128)(2,1)S(1)} collective-permute-done((bf16[272,896]{1,0:T(8,128)(2,1)S(1)}, bf16[272,896]{1,0:T(8,128)(2,1)S(1)}, u32[]{:S(2)}, u32[]{:S(2)}) %collective-permute-start.46) | collective-permute-done | bytes 487456 | tf_op jit(solution)/shard_map/ppermute | solution.py:31
  283.6 1.5 split_columns.1
  285.6 1.3 collective-permute-done.47.got_ref
  286.9 1.7 join_halves.1
  (112 shorter events, 16.1 us)
Async XLA Ops:
  2.4 13.6 %collective-permute-start.4 = (bf16[2,448,256]{2,1,0:T(8,128)(2,1)S(1)}, bf16[2,448,256]{2,1,0:T(8,128)(2,1)S(1)}, u32[]{:S(2)}, u32[]{:S(2)}) collective-permute-start(bf16[2,448,256]{2,1,0:T(8,128)(2,1)S(1)} %pad_maximum_fusion.5), channel_id=1, source_target_pairs={{0,12},{1,13},{2,14},{3,15},{4,0},{5,1},{6,2},{7,3},{8,4},{9,5},{1... | collective-permute-start | bytes 1376264 | tf_op jit(solution)/shard_map/ppermute | solution.py:23
  5.3 13.2 %collective-permute-start.3 = (bf16[2,448,256]{2,1,0:T(8,128)(2,1)S(1)}, bf16[2,448,256]{2,1,0:T(8,128)(2,1)S(1)}, u32[]{:S(2)}, u32[]{:S(2)}) collective-permute-start(bf16[2,448,256]{2,1,0:T(8,128)(2,1)S(1)} %pad_maximum_fusion.5), channel_id=1, source_target_pairs={{0,4},{1,5},{2,6},{3,7},{4,8},{5,9},{6,10},{7,11},{8,12},{9,13},{1... | collective-permute-start | bytes 1376264 | tf_op jit(solution)/shard_map/ppermute | solution.py:23
  5.3 14.8 %collective-permute-start = (bf16[2,448,256]{2,1,0:T(8,128)(2,1)S(1)}, bf16[2,448,256]{2,1,0:T(8,128)(2,1)S(1)}, u32[]{:S(2)}, u32[]{:S(2)}) collective-permute-start(bf16[2,448,256]{2,1,0:T(8,128)(2,1)S(1)} %pad_maximum_fusion.5), channel_id=1, source_target_pairs={{0,2},{1,3},{2,0},{3,1},{4,6},{5,7},{6,4},{7,5},{8,10},{9,11},{10,... | collective-permute-start | bytes 1376264 | tf_op jit(solution)/shard_map/ppermute | solution.py:23
  9.9 6.1 %collective-permute-start.5 = (f32[58,128]{1,0:T(8,128)S(1)}, f32[58,128]{1,0:T(8,128)S(1)}, u32[]{:S(2)}, u32[]{:S(2)}) collective-permute-start(f32[58,128]{1,0:T(8,128)S(1)} %maximum_bitcast_fusion), channel_id=1, source_target_pairs={{0,112},{1,113},{2,114},{3,115},{4,116},{5,117},{6,118},{7,119},{8... | collective-permute-start | bytes 89096 | tf_op jit(solution)/shard_map/ppermute | solution.py:31
  20.1 11.5 %collective-permute-start.8 = (bf16[2,448,256]{2,1,0:T(8,128)(2,1)S(1)}, bf16[2,448,256]{2,1,0:T(8,128)(2,1)S(1)}, u32[]{:S(2)}, u32[]{:S(2)}) collective-permute-start(bf16[2,448,256]{2,1,0:T(8,128)(2,1)S(1)} %collective-permute-done), channel_id=1, source_target_pairs={{0,12},{1,13},{2,14},{3,15},{4,0},{5,1},{6,2},{7,3},{8,4},{9,5},{1... | collective-permute-start | bytes 1376264 | tf_op jit(solution)/shard_map/ppermute | solution.py:23
  23.0 12.4 %collective-permute-start.6 = (bf16[2,448,256]{2,1,0:T(8,128)(2,1)S(1)}, bf16[2,448,256]{2,1,0:T(8,128)(2,1)S(1)}, u32[]{:S(2)}, u32[]{:S(2)}) collective-permute-start(bf16[2,448,256]{2,1,0:T(8,128)(2,1)S(1)} %collective-permute-done), channel_id=1, source_target_pairs={{0,4},{1,5},{2,6},{3,7},{4,8},{5,9},{6,10},{7,11},{8,12},{9,13},{1... | collective-permute-start | bytes 1376264 | tf_op jit(solution)/shard_map/ppermute | solution.py:23
  23.0 17.3 %collective-permute-start.2 = (bf16[2,448,256]{2,1,0:T(8,128)(2,1)S(1)}, bf16[2,448,256]{2,1,0:T(8,128)(2,1)S(1)}, u32[]{:S(2)}, u32[]{:S(2)}) collective-permute-start(bf16[2,448,256]{2,1,0:T(8,128)(2,1)S(1)} %pad_maximum_fusion.5), channel_id=1, source_target_pairs={{0,114},{1,115},{2,112},{3,113},{4,118},{5,119},{6,116},{7,117},{8... | collective-permute-start | bytes 1376264 | tf_op jit(solution)/shard_map/ppermute | solution.py:31
  28.9 17.8 %collective-permute-start.1 = (bf16[2,448,256]{2,1,0:T(8,128)(2,1)S(1)}, bf16[2,448,256]{2,1,0:T(8,128)(2,1)S(1)}, u32[]{:S(2)}, u32[]{:S(2)}) collective-permute-start(bf16[2,448,256]{2,1,0:T(8,128)(2,1)S(1)} %pad_maximum_fusion.5), channel_id=1, source_target_pairs={{0,112},{1,113},{2,114},{3,115},{4,116},{5,117},{6,118},{7,119},{8... | collective-permute-start | bytes 1376264 | tf_op jit(solution)/shard_map/ppermute | solution.py:31
  31.7 15.1 %collective-permute-start.9 = (bf16[2,448,256]{2,1,0:T(8,128)(2,1)S(1)}, bf16[2,448,256]{2,1,0:T(8,128)(2,1)S(1)}, u32[]{:S(2)}, u32[]{:S(2)}) collective-permute-start(bf16[2,448,256]{2,1,0:T(8,128)(2,1)S(1)} %fusion.2), channel_id=1, source_target_pairs={{0,12},{1,13},{2,14},{3,15},{4,0},{5,1},{6,2},{7,3},{8,4},{9,5},{1... | collective-permute-start | bytes 1376264 | tf_op jit(solution)/shard_map/ppermute | solution.py:23
  35.5 11.8 %collective-permute-start.7 = (bf16[2,448,256]{2,1,0:T(8,128)(2,1)S(1)}, bf16[2,448,256]{2,1,0:T(8,128)(2,1)S(1)}, u32[]{:S(2)}, u32[]{:S(2)}) collective-permute-start(bf16[2,448,256]{2,1,0:T(8,128)(2,1)S(1)} %fusion.4), channel_id=1, source_target_pairs={{0,4},{1,5},{2,6},{3,7},{4,8},{5,9},{6,10},{7,11},{8,12},{9,13},{1... | collective-permute-start | bytes 1376264 | tf_op jit(solution)/shard_map/ppermute | solution.py:23
  35.7 12.0 %collective-permute-start.12 = (bf16[2,2,448,256]{3,2,1,0:T(8,128)(2,1)S(1)}, bf16[2,2,448,256]{3,2,1,0:T(8,128)(2,1)S(1)}, u32[]{:S(2)}, u32[]{:S(2)}) collective-permute-start(bf16[2,2,448,256]{3,2,1,0:T(8,128)(2,1)S(1)} %pad_maximum_fusion.4.refs_0_), channel_id=1, source_target_pairs={{0,1},{1,0},{2,3},{3,2},{4,5},{5,4},{6,7},{7,6},{8,9},{9,8},{10,11... | collective-permute-start | bytes 2752520 | tf_op jit(solution)/shard_map/ppermute | solution.py:23
  40.3 10.4 %collective-permute-start.13 = (bf16[2,2,448,256]{3,2,1,0:T(8,128)(2,1)S(1)}, bf16[2,2,448,256]{3,2,1,0:T(8,128)(2,1)S(1)}, u32[]{:S(2)}, u32[]{:S(2)}) collective-permute-start(bf16[2,2,448,256]{3,2,1,0:T(8,128)(2,1)S(1)} %pad_maximum_fusion.1.refs_1_), channel_id=1, source_target_pairs={{0,1},{1,0},{2,3},{3,2},{4,5},{5,4},{6,7},{7,6},{8,9},{9,8},{10,11... | collective-permute-start | bytes 2752520 | tf_op jit(solution)/shard_map/ppermute | solution.py:23
  46.7 4.0 %collective-permute-start.14 = (bf16[2,2,448,256]{3,2,1,0:T(8,128)(2,1)S(1)}, bf16[2,2,448,256]{3,2,1,0:T(8,128)(2,1)S(1)}, u32[]{:S(2)}, u32[]{:S(2)}) collective-permute-start(bf16[2,2,448,256]{3,2,1,0:T(8,128)(2,1)S(1)} %pad_maximum_fusion.2.refs_2_), channel_id=1, source_target_pairs={{0,1},{1,0},{2,3},{3,2},{4,5},{5,4},{6,7},{7,6},{8,9},{9,8},{10,11... | collective-permute-start | bytes 2752520 | tf_op jit(solution)/shard_map/ppermute | solution.py:23
  46.7 4.0 %collective-permute-start.16 = (bf16[2,448,256]{2,1,0:T(8,128)(2,1)S(1)}, bf16[2,448,256]{2,1,0:T(8,128)(2,1)S(1)}, u32[]{:S(2)}, u32[]{:S(2)}) collective-permute-start(bf16[2,448,256]{2,1,0:T(8,128)(2,1)S(1)} %collective-permute-done.9.refs_4_), channel_id=1, source_target_pairs={{0,1},{1,0},{2,3},{3,2},{4,5},{5,4},{6,7},{7,6},{8,9},{9,8},{10,11... | collective-permute-start | bytes 1376264 | tf_op jit(solution)/shard_map/ppermute | solution.py:23
  47.3 3.5 %collective-permute-start.15 = (bf16[2,448,256]{2,1,0:T(8,128)(2,1)S(1)}, bf16[2,448,256]{2,1,0:T(8,128)(2,1)S(1)}, u32[]{:S(2)}, u32[]{:S(2)}) collective-permute-start(bf16[2,448,256]{2,1,0:T(8,128)(2,1)S(1)} %collective-permute-done.7.refs_3_), channel_id=1, source_target_pairs={{0,1},{1,0},{2,3},{3,2},{4,5},{5,4},{6,7},{7,6},{8,9},{9,8},{10,11... | collective-permute-start | bytes 1376264 | tf_op jit(solution)/shard_map/ppermute | solution.py:23
  47.7 23.2 %collective-permute-start.11 = (bf16[2,2,448,256]{3,2,0,1:T(8,128)(2,1)S(1)}, bf16[2,2,448,256]{3,2,0,1:T(8,128)(2,1)S(1)}, u32[]{:S(2)}, u32[]{:S(2)}) collective-permute-start(bf16[2,2,448,256]{3,2,0,1:T(8,128)(2,1)S(1)} %pad_maximum_fusion.3), channel_id=1, source_target_pairs={{0,12},{1,13},{2,14},{3,15},{4,0},{5,1},{6,2},{7,3},{8,4},{9,5},{1... | collective-permute-start | bytes 2752520 | tf_op jit(solution)/shard_map/ppermute | solution.py:23
  50.7 23.6 %collective-permute-start.10 = (bf16[2,2,448,256]{3,2,0,1:T(8,128)(2,1)S(1)}, bf16[2,2,448,256]{3,2,0,1:T(8,128)(2,1)S(1)}, u32[]{:S(2)}, u32[]{:S(2)}) collective-permute-start(bf16[2,2,448,256]{3,2,0,1:T(8,128)(2,1)S(1)} %pad_maximum_fusion.3), channel_id=1, source_target_pairs={{0,4},{1,5},{2,6},{3,7},{4,8},{5,9},{6,10},{7,11},{8,12},{9,13},{1... | collective-permute-start | bytes 2752520 | tf_op jit(solution)/shard_map/ppermute | solution.py:23
  58.5 30.8 %collective-permute-start.24 = (bf16[64,7168]{1,0:T(8,128)(2,1)S(1)}, bf16[64,7168]{1,0:T(8,128)(2,1)S(1)}, u32[]{:S(2)}, u32[]{:S(2)}) collective-permute-start(bf16[64,7168]{1,0:T(8,128)(2,1)S(1)} %get-tuple-element.129), channel_id=1, source_target_pairs={{16,0},{17,1},{18,2},{19,3},{20,4},{21,5},{22,6},{23,7},{24,8},{25... | collective-permute-start | bytes 2752520 | tf_op jit(solution)/shard_map/ppermute | solution.py:42
  74.4 15.4 %collective-permute-start.19 = (bf16[2,2,448,256]{3,2,0,1:T(8,128)(2,1)S(1)}, bf16[2,2,448,256]{3,2,0,1:T(8,128)(2,1)S(1)}, u32[]{:S(2)}, u32[]{:S(2)}) collective-permute-start(bf16[2,2,448,256]{3,2,0,1:T(8,128)(2,1)S(1)} %pad_maximum_fusion.3), channel_id=1, source_target_pairs={{0,1},{1,0},{2,3},{3,2},{4,5},{5,4},{6,7},{7,6},{8,9},{9,8},{10,11... | collective-permute-start | bytes 2752520 | tf_op jit(solution)/shard_map/ppermute | solution.py:23
  74.4 13.0 %collective-permute-start.18 = (bf16[2,448,256]{2,1,0:T(8,128)(2,1)S(1)}, bf16[2,448,256]{2,1,0:T(8,128)(2,1)S(1)}, u32[]{:S(2)}, u32[]{:S(2)}) collective-permute-start(bf16[2,448,256]{2,1,0:T(8,128)(2,1)S(1)} %slice_bitcast_fusion.7), channel_id=1, source_target_pairs={{0,12},{1,13},{2,14},{3,15},{4,0},{5,1},{6,2},{7,3},{8,4},{9,5},{1... | collective-permute-start | bytes 1376264 | tf_op jit(solution)/shard_map/ppermute | solution.py:23
  75.4 13.9 %collective-permute-start.17 = (bf16[2,448,256]{2,1,0:T(8,128)(2,1)S(1)}, bf16[2,448,256]{2,1,0:T(8,128)(2,1)S(1)}, u32[]{:S(2)}, u32[]{:S(2)}) collective-permute-start(bf16[2,448,256]{2,1,0:T(8,128)(2,1)S(1)} %slice_bitcast_fusion.8), channel_id=1, source_target_pairs={{0,4},{1,5},{2,6},{3,7},{4,8},{5,9},{6,10},{7,11},{8,12},{9,13},{1... | collective-permute-start | bytes 1376264 | tf_op jit(solution)/shard_map/ppermute | solution.py:23
  76.6 33.3 %collective-permute-start.26 = (bf16[64,7168]{1,0:T(8,128)(2,1)S(1)}, bf16[64,7168]{1,0:T(8,128)(2,1)S(1)}, u32[]{:S(2)}, u32[]{:S(2)}) collective-permute-start(bf16[64,7168]{1,0:T(8,128)(2,1)S(1)} %get-tuple-element.128), channel_id=1, source_target_pairs={{16,0},{17,1},{18,2},{19,3},{20,4},{21,5},{22,6},{23,7},{24,8},{25... | collective-permute-start | bytes 2752520 | tf_op jit(solution)/shard_map/ppermute | solution.py:42
  87.4 7.1 %collective-permute-start.20 = (bf16[2,2,448,256]{3,2,0,1:T(8,128)(2,1)S(1)}, bf16[2,2,448,256]{3,2,0,1:T(8,128)(2,1)S(1)}, u32[]{:S(2)}, u32[]{:S(2)}) collective-permute-start(bf16[2,2,448,256]{3,2,0,1:T(8,128)(2,1)S(1)} %collective-permute-done.10), channel_id=1, source_target_pairs={{0,1},{1,0},{2,3},{3,2},{4,5},{5,4},{6,7},{7,6},{8,9},{9,8},{10,11... | collective-permute-start | bytes 2752520 | tf_op jit(solution)/shard_map/ppermute | solution.py:23
  89.3 5.3 %collective-permute-start.21 = (bf16[2,2,448,256]{3,2,0,1:T(8,128)(2,1)S(1)}, bf16[2,2,448,256]{3,2,0,1:T(8,128)(2,1)S(1)}, u32[]{:S(2)}, u32[]{:S(2)}) collective-permute-start(bf16[2,2,448,256]{3,2,0,1:T(8,128)(2,1)S(1)} %collective-permute-done.11), channel_id=1, source_target_pairs={{0,1},{1,0},{2,3},{3,2},{4,5},{5,4},{6,7},{7,6},{8,9},{9,8},{10,11... | collective-permute-start | bytes 2752520 | tf_op jit(solution)/shard_map/ppermute | solution.py:23
  89.3 5.4 %collective-permute-start.23 = (bf16[2,448,256]{2,1,0:T(8,128)(2,1)S(1)}, bf16[2,448,256]{2,1,0:T(8,128)(2,1)S(1)}, u32[]{:S(2)}, u32[]{:S(2)}) collective-permute-start(bf16[2,448,256]{2,1,0:T(8,128)(2,1)S(1)} %collective-permute-done.18.refs_4_), channel_id=1, source_target_pairs={{0,1},{1,0},{2,3},{3,2},{4,5},{5,4},{6,7},{7,6},{8,9},{9,8},{10,11... | collective-permute-start | bytes 1376264 | tf_op jit(solution)/shard_map/ppermute | solution.py:23
  89.8 4.9 %collective-permute-start.22 = (bf16[2,448,256]{2,1,0:T(8,128)(2,1)S(1)}, bf16[2,448,256]{2,1,0:T(8,128)(2,1)S(1)}, u32[]{:S(2)}, u32[]{:S(2)}) collective-permute-start(bf16[2,448,256]{2,1,0:T(8,128)(2,1)S(1)} %collective-permute-done.17.refs_3_), channel_id=1, source_target_pairs={{0,1},{1,0},{2,3},{3,2},{4,5},{5,4},{6,7},{7,6},{8,9},{9,8},{10,11... | collective-permute-start | bytes 1376264 | tf_op jit(solution)/shard_map/ppermute | solution.py:23
  105.5 83.5 %collective-permute-start.25 = (bf16[256,7168]{1,0:T(8,128)(2,1)}, bf16[256,7168]{1,0:T(8,128)(2,1)S(1)}, u32[]{:S(2)}, u32[]{:S(2)}) collective-permute-start(bf16[256,7168]{1,0:T(8,128)(2,1)} %get-tuple-element.78), channel_id=1, source_target_pairs={{0,16},{1,17},{2,18},{3,19},{4,20},{5,21},{6,22},{7,23},{8,24},{9,... | collective-permute-start | bytes 11010056 | tf_op jit(solution)/shard_map/ppermute | solution.py:42
  124.4 2.6 collective-permute-start.28
  124.4 3.9 %collective-permute-start.30 = (bf16[2,272,896]{2,1,0:T(8,128)(2,1)S(1)}, bf16[2,272,896]{2,1,0:T(8,128)(2,1)S(1)}, u32[]{:S(2)}, u32[]{:S(2)}) collective-permute-start(bf16[2,272,896]{2,1,0:T(8,128)(2,1)S(1)} %get-tuple-element.92), channel_id=1, source_target_pairs={{0,1},{1,0},{2,3},{3,2},{4,5},{5,4},{6,7},{7,6},{8,9},{9,8},{10,11... | collective-permute-start | bytes 2924552 | tf_op jit(solution)/shard_map/ppermute | solution.py:23
  124.9 4.8 %collective-permute-start.32 = (bf16[2,272,896]{2,1,0:T(8,128)(2,1)S(1)}, bf16[2,272,896]{2,1,0:T(8,128)(2,1)S(1)}, u32[]{:S(2)}, u32[]{:S(2)}) collective-permute-start(bf16[2,272,896]{2,1,0:T(8,128)(2,1)S(1)} %get-tuple-element.94), channel_id=1, source_target_pairs={{0,1},{1,0},{2,3},{3,2},{4,5},{5,4},{6,7},{7,6},{8,9},{9,8},{10,11... | collective-permute-start | bytes 2924552 | tf_op jit(solution)/shard_map/ppermute | solution.py:23
  124.9 7.5 %collective-permute-start.27 = (bf16[2,272,896]{2,1,0:T(8,128)(2,1)S(1)}, bf16[2,272,896]{2,1,0:T(8,128)(2,1)S(1)}, u32[]{:S(2)}, u32[]{:S(2)}) collective-permute-start(bf16[2,272,896]{2,1,0:T(8,128)(2,1)S(1)} %get-tuple-element.88), channel_id=1, source_target_pairs={{0,1},{1,0},{2,3},{3,2},{4,5},{5,4},{6,7},{7,6},{8,9},{9,8},{10,11... | collective-permute-start | bytes 2924552 | tf_op jit(solution)/shard_map/ppermute | solution.py:23
  127.2 26.0 %collective-permute-start.29 = (bf16[2,272,896]{2,1,0:T(8,128)(2,1)S(1)}, bf16[2,272,896]{2,1,0:T(8,128)(2,1)S(1)}, u32[]{:S(2)}, u32[]{:S(2)}) collective-permute-start(bf16[2,272,896]{2,1,0:T(8,128)(2,1)S(1)} %add_convert_fusion.5), channel_id=1, source_target_pairs={{0,8},{1,9},{2,10},{3,11},{4,12},{5,13},{6,14},{7,15},{8,0},{9,1},... | collective-permute-start | bytes 2924552 | tf_op jit(solution)/shard_map/ppermute | solution.py:23
  128.6 44.7 %collective-permute-start.31 = (bf16[2,272,896]{2,1,0:T(8,128)(2,1)S(1)}, bf16[2,272,896]{2,1,0:T(8,128)(2,1)S(1)}, u32[]{:S(2)}, u32[]{:S(2)}) collective-permute-start(bf16[2,272,896]{2,1,0:T(8,128)(2,1)S(1)} %add_convert_fusion.4), channel_id=1, source_target_pairs={{0,4},{1,5},{2,6},{3,7},{4,8},{5,9},{6,10},{7,11},{8,12},{9,13},{1... | collective-permute-start | bytes 2924552 | tf_op jit(solution)/shard_map/ppermute | solution.py:23
  130.0 43.3 %collective-permute-start.33 = (bf16[2,272,896]{2,1,0:T(8,128)(2,1)S(1)}, bf16[2,272,896]{2,1,0:T(8,128)(2,1)S(1)}, u32[]{:S(2)}, u32[]{:S(2)}) collective-permute-start(bf16[2,272,896]{2,1,0:T(8,128)(2,1)S(1)} %add_convert_fusion.3), channel_id=1, source_target_pairs={{0,12},{1,13},{2,14},{3,15},{4,0},{5,1},{6,2},{7,3},{8,4},{9,5},{1... | collective-permute-start | bytes 2924552 | tf_op jit(solution)/shard_map/ppermute | solution.py:23
  199.4 2.6 collective-permute-start.38
  199.4 21.6 %collective-permute-start.37 = (bf16[2,272,896]{2,1,0:T(8,128)(2,1)S(1)}, bf16[2,272,896]{2,1,0:T(8,128)(2,1)S(1)}, u32[]{:S(2)}, u32[]{:S(2)}) collective-permute-start(bf16[2,272,896]{2,1,0:T(8,128)(2,1)S(1)} %get-tuple-element.105), channel_id=1, source_target_pairs={{0,1},{1,0},{2,3},{3,2},{4,5},{5,4},{6,7},{7,6},{8,9},{9,8},{10,11... | collective-permute-start | bytes 2924552 | tf_op jit(solution)/shard_map/ppermute | solution.py:23
  200.0 14.6 %collective-permute-start.34 = (bf16[272,896]{1,0:T(8,128)(2,1)S(1)}, bf16[272,896]{1,0:T(8,128)(2,1)S(1)}, u32[]{:S(2)}, u32[]{:S(2)}) collective-permute-start(bf16[272,896]{1,0:T(8,128)(2,1)S(1)} %fusion), channel_id=1, source_target_pairs={{0,2},{1,3},{2,0},{3,1},{4,6},{5,7},{6,4},{7,5},{8,10},{9,11},{10,... | collective-permute-start | bytes 1462280 | tf_op jit(solution)/shard_map/ppermute | solution.py:23
  200.6 20.8 %collective-permute-start.40 = (bf16[2,272,896]{2,1,0:T(8,128)(2,1)S(1)}, bf16[2,272,896]{2,1,0:T(8,128)(2,1)S(1)}, u32[]{:S(2)}, u32[]{:S(2)}) collective-permute-start(bf16[2,272,896]{2,1,0:T(8,128)(2,1)S(1)} %get-tuple-element.110), channel_id=1, source_target_pairs={{0,1},{1,0},{2,3},{3,2},{4,5},{5,4},{6,7},{7,6},{8,9},{9,8},{10,11... | collective-permute-start | bytes 2924552 | tf_op jit(solution)/shard_map/ppermute | solution.py:23
  202.3 18.7 %collective-permute-start.39 = (bf16[2,128,896]{2,1,0:T(8,128)(2,1)S(1)}, bf16[2,128,896]{2,1,0:T(8,128)(2,1)S(1)}, u32[]{:S(2)}, u32[]{:S(2)}) collective-permute-start(bf16[2,128,896]{2,1,0:T(8,128)(2,1)S(1)} %slice.70), channel_id=1, source_target_pairs={{0,4},{1,5},{2,6},{3,7},{4,8},{5,9},{6,10},{7,11},{8,12},{9,13},{1... | collective-permute-start | bytes 1376264 | tf_op jit(solution)/shard_map/ppermute | solution.py:23
  202.4 18.9 %collective-permute-start.41 = (bf16[2,144,896]{2,1,0:T(8,128)(2,1)S(1)}, bf16[2,144,896]{2,1,0:T(8,128)(2,1)S(1)}, u32[]{:S(2)}, u32[]{:S(2)}) collective-permute-start(bf16[2,144,896]{2,1,0:T(8,128)(2,1)S(1)} %slice.71), channel_id=1, source_target_pairs={{0,12},{1,13},{2,14},{3,15},{4,0},{5,1},{6,2},{7,3},{8,4},{9,5},{1... | collective-permute-start | bytes 1548296 | tf_op jit(solution)/shard_map/ppermute | solution.py:23
  214.6 43.3 %collective-permute-start.35 = (bf16[128,7168]{1,0:T(8,128)(2,1)S(1)}, bf16[128,7168]{1,0:T(8,128)(2,1)S(1)}, u32[]{:S(2)}, u32[]{:S(2)}) collective-permute-start(bf16[128,7168]{1,0:T(8,128)(2,1)S(1)} %forward.5), channel_id=1, source_target_pairs={{16,1},{17,0},{18,3},{19,2},{20,5},{21,4},{22,7},{23,6},{24,9},{25... | collective-permute-start | bytes 5505032 | tf_op jit(solution)/shard_map/ppermute | solution.py:42
  221.0 4.0 %collective-permute-start.36 = (bf16[2,272,896]{2,1,0:T(8,128)(2,1)S(1)}, bf16[2,272,896]{2,1,0:T(8,128)(2,1)S(1)}, u32[]{:S(2)}, u32[]{:S(2)}) collective-permute-start(bf16[2,272,896]{2,1,0:T(8,128)(2,1)S(1)} %get-tuple-element.103), channel_id=1, source_target_pairs={{0,1},{1,0},{2,3},{3,2},{4,5},{5,4},{6,7},{7,6},{8,9},{9,8},{10,11... | collective-permute-start | bytes 2924552 | tf_op jit(solution)/shard_map/ppermute | solution.py:23
  221.6 25.3 %collective-permute-start.42 = (bf16[2,272,896]{2,1,0:T(8,128)(2,1)S(1)}, bf16[2,272,896]{2,1,0:T(8,128)(2,1)S(1)}, u32[]{:S(2)}, u32[]{:S(2)}) collective-permute-start(bf16[2,272,896]{2,1,0:T(8,128)(2,1)S(1)} %add_convert_fusion.1), channel_id=1, source_target_pairs={{0,4},{1,5},{2,6},{3,7},{4,8},{5,9},{6,10},{7,11},{8,12},{9,13},{1... | collective-permute-start | bytes 2924552 | tf_op jit(solution)/shard_map/ppermute | solution.py:23
  221.7 25.2 %collective-permute-start.43 = (bf16[2,272,896]{2,1,0:T(8,128)(2,1)S(1)}, bf16[2,272,896]{2,1,0:T(8,128)(2,1)S(1)}, u32[]{:S(2)}, u32[]{:S(2)}) collective-permute-start(bf16[2,272,896]{2,1,0:T(8,128)(2,1)S(1)} %add_convert_fusion), channel_id=1, source_target_pairs={{0,12},{1,13},{2,14},{3,15},{4,0},{5,1},{6,2},{7,3},{8,4},{9,5},{1... | collective-permute-start | bytes 2924552 | tf_op jit(solution)/shard_map/ppermute | solution.py:23
  257.9 4.2 %collective-permute-start.44 = (bf16[128,7168]{1,0:T(8,128)(2,1)S(1)}, bf16[128,7168]{1,0:T(8,128)(2,1)S(1)}, u32[]{:S(2)}, u32[]{:S(2)}) collective-permute-start(bf16[128,7168]{1,0:T(8,128)(2,1)S(1)} %collective-permute-done.35), channel_id=1, source_target_pairs={{0,1},{1,0},{2,3},{3,2},{4,5},{5,4},{6,7},{7,6},{8,9},{9,8},{10,11... | collective-permute-start | bytes 5505032 | tf_op jit(solution)/shard_map/ppermute | solution.py:23
  258.7 16.2 %collective-permute-start.45 = (bf16[272,896]{1,0:T(8,128)(2,1)S(1)}, bf16[272,896]{1,0:T(8,128)(2,1)S(1)}, u32[]{:S(2)}, u32[]{:S(2)}) collective-permute-start(bf16[272,896]{1,0:T(8,128)(2,1)S(1)} %get-tuple-element.131), channel_id=1, source_target_pairs={{0,112},{1,113},{2,114},{3,115},{4,116},{5,117},{6,118},{7,119},{8... | collective-permute-start | bytes 1462280 | tf_op jit(solution)/shard_map/ppermute | solution.py:31
  261.5 22.1 %collective-permute-start.46 = (bf16[272,896]{1,0:T(8,128)(2,1)S(1)}, bf16[272,896]{1,0:T(8,128)(2,1)S(1)}, u32[]{:S(2)}, u32[]{:S(2)}) collective-permute-start(bf16[272,896]{1,0:T(8,128)(2,1)S(1)} %get-tuple-element.130), channel_id=1, source_target_pairs={{0,114},{1,115},{2,112},{3,113},{4,118},{5,119},{6,116},{7,117},{8... | collective-permute-start | bytes 1462280 | tf_op jit(solution)/shard_map/ppermute | solution.py:31
  285.0 1.9 collective-permute-start.47
  (8 other events, 96.2 us)
